TPU v7x, 256 devices: a whole 4x4x8 slice. The times are simulated.
256 devices in a mesh: group: 16 (over z_lo, x), expert: 16 (over y, z_hi, core).
Axes of the slice: x: 4, y: 4, z: 8 (z_hi: 2, z_lo: 4; z = z_hi * 4 + z_lo), core: 2. Of those that a mesh axis runs over, the one named last changes fastest.
Arguments:
- query_nope: bfloat16 [2048, 16, 128], P('group', 'expert'), may hold values from -6 to 6
- query_rope: bfloat16 [2048, 16, 64], P('group', 'expert'), may hold values from -8 to 8
- absorb_weight: bfloat16 [16, 128, 512], P('expert'), may hold values from -0.5 to 0.5
- value_weight: bfloat16 [16, 512, 128], P('expert'), may hold values from -1 to 1
- output_weight: bfloat16 [2048, 2048], P('expert'), may hold values from -0.25 to 0.25
- cache_latent: bfloat16 [32, 1024, 512], P('group'), may hold values from -6 to 6
- cache_rope: bfloat16 [32, 1024, 64], P('group'), may hold values from -8 to 8
- node_length: int32 [32], P('group'), may hold values from 128 to 1024, as said below
- new_latent: bfloat16 [2048, 512], P('group'), may hold values from -6 to 6
- new_rope: bfloat16 [2048, 64], P('group'), may hold values from -8 to 8
- parent_node: int32 [32], replicated, may hold values from 0 to 31, as said below
- leaf_node: int32 [256], replicated, may hold values from 0 to 31, as said below
- residual: bfloat16 [2048, 2048], P(('group', 'expert')), may hold values from -6 to 6
- norm_gain: bfloat16 [2048], replicated, may hold values from 0.5 to 1.5
- router_weight: bfloat16 [2048, 64], replicated, may hold values from -0.25 to 0.25
- routes: int32 [2048, 6], P(('group', 'expert')), may hold values from 0 to 63, all different within a row; in each aligned block of 8 rows (0 to 7, 8 to 15, ...) at most 2 rows name the same one
- expert_gate: bfloat16 [256, 2048, 352], P(('group', 'expert')), may hold values from -0.125 to 0.125
- expert_up: bfloat16 [256, 2048, 352], P(('group', 'expert')), may hold values from -0.125 to 0.125
- expert_down: bfloat16 [256, 352, 2048], P(('group', 'expert')), may hold values from -0.15625 to 0.15625
- shared_gate: bfloat16 [2048, 2816], P(None, 'group'), may hold values from -0.125 to 0.125
- shared_up: bfloat16 [2048, 2816], P(None, 'group'), may hold values from -0.125 to 0.125
- shared_down: bfloat16 [2816, 2048], P('group'), may hold values from -0.109375 to 0.109375
Outputs:
- layer_out: bfloat16 [2048, 2048], P(('group', 'expert'))
Inputs may be any that keep to these rules, and one draw needn't show every extreme that they name: `parent_node`: a root is its own parent; every other node's parent is one level nearer the root in a tree of three levels. leaf_node[r], its parent and that node's parent are three different nodes, the path from a leaf to a root. `node_length`: some node holds all 1024 slots. `routes`: the 6 experts of a token differ; in the 8 rows of one device no expert is named more than 2 times.
All inputs are finite; a program needn't handle non-finite values.
Results may differ from a plain program's by a relative error of at most 0.022.
Values may be sent and summed in bfloat16 or wider, within the bound.
A program may use at most 128 MiB of HBM per device.

v0:
```python
import jax
import jax.numpy as jnp
from jax import lax
from jax.sharding import PartitionSpec as P

ROUTE_SCALE = 2.446
NEGATIVE = -1e30
EPSILON = 1e-06


def block_partial(query_lat, query_rot, key_lat, key_rot, usable, scaling):
    scores = jnp.einsum("bhl,kl->bhk", query_lat, key_lat, preferred_element_type=jnp.float32)
    scores = scores + jnp.einsum(
        "bhr,kr->bhk", query_rot, key_rot, preferred_element_type=jnp.float32
    )
    scores = jnp.where(usable[:, None, :], scores * scaling, NEGATIVE)
    top_score = jnp.max(scores, axis=-1)
    weights = jnp.where(usable[:, None, :], jnp.exp(scores - top_score[..., None]), 0.0).astype(
        jnp.bfloat16
    )
    totals = jnp.sum(weights.astype(jnp.float32), axis=-1)
    summed = jnp.einsum("bhk,kl->bhl", weights, key_lat, preferred_element_type=jnp.float32)
    return (top_score, totals, summed)


def merge_pair(former, latter):
    top_score = jnp.maximum(former[0], latter[0])
    scale_one = jnp.exp(former[0] - top_score)
    scale_two = jnp.exp(latter[0] - top_score)
    totals = former[1] * scale_one + latter[1] * scale_two
    summed = former[2] * scale_one[..., None] + latter[2] * scale_two[..., None]
    return (top_score, totals, summed)


def path_nodes(parent_node, leaf_node):
    identity = jnp.arange(parent_node.shape[0], dtype=jnp.int32)
    middle = jnp.sum(
        jnp.where(leaf_node[:, None] == identity[None, :], parent_node[None, :], 0), axis=1
    )
    root_node = jnp.sum(
        jnp.where(middle[:, None] == identity[None, :], parent_node[None, :], 0), axis=1
    )
    return jnp.stack([leaf_node, middle, root_node], axis=1)


def route_weights(normed, router_weight, route_rows):
    logits = jnp.dot(normed, router_weight, preferred_element_type=jnp.float32)
    sigma = jax.nn.sigmoid(logits)
    identity = jnp.arange(router_weight.shape[1], dtype=jnp.int32)
    picked = jnp.sum(jnp.where(route_rows[:, :, None] == identity, sigma[:, None, :], 0.0), axis=-1)
    return ROUTE_SCALE * picked / jnp.sum(picked, axis=-1, keepdims=True)


def slot_tables(route_rows, experts, capacity):
    tokens_here, top_count = route_rows.shape
    identity = jnp.arange(experts, dtype=jnp.int32)
    chosen = (route_rows.reshape(-1)[:, None] == identity[None, :]).astype(jnp.int32)
    earlier = jnp.cumsum(chosen, axis=0) - chosen
    ranking = jnp.sum(earlier * chosen, axis=1)
    placed = ranking[:, None] == jnp.arange(capacity, dtype=jnp.int32)[None, :]
    slot_table = ((chosen[:, :, None] > 0) & placed[:, None, :]).astype(jnp.float32)
    return slot_table.reshape(tokens_here, top_count, experts * capacity)


def block_terms(arrived, gate_w, up_w, down_w):
    gate_val = jnp.einsum("gejcd,jdf->gejcf", arrived, gate_w, preferred_element_type=jnp.float32)
    up_val = jnp.einsum("gejcd,jdf->gejcf", arrived, up_w, preferred_element_type=jnp.float32)
    hidden = (jax.nn.silu(gate_val) * up_val).astype(jnp.bfloat16)
    return jnp.einsum(
        "gejcf,jfd->gejcd", hidden, down_w, preferred_element_type=jnp.float32
    ).astype(jnp.bfloat16)


def shared_ffn(rows_in, gate_w, up_w, down_w):
    gate_val = jnp.dot(rows_in, gate_w, preferred_element_type=jnp.float32)
    up_val = jnp.dot(rows_in, up_w, preferred_element_type=jnp.float32)
    hidden = (jax.nn.silu(gate_val) * up_val).astype(jnp.bfloat16)
    return jnp.dot(hidden, down_w, preferred_element_type=jnp.float32)


def on_device(
    query_nope,
    query_rope,
    absorb_weight,
    value_weight,
    output_weight,
    cache_latent,
    cache_rope,
    node_length,
    new_latent,
    new_rope,
    parent_node,
    leaf_node,
    residual,
    norm_gain,
    router_weight,
    routes,
    expert_gate,
    expert_up,
    expert_down,
    shared_gate,
    shared_up,
    shared_down,
):
    groups = lax.axis_size("group")
    columns = lax.axis_size("expert")
    group_index = lax.axis_index("group")
    tok_grp = query_nope.shape[0]
    tok_dev = tok_grp // columns
    scaling = float(query_nope.shape[2] + query_rope.shape[2]) ** (-0.5)
    own_start = group_index * tok_grp
    own_latent = jnp.einsum(
        "thn,hnl->thl", query_nope, absorb_weight, preferred_element_type=jnp.float32
    ).astype(jnp.bfloat16)
    all_latent, all_rope = (
        lax.all_gather(own_latent, "group", axis=0, tiled=True),
        lax.all_gather(query_rope, "group", axis=0, tiled=True),
    )
    requests = leaf_node.shape[0]
    per_request = all_latent.shape[0] // requests
    path_table = path_nodes(parent_node, leaf_node)
    node_grp = cache_latent.shape[0]
    positions = jnp.arange(cache_latent.shape[1], dtype=jnp.int32)
    running = None
    for slot_index in range(node_grp):
        node_id = group_index * node_grp + slot_index
        on_path = jnp.any(path_table == node_id, axis=1)
        token_on = jnp.repeat(on_path, per_request)
        usable = token_on[:, None] & (positions < node_length[slot_index])[None, :]
        block_part = block_partial(
            all_latent, all_rope, cache_latent[slot_index], cache_rope[slot_index], usable, scaling
        )
        running = block_part if running is None else merge_pair(running, block_part)
    dev_peak, dev_total, dev_sum = running
    global_peak = lax.pmax(dev_peak, "group")
    factor = jnp.exp(dev_peak - global_peak)
    home_sum, home_total = (
        lax.psum_scatter(dev_sum * factor[..., None], "group", scatter_dimension=0, tiled=True),
        lax.psum_scatter(dev_total * factor, "group", scatter_dimension=0, tiled=True),
    )
    home_peak = lax.dynamic_slice_in_dim(global_peak, own_start, tok_grp, 0)
    request_of = jnp.arange(tok_grp, dtype=jnp.int32) // per_request
    order_pos = jnp.arange(tok_grp, dtype=jnp.int32)
    causal = (request_of[:, None] == request_of[None, :]) & (
        order_pos[None, :] <= order_pos[:, None]
    )
    new_block = block_partial(own_latent, query_rope, new_latent, new_rope, causal, scaling)
    final_peak, final_total, final_sum = merge_pair((home_peak, home_total, home_sum), new_block)
    attended = (final_sum / final_total[..., None]).astype(jnp.bfloat16)
    valued = jnp.einsum(
        "thl,hlv->thv", attended, value_weight, preferred_element_type=jnp.float32
    ).astype(jnp.bfloat16)
    valued = valued.reshape(tok_grp, -1)
    attention = lax.psum_scatter(
        jnp.dot(valued, output_weight, preferred_element_type=jnp.float32).astype(jnp.bfloat16),
        "expert",
        scatter_dimension=0,
        tiled=True,
    ).astype(jnp.float32)
    hidden_state = residual.astype(jnp.float32) + attention
    normed = (
        hidden_state
        * lax.rsqrt(jnp.mean(hidden_state * hidden_state, axis=-1, keepdims=True) + EPSILON)
        * norm_gain.astype(jnp.float32)
    ).astype(jnp.bfloat16)
    experts = router_weight.shape[1]
    top_count = routes.shape[1]
    width = normed.shape[1]
    capacity = max(2, (tok_dev * top_count + experts - 1) // experts)
    items_dev = expert_gate.shape[0]
    blocks_per = items_dev * groups * columns // experts
    weights_here = route_weights(normed, router_weight, routes)
    slot_table = slot_tables(routes, experts, capacity)
    dispatch = jnp.sum(slot_table, axis=1)
    packed = jnp.dot(
        dispatch.T.astype(jnp.bfloat16), normed, preferred_element_type=jnp.float32
    ).astype(jnp.bfloat16)
    packed = jnp.broadcast_to(
        packed.reshape(experts, 1, capacity, width), (experts, blocks_per, capacity, width)
    )
    packed = packed.reshape(groups, columns, items_dev, capacity, width)
    arrived = lax.all_to_all(
        lax.all_to_all(packed, "group", split_axis=0, concat_axis=0, tiled=True),
        "expert",
        split_axis=1,
        concat_axis=1,
        tiled=True,
    )
    outputs = block_terms(arrived, expert_gate, expert_up, expert_down)
    returned = lax.all_to_all(
        lax.all_to_all(outputs, "group", split_axis=0, concat_axis=0, tiled=True),
        "expert",
        split_axis=1,
        concat_axis=1,
        tiled=True,
    )
    combined = jnp.sum(
        returned.reshape(experts, blocks_per, capacity, width).astype(jnp.float32), axis=1
    )
    combined = combined.reshape(experts * capacity, width)
    combine = jnp.sum(slot_table * weights_here[:, :, None], axis=1)
    routed = jnp.dot(combine, combined, precision=lax.Precision.HIGHEST)
    column_normed = lax.all_gather(normed, "group", axis=0, tiled=True)
    shared = lax.psum_scatter(
        shared_ffn(column_normed, shared_gate, shared_up, shared_down).astype(jnp.bfloat16),
        "group",
        scatter_dimension=0,
        tiled=True,
    ).astype(jnp.float32)
    return (hidden_state + routed + shared).astype(jnp.bfloat16)


def solution(mesh):
    in_specs = (
        P("group", "expert", None),
        P("group", "expert", None),
        P("expert", None, None),
        P("expert", None, None),
        P("expert", None),
        P("group", None, None),
        P("group", None, None),
        P("group"),
        P("group", None),
        P("group", None),
        P(),
        P(),
        P(("group", "expert"), None),
        P(),
        P(),
        P(("group", "expert"), None),
        P(("group", "expert"), None, None),
        P(("group", "expert"), None, None),
        P(("group", "expert"), None, None),
        P(None, "group"),
        P(None, "group"),
        P("group", None),
    )
    out_specs = P(("group", "expert"), None)
    return jax.shard_map(
        on_device, mesh=mesh, in_specs=in_specs, out_specs=out_specs, check_vma=False
    )
```

profile of v0, /device:TPU:24, one launch (start us, length us, event | category | flops | bytes accessed | tf_op | source)
XLA Modules:
  0.0 776.0 jit_solution(715661644524481685)
XLA Ops:
  13.8 45.6 %all_gather.10 = bf16[2048,1,64]{0,2,1:T(8,128)(2,1)S(1)} all-gather(bf16[128,1,64]{0,2,1:T(8,128)(2,1)} %param.23), channel_id=1, replica_groups=mesh['group'=16,'expert'=16] {'group'}, dimensions={0}, use_global_device_ids=true | all-gather | bytes 278528 | tf_op jit(solution)/shard_map/all_gather | solution.py:117
  59.4 27.4 %all-gather.2.cloned.1.call-done = bf16[2048,1,512]{0,2,1:T(8,128)(2,1)} async-done(((bf16[128,1,512]{0,2,1:T(8,128)(2,1)}), bf16[2048,1,512]{0,2,1:T(8,128)(2,1)}) %all-gather.2.cloned.1.call-update) | async-done | bytes 2097168 | tf_op jit(solution)/shard_map/all_gather | solution.py:116
  86.9 4.3 fusion.9
  93.4 2.5 convert_reduce_fusion.1
  95.9 5.0 fusion.56
  103.3 4.4 fusion.106
  107.8 43.3 %pmax.7 = f32[2048,1]{0,1:T(1,128)S(1)} all-reduce(f32[2048,1]{0,1:T(1,128)S(1)} %max.32), channel_id=1, replica_groups=mesh['group'=16,'expert'=16] {'group'}, use_global_device_ids=true, to_apply=%region_6.7 | all-reduce | flops 2048 | bytes 16384 | tf_op jit(solution)/shard_map/pmax | solution.py:135
  151.1 4.6 convert_reduce_fusion
  157.3 7.8 %multiply_bitcast_fusion = f32[2048,1,512]{2,0,1:T(8,128)} fusion(f32[2048,512]{1,0:T(8,128)} %fusion.56, f32[2048]{0:T(1024)S(1)} %bitcast.209, f32[2048]{0:T(1024)S(1)} %get-tuple-element.19, f32[2048]{0:T(1024)S(1)} %get-tuple-element.18, bf16[2,1024,512]{2,1,0:T(8,128)(2,1)} %param.27, f32[2048,1024]{0,1:T(8,128)} %get-tuple-element.29, ...), kind=kOutput, calls=%fused_computation.8 | convolution fusion | flops 2160066560 | bytes 17861632 | tf_op jit(solution)/shard_map/bhk,kl->bhl/dot_general | solution.py:22
  166.5 73.2 %reduce-scatter.13.cloned.1.call-done = f32[128,1]{1,0:T(8,128)} async-done(((f32[2048,1]{1,0:T(8,128)}), f32[128,1]{1,0:T(8,128)}) %reduce-scatter.13.cloned.1.call-update) | async-done | bytes 528
  240.6 92.1 %reduce-scatter.7.cloned.1.call-done = f32[128,1,512]{2,0,1:T(8,128)} async-done(((f32[2048,1,512]{2,0,1:T(8,128)}), f32[128,1,512]{2,0,1:T(8,128)}) %reduce-scatter.7.cloned.1.call-update) | async-done | bytes 262160 | tf_op jit(solution)/shard_map/reduce_scatter | solution.py:138
  335.9 73.8 %reduce-scatter.9.cloned.1.call-done = bf16[8,2048]{1,0:T(8,128)(2,1)} async-done(((bf16[128,2048]{1,0:T(8,128)(2,1)}), bf16[8,2048]{1,0:T(8,128)(2,1)}) %reduce-scatter.9.cloned.1.call-update) | async-done | bytes 32784 | tf_op jit(solution)/shard_map/reduce_scatter | solution.py:154
  415.8 51.6 %all_to_all.20 = bf16[16,16,1,2,2048]{4,1,3,2,0:T(8,128)(2,1)S(1)} all-to-all(bf16[16,16,1,2,2048]{4,1,3,2,0:T(8,128)(2,1)S(1)} %copy.45), channel_id=1, replica_groups=mesh['group'=16,'expert'=16] {'group'}, dimensions={0} | all-to-all | bytes 4194304 | tf_op jit(solution)/shard_map/all_to_all | solution.py:183
  469.6 58.4 %all_to_all.21 = bf16[16,16,1,2,2048]{4,3,0,2,1:T(2,128)(2,1)S(1)} all-to-all(bf16[16,16,1,2,2048]{4,3,0,2,1:T(2,128)(2,1)S(1)} %copy.46), channel_id=1, replica_groups=mesh['group'=16,'expert'=16] {'expert'}, dimensions={1} | all-to-all | bytes 4194304 | tf_op jit(solution)/shard_map/all_to_all | solution.py:182
  528.0 2.4 fusion.18
  530.4 5.6 fusion.2
  536.0 52.9 %all_to_all.22 = bf16[16,16,1,2,2048]{4,1,3,2,0:T(8,128)(2,1)S(1)} all-to-all(bf16[16,16,1,2,2048]{4,1,3,2,0:T(8,128)(2,1)} %fusion.2), channel_id=1, replica_groups=mesh['group'=16,'expert'=16] {'group'}, dimensions={0} | all-to-all | bytes 4194304 | tf_op jit(solution)/shard_map/all_to_all | solution.py:191
  588.9 3.5 copy.49
  592.4 6.0 all-to-all-start.3
  598.4 81.2 %all_gather.11 = bf16[128,2048]{1,0:T(8,128)(2,1)S(1)} all-gather(bf16[8,2048]{1,0:T(8,128)(2,1)} %copy-done.3), channel_id=1, replica_groups=mesh['group'=16,'expert'=16] {'group'}, dimensions={0}, use_global_device_ids=true | all-gather | bytes 557056 | tf_op jit(solution)/shard_map/all_gather | solution.py:203
  682.5 3.2 convolution_convert_fusion.1
  687.0 5.2 copy.51
  692.2 5.0 reduce_sum.128
  698.0 68.9 %reduce-scatter.11.cloned.1.call-done = bf16[8,2048]{1,0:T(8,128)(2,1)} async-done(((bf16[128,2048]{1,0:T(8,128)(2,1)}), bf16[8,2048]{1,0:T(8,128)(2,1)}) %reduce-scatter.11.cloned.1.call-update) | async-done | bytes 32784 | tf_op jit(solution)/shard_map/reduce_scatter | solution.py:204
  (97 shorter events, 33.8 us)
Async XLA Ops:
  6.5 523.9 %copy-start = (bf16[1,352,2048]{2,1,0:T(8,128)(2,1)S(1)}, bf16[1,352,2048]{2,1,0:T(8,128)(2,1)}, u32[]{:S(2)}) copy-start(bf16[1,352,2048]{2,1,0:T(8,128)(2,1)} %param.40) | copy-start | bytes 4325380
  6.5 80.3 %all-gather.2.cloned.1.call-start = ((), (), s32[]{:S(2)}) async-start(), calls=%async_computation.8 | async-start | bytes 2228224 | tf_op jit(solution)/shard_map/all_gather | solution.py:116
  8.4 231.3 %reduce-scatter.13.cloned.1.call-start = ((), (), s32[]{:S(2)}) async-start(), calls=%async_computation.12 | async-start | bytes 1114112
  59.4 31.7 %copy-start.6 = (bf16[2,1024,64]{1,2,0:T(8,128)(2,1)S(1)}, bf16[2,1024,64]{1,2,0:T(8,128)(2,1)}, u32[]{:S(2)}) copy-start(bf16[2,1024,64]{1,2,0:T(8,128)(2,1)} %param.28) | copy-start | bytes 786436
  93.4 2.5 copy-start.14
  95.9 5.1 copy-start.15
  157.2 175.5 %reduce-scatter.7.cloned.1.call-start = ((), (), s32[]{:S(2)}) async-start(), calls=%async_computation.9 | async-start | bytes 4456448 | tf_op jit(solution)/shard_map/reduce_scatter | solution.py:138
  165.1 0.7 copy-start.11
  165.1 0.8 copy-start.13
  165.1 0.9 copy-start.10
  165.1 0.9 copy-start.12
  165.1 1.1 copy-start.2
  165.1 1.1 copy-start.9
  165.1 168.8 %copy-start.4 = (bf16[128,2048]{1,0:T(8,128)(2,1)S(1)}, bf16[128,2048]{1,0:T(8,128)(2,1)}, u32[]{:S(2)}) copy-start(bf16[128,2048]{1,0:T(8,128)(2,1)} %param.26) | copy-start | bytes 1572868
  165.2 168.8 %copy-start.8 = (bf16[1,512,128]{2,1,0:T(8,128)(2,1)S(1)}, bf16[1,512,128]{2,1,0:T(8,128)(2,1)}, u32[]{:S(2)}) copy-start(bf16[1,512,128]{2,1,0:T(8,128)(2,1)} %param.25) | copy-start | bytes 393220
  165.2 244.6 %copy-start.5 = (bf16[8,2048]{1,0:T(8,128)(2,1)S(1)}, bf16[8,2048]{1,0:T(8,128)(2,1)}, u32[]{:S(2)}) copy-start(bf16[8,2048]{1,0:T(8,128)(2,1)} %param.34) | copy-start | bytes 98308
  165.2 246.3 %copy-start.7 = (bf16[2048,64]{0,1:T(8,128)(2,1)S(1)}, bf16[2048,64]{0,1:T(8,128)(2,1)}, u32[]{:S(2)}) copy-start(bf16[2048,64]{0,1:T(8,128)(2,1)} %param.36) | copy-start | bytes 786436
  165.2 244.5 %reduce-scatter.9.cloned.1.call-start = ((), (), s32[]{:S(2)}) async-start(), calls=%async_computation.10 | async-start | bytes 557056 | tf_op jit(solution)/shard_map/reduce_scatter | solution.py:154
  411.5 1.5 copy-start.3
  467.4 60.5 %copy-start.16 = (bf16[1,2048,352]{1,2,0:T(8,128)(2,1)S(1)}, bf16[1,2048,352]{1,2,0:T(8,128)(2,1)}, u32[]{:S(2)}) copy-start(bf16[1,2048,352]{1,2,0:T(8,128)(2,1)} %param.38) | copy-start | bytes 4325380
  592.4 93.4 %all-to-all-start.3 = ((bf16[16,16,1,2,2048]{4,3,0,2,1:T(2,128)(2,1)}), bf16[16,16,1,2,2048]{4,3,0,2,1:T(2,128)(2,1)S(1)}, u32[]{:S(2)}, u32[]{:S(2)}) async-start(bf16[16,16,1,2,2048]{4,3,0,2,1:T(2,128)(2,1)} %copy.49), calls=%async_computation.5 | async-start | bytes 4194304 | tf_op jit(solution)/shard_map/all_to_all | solution.py:190
  598.4 168.6 %reduce-scatter.11.cloned.1.call-start = ((), (), s32[]{:S(2)}) async-start(), calls=%async_computation.11 | async-start | bytes 557056 | tf_op jit(solution)/shard_map/reduce_scatter | solution.py:204
  679.6 0.8 copy-start.1
Sparse Core Ops, SparseCore 0:
  9.1 77.7 all-gather.1
  157.3 82.3 reduce-scatter.12
  242.4 90.2 reduce-scatter.6
  337.2 72.5 reduce-scatter.8
  685.9 80.9 reduce-scatter.10
where the time goes:
time: 785 us; the launch traced here: 776 us
  waiting for transfers between devices  336 us (43%)
  blocking collectives  333 us (42%)
  matrix products  46.6 us (6%)
  other arithmetic  20.4 us (3%)
  local copies, waits for them, and re-layouts  20.2 us (3%)
  between operations  14 us (2%)
    reduce_scatter x1, waiting for transfers between devices, on_device(): lax.psum_scatter(dev_sum * factor[..., None], 'group', scatter_dimension=...  92.1 us
    all_gather x1, blocking collectives, on_device(): column_normed = lax.all_gather(normed, 'group', axis=0, tiled=True)  81.2 us
    reduce_scatter x1, waiting for transfers between devices, on_device(): lax.psum_scatter(jnp.dot(valued, output_weight, preferred_element_type=jn...  73.8 us
    unnamed x6, waiting for transfers between devices  73.3 us
    reduce_scatter x1, waiting for transfers between devices, on_device(): lax.psum_scatter(shared_ffn(column_normed, shared_gate, shared_up, shared...  68.9 us
    all_to_all x1, blocking collectives, on_device(): lax.all_to_all(lax.all_to_all(packed, 'group', split_axis=0, concat_axis=...  58.4 us
    all_to_all x1, blocking collectives, on_device(): lax.all_to_all(outputs, 'group', split_axis=0, concat_axis=0, tiled=True)  52.9 us
    all_to_all x1, blocking collectives, on_device(): lax.all_to_all(packed, 'group', split_axis=0, concat_axis=0, tiled=True)  51.6 us
  transfers between devices with their start and end apart: 6, of which 5 were waited for; matrix products, arithmetic and copies ran while one was open for 4% of the time, Pallas kernels for 0%

commit v1 on v0

v1 whole, which is shorter than its diff:
```python
import jax
import jax.numpy as jnp
from jax import lax
from jax.experimental import pallas as pl
from jax.experimental.pallas import tpu as pltpu
from jax.sharding import PartitionSpec as P

ROUTE_SCALE = 2.446
NEGATIVE = -1e30
EPSILON = 1e-06
MESH = pl.DeviceIdType.MESH
F32 = jnp.float32
BF16 = jnp.bfloat16
VMEM = pltpu.VMEM
DMA = pltpu.SemaphoreType.DMA

REQ = 16
QT = 8
MSG = 1024 + 128


def vmem_spec():
    return pl.BlockSpec(memory_space=pltpu.VMEM)


def any_spec():
    return pl.BlockSpec(memory_space=pl.ANY)


def coords():
    g = lax.axis_index("group")
    e = lax.axis_index("expert")
    zl, x = g // 4, g % 4
    y, zh, c = e // 4, (e % 4) // 2, e % 2
    return g, e, x, y, zl, zh, c


def dev(x, y, zl, zh, c):
    return (zl * 4 + x, y * 4 + zh * 2 + c)


def remote(src, dst, send, recv, device):
    return pltpu.make_async_remote_copy(
        src_ref=src,
        dst_ref=dst,
        send_sem=send,
        recv_sem=recv,
        device_id=device,
        device_id_type=MESH,
    )


def greet(barrier, device):
    pl.semaphore_signal(barrier, inc=1, device_id=device, device_id_type=MESH)


def dot(a, b):
    return jnp.dot(a, b, preferred_element_type=F32)


def flag(condition):
    return jnp.where(condition, 1.0, 0.0).astype(BF16)


def dot_nt(a, b):
    return lax.dot_general(a, b, (((1,), (1,)), ((), ())), preferred_element_type=F32)


def gather_kernel(q_ref, routes_ref, resid_ref, qall, routes8, resid2, qs, qr, rs, rr, zs, zr):
    g, e, x, y, zl, zh, c = coords()
    barrier = pltpu.get_barrier_semaphore()

    def hello(i, carry):
        greet(barrier, (lax.rem(g + i, 16), e))
        return carry

    lax.fori_loop(1, 16, hello, 0)
    for k in (1, 3, 5, 7):
        s = lax.rem(zl * 2 + zh + k, 8)
        greet(barrier, dev(x, y, s // 2, s % 2, c))
    pl.semaphore_wait(barrier, 19)

    def send(i, carry):
        remote(q_ref, qall.at[g], qs.at[i], qr.at[i], (lax.rem(g + i, 16), e)).start()
        return carry

    lax.fori_loop(1, 16, send, 0)
    me = zl * 2 + zh
    for k in range(1, 8):
        s = lax.rem(me + k, 8)
        remote(routes_ref, routes8.at[me], rs.at[k], rr.at[k], dev(x, y, s // 2, s % 2, c)).start()
    partner = dev(x, y, zl, 1 - zh, c)
    remote(resid_ref, resid2.at[zh], zs, zr, partner).start()
    qall[g] = q_ref[...]
    routes8[me] = routes_ref[...]
    resid2[zh] = resid_ref[...]
    remote(resid_ref, resid2.at[1 - zh], zs, zr, partner).wait()
    for k in range(1, 8):
        s = lax.rem(me - k + 8, 8)
        remote(routes_ref, routes8.at[s], rs.at[k], rr.at[k], partner).wait()

    def wait(i, carry):
        remote(q_ref, qall.at[lax.rem(g - i + 16, 16)], qs.at[i], qr.at[i], partner).wait()
        return carry

    lax.fori_loop(1, 16, wait, 0)


def gather(q2, routes_pad, residual):
    return pl.pallas_call(
        gather_kernel,
        name="gather_queries",
        out_shape=(
            jax.ShapeDtypeStruct((16,) + q2.shape, q2.dtype),
            jax.ShapeDtypeStruct((8,) + routes_pad.shape, routes_pad.dtype),
            jax.ShapeDtypeStruct((2,) + residual.shape, residual.dtype),
        ),
        in_specs=[vmem_spec()] * 3,
        out_specs=(vmem_spec(),) * 3,
        scratch_shapes=[
            DMA((16,)),
            DMA((16,)),
            DMA((8,)),
            DMA((8,)),
            DMA,
            DMA,
        ],
        compiler_params=pltpu.CompilerParams(
            collective_id=0, has_side_effects=True, vmem_limit_bytes=32 << 20
        ),
    )(q2, routes_pad, residual)


TILE = 32


def split3(v):
    hi = v.astype(BF16)
    rest = v - hi.astype(F32)
    mid = rest.astype(BF16)
    low = (rest - mid.astype(F32)).astype(BF16)
    return hi.astype(F32), mid.astype(F32), low.astype(F32)


def join3(part):
    return part[:, 0:8] + part[:, 8:16] + part[:, 16:24]


def on_path_row(leaf_row, parent_col, node):
    nodes = parent_col.shape[0]
    ids = lax.broadcasted_iota(jnp.int32, (nodes, leaf_row.shape[1]), 0)
    mid = jnp.sum(jnp.where(leaf_row == ids, parent_col, 0), axis=0, keepdims=True)
    top = jnp.sum(jnp.where(mid == ids, parent_col, 0), axis=0, keepdims=True)
    return (leaf_row == node) | (mid == node) | (top == node)


def on_path_col(leaf_col, parent_row, node):
    nodes = parent_row.shape[1]
    ids = lax.broadcasted_iota(jnp.int32, (leaf_col.shape[0], nodes), 1)
    mid = jnp.sum(jnp.where(leaf_col == ids, parent_row, 0), axis=1, keepdims=True)
    top = jnp.sum(jnp.where(mid == ids, parent_row, 0), axis=1, keepdims=True)
    return (leaf_col == node) | (mid == node) | (top == node)


def attn_kernel(
    len_ref,
    q_ref,
    absorb_ref,
    value_ref,
    lat_ref,
    rope_ref,
    leaf_row_ref,
    leaf_col_ref,
    parent_row_ref,
    parent_col_ref,
    out_ref,
    acc,
):
    g = lax.axis_index("group")
    requests = q_ref.shape[0]
    slots, keys = lat_ref.shape[0], lat_ref.shape[1]
    scaling = float(128 + 64) ** (-0.5)
    earlier = flag(
        lax.broadcasted_iota(jnp.int32, (requests, requests), 0)
        < lax.broadcasted_iota(jnp.int32, (requests, requests), 1)
    )
    later = flag(
        lax.broadcasted_iota(jnp.int32, (requests, requests), 1)
        < lax.broadcasted_iota(jnp.int32, (requests, requests), 0)
    )
    acc[...] = jnp.zeros_like(acc)
    lane = lax.broadcasted_iota(jnp.int32, (TILE, 128), 1)
    positions = lax.broadcasted_iota(jnp.int32, (1, keys), 1)
    on_cols = []
    for slot in range(slots):
        node = g * slots + slot
        on_row = on_path_row(leaf_row_ref[...], parent_col_ref[...], node)
        on_col = on_path_col(leaf_col_ref[...], parent_row_ref[...], node)
        on_cols.append(on_col)
        row_f = jnp.where(on_row, 1.0, 0.0)
        count = jnp.sum(row_f).astype(jnp.int32)
        rank_row = dot(jnp.broadcast_to(row_f, (8, requests)).astype(BF16), earlier)[0:1]
        rank_row = jnp.where(on_row, rank_row, -1.0).astype(jnp.int32)
        rank_col = dot(
            later, jnp.broadcast_to(jnp.where(on_col, 1.0, 0.0), (requests, 128)).astype(BF16)
        )[:, 0:1]
        rank_col = jnp.where(on_col, rank_col, -1.0).astype(jnp.int32)
        length = len_ref[slot]

        def tile(step, carry):
            base = step * TILE
            pick = flag(rank_row == lax.broadcasted_iota(jnp.int32, (TILE, requests), 0) + base)
            place = flag(rank_col == lax.broadcasted_iota(jnp.int32, (requests, TILE), 1) + base)
            qt = dot(pick, q_ref[...]).astype(BF16)
            nope = jnp.concatenate([qt[:, j * 128 : j * 128 + 128] for j in range(QT)], axis=0)
            rot = jnp.concatenate(
                [qt[:, 1024 + j * 64 : 1024 + j * 64 + 64] for j in range(QT)], axis=0
            )
            lat = dot(nope, absorb_ref[...]).astype(BF16)
            scores = dot_nt(lat, lat_ref[slot]) + dot_nt(rot, rope_ref[slot])
            scores = jnp.where(positions < length, scores * scaling, NEGATIVE)
            top = jnp.max(scores, axis=1, keepdims=True)
            weights = jnp.exp(scores - top).astype(BF16)
            total = jnp.sum(weights.astype(F32), axis=1, keepdims=True)
            summed = dot(weights, lat_ref[slot])
            attended = (summed / total).astype(BF16)
            valued = dot(attended, value_ref[...]).astype(BF16)
            log_sum = top + jnp.log(total)
            parts = split3(log_sum)
            tail = jnp.zeros((TILE, 128), F32)
            for j in range(QT):
                for k in range(3):
                    piece = parts[k][j * TILE : (j + 1) * TILE]
                    tail = jnp.where(lane == k * 8 + j, piece, tail)
            block = jnp.concatenate(
                [valued[j * TILE : (j + 1) * TILE] for j in range(QT)] + [tail.astype(BF16)],
                axis=1,
            )
            acc[slot] += dot(place, block)
            return carry

        lax.fori_loop(0, (count + TILE - 1) // TILE, tile, 0)

    logs = [
        jnp.where(on_cols[s], join3(acc[s, :, 1024:]), NEGATIVE) for s in range(slots)
    ]
    top = logs[0]
    for s in range(1, slots):
        top = jnp.maximum(top, logs[s])
    shares = [jnp.exp(v - top) for v in logs]
    total = shares[0]
    for s in range(1, slots):
        total = total + shares[s]
    log_sum = top + jnp.log(total)
    for j in range(QT):
        out = 0.0
        for s in range(slots):
            out = out + (shares[s] / total)[:, j : j + 1] * acc[s, :, j * 128 : j * 128 + 128]
        out_ref[:, j * 128 : j * 128 + 128] = out.astype(BF16)
    parts = split3(log_sum)
    lane = lax.broadcasted_iota(jnp.int32, (requests, 128), 1)
    tail = jnp.zeros((requests, 128), F32)
    for j in range(QT):
        for k in range(3):
            tail = jnp.where(lane == k * 8 + j, parts[k][:, j : j + 1], tail)
    out_ref[:, 1024:] = tail.astype(BF16)


def attend(node_length, q_all, absorb, value, cache_latent, cache_rope, leaf, parent):
    requests = q_all.shape[0]
    slots = cache_latent.shape[0]
    return pl.pallas_call(
        attn_kernel,
        name="attend_nodes",
        out_shape=jax.ShapeDtypeStruct((requests, MSG), BF16),
        in_specs=[pl.BlockSpec(memory_space=pltpu.SMEM)] + [vmem_spec()] * 9,
        out_specs=vmem_spec(),
        scratch_shapes=[VMEM((slots, requests, MSG), F32)],
        compiler_params=pltpu.CompilerParams(vmem_limit_bytes=48 << 20),
    )(
        node_length,
        q_all,
        absorb,
        value,
        cache_latent,
        cache_rope,
        leaf[None, :],
        leaf[:, None],
        parent[None, :],
        parent[:, None],
    )


def merge_kernel(
    msg_ref,
    q_ref,
    absorb_ref,
    value_ref,
    newlat_ref,
    newrope_ref,
    outw_ref,
    resid_ref,
    gain_ref,
    hidden_ref,
    normed_ref,
    got,
    valued_s,
    csend,
    crecv,
    acc,
    ysend,
    yrecv,
    zsend,
    zrecv,
    ms,
    mr,
    cs,
    cr,
    ys,
    yr,
    hs,
    hr,
    ls,
    lr,
):
    g, e, x, y, zl, zh, c = coords()
    barrier = pltpu.get_barrier_semaphore()

    def hello(i, carry):
        greet(barrier, (lax.rem(g + i, 16), e))
        return carry

    lax.fori_loop(1, 16, hello, 0)
    other = dev(x, y, zl, zh, 1 - c)
    partner = dev(x, y, zl, 1 - zh, c)
    greet(barrier, other)
    greet(barrier, partner)
    for i in range(1, 4):
        greet(barrier, dev(x, lax.rem(y + i, 4), zl, zh, c))
    pl.semaphore_wait(barrier, 20)

    def send(i, carry):
        peer = lax.rem(g + i, 16)
        remote(msg_ref.at[peer], got.at[g], ms.at[i], mr.at[i], (peer, e)).start()
        return carry

    lax.fori_loop(1, 16, send, 0)
    got[g] = msg_ref[g]

    scaling = float(128 + 64) ** (-0.5)
    q = q_ref[...]
    nope = jnp.concatenate([q[:, j * 128 : j * 128 + 128] for j in range(QT)], axis=0)
    rot = jnp.concatenate([q[:, 1024 + j * 64 : 1024 + j * 64 + 64] for j in range(QT)], axis=0)
    lat = dot(nope, absorb_ref[...]).astype(BF16)
    scores = dot_nt(lat, newlat_ref[...]) + dot_nt(rot, newrope_ref[...])
    rows = REQ * QT
    qi = lax.broadcasted_iota(jnp.int32, (rows, rows), 0)
    ki = lax.broadcasted_iota(jnp.int32, (rows, rows), 1)
    usable = ((qi % REQ) == (ki // QT)) & ((ki % QT) <= (qi // REQ))
    scores = jnp.where(usable, scores * scaling, NEGATIVE)
    top = jnp.max(scores, axis=1, keepdims=True)
    weights = jnp.where(usable, jnp.exp(scores - top), 0.0).astype(BF16)
    total = jnp.sum(weights.astype(F32), axis=1, keepdims=True)
    summed = dot(weights, newlat_ref[...]) / total
    new_valued = dot(summed.astype(BF16), value_ref[...])
    new_log = top + jnp.log(total)

    def wait(i, carry):
        src = lax.rem(g - i + 16, 16)
        remote(msg_ref.at[src], got.at[src], ms.at[i], mr.at[i], other).wait()
        return carry

    lax.fori_loop(1, 16, wait, 0)

    logs = join3(got[:, :, 1024:].astype(F32).reshape(16 * REQ, 128)).reshape(16, REQ, 8)
    pieces = []
    for j in range(QT):
        log_j = logs[:, :, j : j + 1]
        new_j = new_log[j * REQ : (j + 1) * REQ]
        peak = jnp.maximum(jnp.max(log_j, axis=0), new_j)
        share = jnp.exp(log_j - peak[None])
        new_share = jnp.exp(new_j - peak)
        whole = jnp.sum(share, axis=0) + new_share
        value = jnp.sum(share * got[:, :, j * 128 : j * 128 + 128].astype(F32), axis=0)
        value = value + new_share * new_valued[j * REQ : (j + 1) * REQ]
        pieces.append((value / whole).astype(BF16))
    valued = jnp.concatenate(pieces, axis=0)
    di = lax.broadcasted_iota(jnp.int32, (rows, rows), 0)
    si = lax.broadcasted_iota(jnp.int32, (rows, rows), 1)
    req = ((di % 64) // 16) * 4 + ((di % 16) // 8) * 2 + di // 64
    perm = flag(si == (di % 8) * REQ + req)
    valued_s[...] = dot(perm, valued).astype(BF16).reshape(2, 64, 128)

    csend[...] = dot(valued_s[1 - c], outw_ref[...]).astype(BF16)
    remote(csend, crecv, cs, cr, other).start()
    own = dot(valued_s[c], outw_ref[...])
    remote(csend, crecv, cs, cr, other).wait()
    acc[...] = (own + crecv[...].astype(F32)).reshape(4, 16, 2048)
    ysend[...] = acc[...].astype(BF16)
    for i in range(1, 4):
        peer = lax.rem(y + i, 4)
        remote(ysend.at[peer], yrecv.at[i], ys.at[i], yr.at[i], dev(x, peer, zl, zh, c)).start()
    for i in range(1, 4):
        remote(ysend.at[0], yrecv.at[i], ys.at[i], yr.at[i], other).wait()
    mine = acc[y]
    for i in range(1, 4):
        mine = mine + yrecv[i].astype(F32)
    zsend[...] = mine.astype(BF16)
    remote(zsend, zrecv, hs, hr, partner).start()
    remote(zsend, zrecv, hs, hr, partner).wait()
    hidden = mine + zrecv[...].astype(F32) + resid_ref[...].reshape(16, 2048).astype(F32)
    hidden_ref[...] = hidden.reshape(2, 8, 2048)
    square = jnp.mean(hidden * hidden, axis=1, keepdims=True)
    normed = (hidden * lax.rsqrt(square + EPSILON) * gain_ref[...].astype(F32)).astype(BF16)
    normed_ref[zl] = normed
    for i in range(1, 4):
        peer = lax.rem(zl + i, 4)
        remote(
            normed_ref.at[zl], normed_ref.at[zl], ls.at[i], lr.at[i], dev(x, y, peer, zh, c)
        ).start()
    for i in range(1, 4):
        src = lax.rem(zl - i + 4, 4)
        remote(normed_ref.at[zl], normed_ref.at[src], ls.at[i], lr.at[i], other).wait()


def merge(msg, q2, absorb, value, new_latent, new_rope, outw, resid2, gain):
    return pl.pallas_call(
        merge_kernel,
        name="merge_project_norm",
        out_shape=(
            jax.ShapeDtypeStruct((2, 8, 2048), F32),
            jax.ShapeDtypeStruct((4, 16, 2048), BF16),
        ),
        in_specs=[vmem_spec()] * 9,
        out_specs=(vmem_spec(),) * 2,
        scratch_shapes=[
            VMEM((16, REQ, MSG), BF16),
            VMEM((2, 64, 128), BF16),
            VMEM((64, 2048), BF16),
            VMEM((64, 2048), BF16),
            VMEM((4, 16, 2048), F32),
            VMEM((4, 16, 2048), BF16),
            VMEM((4, 16, 2048), BF16),
            VMEM((16, 2048), BF16),
            VMEM((16, 2048), BF16),
            DMA((16,)),
            DMA((16,)),
            DMA,
            DMA,
            DMA((4,)),
            DMA((4,)),
            DMA,
            DMA,
            DMA((4,)),
            DMA((4,)),
        ],
        compiler_params=pltpu.CompilerParams(
            collective_id=1, has_side_effects=True, vmem_limit_bytes=48 << 20
        ),
    )(msg, q2, absorb, value, new_latent, new_rope, outw, resid2, gain)


def expert_kernel(
    normed_ref,
    hidden_ref,
    place_ref,
    pick_ref,
    chosen_ref,
    router_ref,
    gate_hbm,
    up_hbm,
    down_hbm,
    sgate_hbm,
    sup_hbm,
    sdown_hbm,
    out_ref,
    gate_w,
    up_w,
    down_w,
    sgate_w,
    sup_w,
    sdown_w,
    packed,
    arrived,
    across,
    own_out,
    cross_send,
    cross_recv,
    ret_send,
    ret_recv,
    share_in,
    share_send,
    share_recv,
    part,
    lsend,
    lrecv,
    hsend,
    hrecv,
    wsem,
    ds,
    dr,
    cs,
    cr,
    os_,
    or_,
    rs,
    rr,
    xs,
    xr,
    bs,
    br,
    ls,
    lr,
    hs,
    hr,
):
    g, e, x, y, zl, zh, c = coords()
    mine = x * 4 + y
    loads = [
        pltpu.make_async_copy(src, dst, wsem.at[i])
        for i, (src, dst) in enumerate(
            [
                (gate_hbm, gate_w),
                (up_hbm, up_w),
                (down_hbm, down_w),
                (sgate_hbm, sgate_w),
                (sup_hbm, sup_w),
                (sdown_hbm, sdown_w),
            ]
        )
    ]
    for load in loads:
        load.start()
    barrier = pltpu.get_barrier_semaphore()

    def plane(p):
        return dev(p // 4, p % 4, zl, zh, c)

    def hello(i, carry):
        greet(barrier, plane(lax.rem(mine + i, 16)))
        return carry

    lax.fori_loop(1, 16, hello, 0)
    other = dev(x, y, zl, zh, 1 - c)
    partner = dev(x, y, zl, 1 - zh, c)
    greet(barrier, other)
    greet(barrier, partner)
    for i in range(1, 4):
        greet(barrier, dev(x, y, lax.rem(zl + i, 4), zh, c))

    tokens = normed_ref[...]
    packed[...] = dot(place_ref[...], tokens).astype(BF16).reshape(16, 16, 2048)
    share_in[x] = normed_ref[...].reshape(4, 2, 8, 2048)[:, 0].reshape(32, 2048)

    @pl.when(zh == 1)
    def _():
        share_in[x] = normed_ref[...].reshape(4, 2, 8, 2048)[:, 1].reshape(32, 2048)

    pl.semaphore_wait(barrier, 20)

    def send(i, carry):
        p = lax.rem(mine + i, 16)
        remote(packed.at[p], arrived.at[mine], ds.at[i], dr.at[i], plane(p)).start()
        return carry

    lax.fori_loop(1, 16, send, 0)
    arrived[mine] = packed[mine]
    remote(arrived.at[mine], across.at[mine], cs.at[0], cr.at[0], other).start()
    for i in range(1, 4):
        peer = lax.rem(x + i, 4)
        remote(share_in.at[x], share_in.at[x], xs.at[i], xr.at[i], dev(peer, y, zl, zh, c)).start()

    sigma = jax.nn.sigmoid(dot(tokens, router_ref[...])) * chosen_ref[...]
    route_w = ROUTE_SCALE * sigma / jnp.sum(sigma, axis=1, keepdims=True)
    experts = chosen_ref.shape[1]
    spread = flag(
        lax.broadcasted_iota(jnp.int32, (experts, 256), 0)
        == zl * 16 + lax.broadcasted_iota(jnp.int32, (experts, 256), 1) // 16
    )
    w_hi, w_mid, w_low = split3(route_w)
    combine = (
        dot(w_hi.astype(BF16), spread)
        + dot(w_mid.astype(BF16), spread)
        + dot(w_low.astype(BF16), spread)
    ) * pick_ref[...].astype(F32)

    def forward(i, carry):
        src = lax.rem(mine - i + 16, 16)
        remote(packed.at[src], arrived.at[src], ds.at[i], dr.at[i], other).wait()
        remote(arrived.at[src], across.at[src], cs.at[i], cr.at[i], other).start()
        return carry

    lax.fori_loop(1, 16, forward, 0)
    for load in loads[:3]:
        load.wait()

    def ffn(rows, gate, up, down):
        gate_val = dot(rows, gate[...])
        up_val = dot(rows, up[...])
        hidden = (jax.nn.silu(gate_val) * up_val).astype(BF16)
        return dot(hidden, down[...])

    own_out[...] = ffn(arrived[...].reshape(256, 2048), gate_w, up_w, down_w)

    def cross(i, carry):
        src = lax.rem(mine - i + 16, 16)
        remote(arrived.at[src], across.at[src], cs.at[i], cr.at[i], other).wait()
        return carry

    lax.fori_loop(0, 16, cross, 0)
    cross_send[...] = ffn(across[...].reshape(256, 2048), gate_w, up_w, down_w).astype(BF16)
    remote(cross_send, cross_recv, os_, or_, other).start()

    for load in loads[3:]:
        load.wait()
    for i in range(1, 4):
        src = lax.rem(x - i + 4, 4)
        remote(share_in.at[x], share_in.at[src], xs.at[i], xr.at[i], other).wait()
    shared = ffn(share_in[...].reshape(128, 2048), sgate_w, sup_w, sdown_w)
    share_send[...] = shared.astype(BF16).reshape(4, 32, 2048)
    for i in range(1, 4):
        peer = lax.rem(x + i, 4)
        remote(
            share_send.at[peer], share_recv.at[i], bs.at[i], br.at[i], dev(peer, y, zl, zh, c)
        ).start()

    remote(cross_send, cross_recv, os_, or_, other).wait()
    ret_send[...] = (
        (own_out[...] + cross_recv[...].astype(F32)).astype(BF16).reshape(16, 16, 2048)
    )

    def give(i, carry):
        p = lax.rem(mine + i, 16)
        remote(ret_send.at[p], ret_recv.at[mine], rs.at[i], rr.at[i], plane(p)).start()
        return carry

    lax.fori_loop(1, 16, give, 0)
    ret_recv[mine] = ret_send[mine]
    for i in range(1, 4):
        remote(share_send.at[0], share_recv.at[i], bs.at[i], br.at[i], other).wait()
    share_sum = share_send[x].astype(F32)
    for i in range(1, 4):
        share_sum = share_sum + share_recv[i].astype(F32)

    def take(i, carry):
        src = lax.rem(mine - i + 16, 16)
        remote(ret_send.at[src], ret_recv.at[src], rs.at[i], rr.at[i], other).wait()
        return carry

    lax.fori_loop(1, 16, take, 0)
    back = ret_recv[...].reshape(256, 2048)
    c_hi = combine.astype(BF16)
    c_low = (combine - c_hi.astype(F32)).astype(BF16)
    routed = (dot(c_hi, back) + dot(c_low, back)).reshape(4, 2, 8, 2048)
    is_own = jnp.where(lax.broadcasted_iota(jnp.int32, (4, 2, 8, 2048), 1) == zh, 1.0, 0.0)
    part[...] = (routed + share_sum.reshape(4, 1, 8, 2048) * is_own).reshape(4, 16, 2048)
    lsend[...] = part[...].astype(BF16)
    for i in range(1, 4):
        peer = lax.rem(zl + i, 4)
        remote(lsend.at[peer], lrecv.at[i], ls.at[i], lr.at[i], dev(x, y, peer, zh, c)).start()
    for i in range(1, 4):
        remote(lsend.at[0], lrecv.at[i], ls.at[i], lr.at[i], other).wait()
    both = part[zl]
    for i in range(1, 4):
        both = both + lrecv[i].astype(F32)
    hsend[...] = both.reshape(2, 8, 2048).astype(BF16)
    remote(hsend.at[1 - zh], hrecv, hs, hr, partner).start()
    remote(hsend.at[1 - zh], hrecv, hs, hr, partner).wait()
    kept = jnp.where(zh == 0, both[0:8], both[8:16])
    out_ref[...] = (hidden_ref[zh] + kept + hrecv[...].astype(F32)).astype(BF16)


def experts_layer(normed, hidden, place, pick, chosen, router, weights):
    shapes = [w.shape for w in weights]
    return pl.pallas_call(
        expert_kernel,
        name="experts",
        out_shape=jax.ShapeDtypeStruct((8, 2048), BF16),
        in_specs=[vmem_spec()] * 6 + [any_spec()] * 6,
        out_specs=vmem_spec(),
        scratch_shapes=[VMEM(s, BF16) for s in shapes]
        + [
            VMEM((16, 16, 2048), BF16),
            VMEM((16, 16, 2048), BF16),
            VMEM((16, 16, 2048), BF16),
            VMEM((256, 2048), F32),
            VMEM((256, 2048), BF16),
            VMEM((256, 2048), BF16),
            VMEM((16, 16, 2048), BF16),
            VMEM((16, 16, 2048), BF16),
            VMEM((4, 32, 2048), BF16),
            VMEM((4, 32, 2048), BF16),
            VMEM((4, 32, 2048), BF16),
            VMEM((4, 16, 2048), F32),
            VMEM((4, 16, 2048), BF16),
            VMEM((4, 16, 2048), BF16),
            VMEM((2, 8, 2048), BF16),
            VMEM((8, 2048), BF16),
            DMA((6,)),
            DMA((16,)),
            DMA((16,)),
            DMA((16,)),
            DMA((16,)),
            DMA,
            DMA,
            DMA((16,)),
            DMA((16,)),
            DMA((4,)),
            DMA((4,)),
            DMA((4,)),
            DMA((4,)),
            DMA((4,)),
            DMA((4,)),
            DMA,
            DMA,
        ],
        compiler_params=pltpu.CompilerParams(
            collective_id=2, has_side_effects=True, vmem_limit_bytes=56 << 20
        ),
    )(normed, hidden, place, pick, chosen, router, *weights)


def slot_tables(routes8, experts):
    zl = lax.axis_index("group") // 4
    routes = routes8[:, :, :6].reshape(64, 6)
    ids = jnp.arange(experts, dtype=jnp.int32)
    chosen = jnp.any(routes[:, :, None] == ids, axis=1)
    token = jnp.arange(64, dtype=jnp.int32)
    before = (token[:, None] // 8 == token[None, :] // 8) & (token[None, :] < token[:, None])
    rank = jnp.dot(before.astype(BF16), chosen.astype(BF16), preferred_element_type=F32)
    rank = jnp.where(chosen, rank, -1.0)
    here = lax.dynamic_slice_in_dim(rank, zl * 16, 16, 1)
    pick = (
        (here[:, :, None, None] == jnp.arange(2, dtype=F32))
        & (token[:, None, None, None] // 8 == jnp.arange(8)[None, None, :, None])
    ).astype(BF16)
    pick = pick.reshape(64, 256)
    return pick.T, pick, chosen.astype(F32)


def on_device(
    query_nope,
    query_rope,
    absorb_weight,
    value_weight,
    output_weight,
    cache_latent,
    cache_rope,
    node_length,
    new_latent,
    new_rope,
    parent_node,
    leaf_node,
    residual,
    norm_gain,
    router_weight,
    routes,
    expert_gate,
    expert_up,
    expert_down,
    shared_gate,
    shared_up,
    shared_down,
):
    q2 = jnp.concatenate(
        [query_nope.reshape(REQ, QT * 128), query_rope.reshape(REQ, QT * 64)], axis=1
    )
    routes_pad = jnp.pad(routes, ((0, 0), (0, 128 - routes.shape[1])), constant_values=-1)
    q_all, routes8, resid2 = gather(q2, routes_pad, residual)
    absorb, value = absorb_weight[0], value_weight[0]
    msg = attend(
        node_length,
        q_all.reshape(16 * REQ, -1),
        absorb,
        value,
        cache_latent,
        cache_rope,
        leaf_node,
        parent_node,
    )
    place, pick, chosen = slot_tables(routes8, router_weight.shape[1])
    hidden, normed = merge(
        msg.reshape(16, REQ, MSG),
        q2,
        absorb,
        value,
        new_latent,
        new_rope,
        output_weight,
        resid2,
        norm_gain[None, :],
    )
    weights = [
        expert_gate[0],
        expert_up[0],
        expert_down[0],
        shared_gate,
        shared_up,
        shared_down,
    ]
    return experts_layer(
        normed.reshape(64, 2048), hidden, place, pick, chosen, router_weight, weights
    )


def solution(mesh):
    in_specs = (
        P("group", "expert", None),
        P("group", "expert", None),
        P("expert", None, None),
        P("expert", None, None),
        P("expert", None),
        P("group", None, None),
        P("group", None, None),
        P("group"),
        P("group", None),
        P("group", None),
        P(),
        P(),
        P(("group", "expert"), None),
        P(),
        P(),
        P(("group", "expert"), None),
        P(("group", "expert"), None, None),
        P(("group", "expert"), None, None),
        P(("group", "expert"), None, None),
        P(None, "group"),
        P(None, "group"),
        P("group", None),
    )
    out_specs = P(("group", "expert"), None)
    return jax.shard_map(
        on_device, mesh=mesh, in_specs=in_specs, out_specs=out_specs, check_vma=False
    )
```

time: 785 us -> 158 us (0.20); the launches traced: 776 us -> 157 us
  waiting for transfers between devices: 336 us -> 0 us
  blocking collectives: 333 us -> 0 us
  Pallas kernels: 0 us -> 136 us
  matrix products: 46.6 us -> 0.23 us
  other arithmetic: 20.4 us -> 0.85 us
  between operations: 14 us -> 0.25 us
    reduce_scatter x3 -> x0, waiting for transfers between devices: 235 us -> none  [the longest x1 92.1 us: on_device(): lax.psum_scatter(dev_sum * factor[..., None], 'group', scatter_dimension=...]
    all_to_all x3 -> x0, blocking collectives: 163 us -> none  [the longest x1 58.4 us: on_device(): lax.all_to_all(lax.all_to_all(packed, 'group', split_axis=0, concat_axis=...]
    pallas_call x0 -> x4, Pallas kernels: none -> 136 us  [the longest x1 59.9 us: experts_layer(): pl.pallas_call(expert_kernel, name='experts', out_shape=jax.ShapeDtypeStr...]
    all_gather x2 -> x0, blocking collectives: 127 us -> none  [the longest x1 81.2 us: on_device(): column_normed = lax.all_gather(normed, 'group', axis=0, tiled=True)]
    unnamed x6 -> x0, waiting for transfers between devices: 73.3 us -> none
    dot_general x18 -> x1, matrix products: 46.6 us -> 0.23 us  [slot_tables(): jnp.dot(before.astype(BF16), chosen.astype(BF16), preferred_element_type=...]
    pmax x1 -> x0, blocking collectives: 43.3 us -> none  [on_device(): global_peak = lax.pmax(dev_peak, 'group')]
    all_gather x1 -> x0, waiting for transfers between devices: 27.4 us -> none  [on_device(): lax.all_gather(own_latent, 'group', axis=0, tiled=True)]
  transfers between devices with their start and end apart: 6 -> 0, of which waited for: 5 -> 0; matrix products, arithmetic and copies ran while one was open for 4% -> 0% of each run, Pallas kernels for 0% -> 0%
where the time goes in v1:
time: 158 us; the launch traced here: 157 us
  Pallas kernels  136 us (86%)
  local copies, waits for them, and re-layouts  20.2 us (13%)
    pallas_call x1, Pallas kernels, experts_layer(): pl.pallas_call(expert_kernel, name='experts', out_shape=jax.ShapeDtypeStr...  59.9 us
    pallas_call x1, Pallas kernels, merge(): pl.pallas_call(merge_kernel, name='merge_project_norm', out_shape=(jax.Sh...  36.6 us
    pallas_call x1, Pallas kernels, gather(): pl.pallas_call(gather_kernel, name='gather_queries', out_shape=(jax.Shape...  30.6 us
    unnamed x45, local copies, waits for them, and re-layouts  15.3 us
    pallas_call x1, Pallas kernels, attend(): pl.pallas_call(attn_kernel, name='attend_nodes', out_shape=jax.ShapeDtype...  8.48 us

profile of v1, /device:TPU:24, one launch (start us, length us, event | category | flops | bytes accessed | tf_op | source)
XLA Modules:
  0.0 157.1 jit_solution(10564494204545171669)
XLA Ops:
  0.1 0.9 pad.4.routes_ref
  0.9 0.7 broadcast_in_dim.32.gain_ref
  1.6 0.7 copy.50.parent_col_ref
  2.4 0.8 reshape.166
  3.2 0.8 copy.47
  4.1 0.8 copy.51.newrope_ref
  4.9 0.8 copy.49.leaf_col_ref
  5.8 1.2 copy.48.rope_ref
  7.0 2.0 %copy.57.router_ref = bf16[2048,64]{1,0:T(8,128)(2,1)} copy(bf16[2048,64]{0,1:T(8,128)(2,1)} %param.36) | data formatting | bytes 524288 | tf_op args[14]
  9.0 30.6 %gather_queries.1 = (bf16[16,16,1536]{2,1,0:T(8,128)(2,1)S(1)}, s32[8,8,128]{2,1,0:T(8,128)S(1)}, bf16[2,8,2048]{2,1,0:T(8,128)(2,1)S(1)}) custom-call(bf16[16,1536]{1,0:T(8,128)(2,1)S(1)} %constant_dynamic-update-slice_fusion.q_ref, s32[8,128]{1,0:T(8,128)S(1)} %pad.4.routes_ref, bf16[8,2048]{1,0:T(8,128)(2,1)S(1)} %copy-done.8), custom_call_target="tpu_custom_call" | custom-call | tf_op jit(solution)/shard_map/gather_queries/pallas_call | solution.py:110
  39.6 0.9 copy-done.2
  40.5 0.9 copy-done.3
  41.4 8.5 %attend_nodes.1 = bf16[256,1152]{1,0:T(8,128)(2,1)S(1)} custom-call(s32[2]{0:T(128)S(1)} %copy-done.11, bf16[256,1536]{1,0:T(8,128)(2,1)S(1)} %bitcast.23, bf16[128,512]{1,0:T(8,128)(2,1)S(1)} %bitcast.24, bf16[512,128]{1,0:T(8,128)(2,1)S(1)} %bitcast.26, bf16[2,1024,512]{2,1,0:T(8,128)(2,1)S(1)} %copy-done, bf16[2,1024,64]{2,1,0:T(8,128)(2,1)S(1)} %copy.48.rope_ref, ...), custom_call_target="tpu_custom_call" | custom-call | tf_op jit(solution)/shard_map/attend_nodes/pallas_call | solution.py:272
  50.0 36.6 %merge_project_norm.1 = (f32[2,8,2048]{2,1,0:T(8,128)S(1)}, bf16[4,16,2048]{2,1,0:T(8,128)(2,1)S(1)}) custom-call(bf16[16,16,1152]{2,1,0:T(8,128)(2,1)S(1)} %bitcast.22, bf16[16,1536]{1,0:T(8,128)(2,1)S(1)} %constant_dynamic-update-slice_fusion.q_ref, bf16[128,512]{1,0:T(8,128)(2,1)S(1)} %bitcast.25, bf16[512,128]{1,0:T(8,128)(2,1)S(1)} %bitcast.27, ...), custom_call_target="tpu_custom_call" | custom-call | tf_op jit(solution)/shard_map/merge_project_norm/pallas_call | solution.py:427
  86.6 0.7 copy-done.5
  87.3 0.7 copy-done.6
  88.6 0.6 convert_element_type.14.chosen_ref
  89.3 0.7 copy.56.pick_ref
  90.0 1.3 copy.58.sgate_hbm
  91.4 1.3 copy.59.sup_hbm
  92.6 1.6 %copy.54 = bf16[1,2048,352]{2,1,0:T(8,128)(2,1)} copy(bf16[1,2048,352]{1,2,0:T(8,128)(2,1)S(1)} %copy-done.12) | data formatting | bytes 2883584 | tf_op args[16]
  94.3 1.6 copy.55
  95.8 59.9 %experts.1 = bf16[8,2048]{1,0:T(8,128)(2,1)} custom-call(bf16[64,2048]{1,0:T(8,128)(2,1)} %bitcast.28, f32[2,8,2048]{2,1,0:T(8,128)} %copy-done.6, bf16[256,64]{1,0:T(8,128)(2,1)} %bitcast.37, bf16[64,256]{1,0:T(8,128)(2,1)} %copy.56.pick_ref, f32[64,64]{1,0:T(8,128)} %convert_element_type.14.chosen_ref, bf16[2048,64]{1,0:T(8,128)(2,1)} %copy.57.router_ref, ...), custom_call_target="tpu_custom_call" | custom-call | tf_op jit(solution)/shard_map/experts/pallas_call | solution.py:675
  155.8 1.4 copy.63
  (44 shorter events, 0.9 us)
Async XLA Ops:
  0.0 39.6 %copy-start.9 = (s32[256]{0:T(256)S(1)}, s32[256]{0:T(256)}, u32[]{:S(2)}) copy-start(s32[256]{0:T(256)} %param.33) | copy-start | bytes 3076
  0.0 39.6 %copy-start.10 = (s32[32]{0:T(128)S(1)}, s32[32]{0:T(128)}, u32[]{:S(2)}) copy-start(s32[32]{0:T(128)} %param.32) | copy-start | bytes 388
  0.0 9.0 %copy-start.8 = (bf16[8,2048]{1,0:T(8,128)(2,1)S(1)}, bf16[8,2048]{1,0:T(8,128)(2,1)}, u32[]{:S(2)}) copy-start(bf16[8,2048]{1,0:T(8,128)(2,1)} %resid_ref.1) | copy-start | bytes 98308
  0.0 39.6 %copy-start.11 = (s32[2]{0:T(128)S(1)}, s32[2]{0:T(128)}, u32[]{:S(2)}) copy-start(s32[2]{0:T(128)} %len_ref.1) | copy-start | bytes 28
  0.0 39.6 %copy-start = (bf16[2,1024,512]{2,1,0:T(8,128)(2,1)S(1)}, bf16[2,1024,512]{2,1,0:T(8,128)(2,1)}, u32[]{:S(2)}) copy-start(bf16[2,1024,512]{2,1,0:T(8,128)(2,1)} %lat_ref.1) | copy-start | bytes 6291460
  39.6 0.9 copy-start.2
  40.5 0.9 copy-start.3
  41.4 8.5 %copy-start.1 = (bf16[128,2048]{1,0:T(8,128)(2,1)S(1)}, bf16[128,2048]{1,0:T(8,128)(2,1)}, u32[]{:S(2)}) copy-start(bf16[128,2048]{1,0:T(8,128)(2,1)} %outw_ref.1) | copy-start | bytes 1572868
  41.4 8.5 %copy-start.4 = (bf16[1,512,128]{2,1,0:T(8,128)(2,1)S(1)}, bf16[1,512,128]{2,1,0:T(8,128)(2,1)}, u32[]{:S(2)}) copy-start(bf16[1,512,128]{2,1,0:T(8,128)(2,1)} %param.25) | copy-start | bytes 393220
  41.4 8.5 %copy-start.7 = (bf16[128,512]{1,0:T(8,128)(2,1)S(1)}, bf16[128,512]{1,0:T(8,128)(2,1)}, u32[]{:S(2)}) copy-start(bf16[128,512]{1,0:T(8,128)(2,1)} %newlat_ref.1) | copy-start | bytes 393220
  49.9 40.1 %copy-start.14 = (bf16[2048,176]{0,1:T(8,128)(2,1)S(1)}, bf16[2048,176]{0,1:T(8,128)(2,1)}, u32[]{:S(2)}) copy-start(bf16[2048,176]{0,1:T(8,128)(2,1)} %param.41) | copy-start | bytes 2162692
  86.6 0.7 copy-start.5
  87.3 0.7 copy-start.6
  88.0 3.4 %copy-start.15 = (bf16[2048,176]{0,1:T(8,128)(2,1)S(1)}, bf16[2048,176]{0,1:T(8,128)(2,1)}, u32[]{:S(2)}) copy-start(bf16[2048,176]{0,1:T(8,128)(2,1)} %param.42) | copy-start | bytes 2162692
  89.3 3.3 %copy-start.16 = (bf16[64,16,8,2]{0,3,2,1:T(2,128)(2,1)}, bf16[64,16,8,2]{0,3,2,1:T(2,128)(2,1)S(1)}, u32[]{:S(2)}) copy-start(bf16[64,16,8,2]{0,3,2,1:T(2,128)(2,1)S(1)} %and_convert_fusion) | copy-start | bytes 98308
  90.0 2.6 %copy-start.12 = (bf16[1,2048,352]{1,2,0:T(8,128)(2,1)S(1)}, bf16[1,2048,352]{1,2,0:T(8,128)(2,1)}, u32[]{:S(2)}) copy-start(bf16[1,2048,352]{1,2,0:T(8,128)(2,1)} %param.38) | copy-start | bytes 4325380
  92.6 1.6 %copy-start.13 = (bf16[1,2048,352]{1,2,0:T(8,128)(2,1)S(1)}, bf16[1,2048,352]{1,2,0:T(8,128)(2,1)}, u32[]{:S(2)}) copy-start(bf16[1,2048,352]{1,2,0:T(8,128)(2,1)} %param.39) | copy-start | bytes 4325380

commit v2 on v1

v2 whole, which is shorter than its diff:
```python
import jax
import jax.numpy as jnp
from jax import lax
from jax.experimental import pallas as pl
from jax.experimental.pallas import tpu as pltpu
from jax.sharding import PartitionSpec as P

ROUTE_SCALE = 2.446
NEGATIVE = -1e30
EPSILON = 1e-06
MESH = pl.DeviceIdType.MESH
F32 = jnp.float32
BF16 = jnp.bfloat16
VMEM = pltpu.VMEM
DMA = pltpu.SemaphoreType.DMA

REQ = 16
QT = 8
MSG = 1024 + 128


def vmem_spec():
    return pl.BlockSpec(memory_space=pltpu.VMEM)


def any_spec():
    return pl.BlockSpec(memory_space=pl.ANY)


def coords():
    g = lax.axis_index("group")
    e = lax.axis_index("expert")
    zl, x = g // 4, g % 4
    y, zh, c = e // 4, (e % 4) // 2, e % 2
    return g, e, x, y, zl, zh, c


def dev(x, y, zl, zh, c):
    return (zl * 4 + x, y * 4 + zh * 2 + c)


def remote(src, dst, send, recv, device):
    return pltpu.make_async_remote_copy(
        src_ref=src,
        dst_ref=dst,
        send_sem=send,
        recv_sem=recv,
        device_id=device,
        device_id_type=MESH,
    )


def greet(barrier, device):
    pl.semaphore_signal(barrier, inc=1, device_id=device, device_id_type=MESH)


def dot(a, b):
    return jnp.dot(a, b, preferred_element_type=F32)


def eye_column(row):
    n = row.shape[1]
    same = lax.broadcasted_iota(jnp.int32, (n, n), 0) == lax.broadcasted_iota(jnp.int32, (n, n), 1)
    return jnp.sum(jnp.where(same, row, 0), axis=1, keepdims=True)


def flag(condition):
    return jnp.where(condition, 1.0, 0.0).astype(BF16)


def dot_nt(a, b):
    return lax.dot_general(a, b, (((1,), (1,)), ((), ())), preferred_element_type=F32)


def gather_kernel(
    nope_ref, rope_ref, routes_ref, resid_ref, qall, routes8, resid2, mine, zq, zqr, xq, xqr, rs, rr, zs, zr
):
    g, e, x, y, zl, zh, c = coords()
    barrier = pltpu.get_barrier_semaphore()
    partner = dev(x, y, zl, 1 - zh, c)
    me = zl * 2 + zh
    for i in range(1, 4):
        greet(barrier, dev(lax.rem(x + i, 4), y, zl, zh, c))
        greet(barrier, dev(x, y, lax.rem(zl + i, 4), zh, c))
    for k in (1, 3, 5, 7):
        s = lax.rem(me + k, 8)
        greet(barrier, dev(x, y, s // 2, s % 2, c))

    rows = REQ * QT
    di = lax.broadcasted_iota(jnp.int32, (rows, rows), 0)
    si = lax.broadcasted_iota(jnp.int32, (rows, rows), 1)
    perm = flag(si == (di % REQ) * QT + di // REQ)
    nope = dot(perm, nope_ref[...]).astype(BF16)
    rope = dot_nt(perm, rope_ref[...]).astype(BF16)
    qall[g] = jnp.concatenate(
        [nope[j * REQ : (j + 1) * REQ] for j in range(QT)]
        + [rope[j * REQ : (j + 1) * REQ] for j in range(QT)],
        axis=1,
    )
    mine[...] = jnp.zeros_like(mine)
    mine[:, 0 : routes_ref.shape[1]] = routes_ref[...]
    routes8[me] = mine[...]
    resid2[zh] = resid_ref[...]
    pl.semaphore_wait(barrier, 10)

    own = qall.at[g]
    for i in (1, 3, 2):
        remote(own, own, zq.at[i], zqr.at[i], dev(x, y, lax.rem(zl + i, 4), zh, c)).start()
    for k in (1, 3, 2):
        remote(own, own, xq.at[0, k], xqr.at[0, k], dev(lax.rem(x + k, 4), y, zl, zh, c)).start()
    remote(resid_ref, resid2.at[zh], zs, zr, partner).start()
    for k in range(1, 8):
        s = lax.rem(me + k, 8)
        remote(mine, routes8.at[me], rs.at[k], rr.at[k], dev(x, y, s // 2, s % 2, c)).start()
    for i in (1, 3, 2):
        block = qall.at[lax.rem(zl - i + 4, 4) * 4 + x]
        remote(own, block, zq.at[i], zqr.at[i], partner).wait()
        for k in (1, 3, 2):
            remote(
                block, block, xq.at[i, k], xqr.at[i, k], dev(lax.rem(x + k, 4), y, zl, zh, c)
            ).start()
    remote(resid_ref, resid2.at[1 - zh], zs, zr, partner).wait()
    for k in range(1, 8):
        s = lax.rem(me - k + 8, 8)
        remote(mine, routes8.at[s], rs.at[k], rr.at[k], partner).wait()
    for i in range(4):
        for k in (1, 3, 2):
            block = qall.at[lax.rem(zl - i + 4, 4) * 4 + lax.rem(x - k + 4, 4)]
            remote(own, block, xq.at[i, k], xqr.at[i, k], partner).wait()


def gather(nope, rope_t, routes, residual):
    return pl.pallas_call(
        gather_kernel,
        name="gather_queries",
        out_shape=(
            jax.ShapeDtypeStruct((16, REQ, QT * 192), BF16),
            jax.ShapeDtypeStruct((8, 8, 128), jnp.int32),
            jax.ShapeDtypeStruct((2,) + residual.shape, BF16),
        ),
        in_specs=[vmem_spec()] * 4,
        out_specs=(vmem_spec(),) * 3,
        scratch_shapes=[
            VMEM((8, 128), jnp.int32),
            DMA((4,)),
            DMA((4,)),
            DMA((4, 4)),
            DMA((4, 4)),
            DMA((8,)),
            DMA((8,)),
            DMA,
            DMA,
        ],
        compiler_params=pltpu.CompilerParams(
            collective_id=0, has_side_effects=True, vmem_limit_bytes=24 << 20
        ),
    )(nope, rope_t, routes, residual)


TILE = 32
KEYS = 256


def split3(v):
    hi = v.astype(BF16)
    rest = v - hi.astype(F32)
    mid = rest.astype(BF16)
    low = (rest - mid.astype(F32)).astype(BF16)
    return hi.astype(F32), mid.astype(F32), low.astype(F32)


def join3(part):
    return part[:, 0:8] + part[:, 8:16] + part[:, 16:24]


def on_path(leaf_row, parent_col, node):
    nodes = parent_col.shape[0]
    ids = lax.broadcasted_iota(jnp.int32, (nodes, leaf_row.shape[1]), 0)
    mid = jnp.sum(jnp.where(leaf_row == ids, parent_col, 0), axis=0, keepdims=True)
    top = jnp.sum(jnp.where(mid == ids, parent_col, 0), axis=0, keepdims=True)
    return (leaf_row == node) | (mid == node) | (top == node)


def attn_kernel(
    len_ref,
    q_ref,
    absorb_ref,
    value_ref,
    lat_ref,
    rope_ref,
    leaf_ref,
    parent_ref,
    out_ref,
    acc,
):
    g = lax.axis_index("group")
    requests = q_ref.shape[0]
    slots, most = lat_ref.shape[0], lat_ref.shape[1]
    scaling = float(128 + 64) ** (-0.5)
    earlier = flag(
        lax.broadcasted_iota(jnp.int32, (requests, requests), 0)
        < lax.broadcasted_iota(jnp.int32, (requests, requests), 1)
    )
    acc[...] = jnp.zeros_like(acc)
    lane = lax.broadcasted_iota(jnp.int32, (TILE, 128), 1)
    parent_col = eye_column(parent_ref[...])
    on_cols = []
    for slot in range(slots):
        on_row = on_path(leaf_ref[...], parent_col, g * slots + slot)
        row_f = jnp.where(on_row, 1.0, 0.0)
        count = jnp.sum(row_f).astype(jnp.int32)
        rank_row = dot(jnp.broadcast_to(row_f, (8, requests)).astype(BF16), earlier)[0:1]
        rank_row = jnp.where(on_row, rank_row, -1.0)
        rank_col = eye_column(rank_row)
        on_cols.append(rank_col >= 0.0)
        rank_row = rank_row.astype(jnp.int32)
        rank_col = rank_col.astype(jnp.int32)
        length = len_ref[slot]

        def tile(keys, step, carry):
            base = step * TILE
            pick = flag(rank_row == lax.broadcasted_iota(jnp.int32, (TILE, requests), 0) + base)
            place = flag(rank_col == lax.broadcasted_iota(jnp.int32, (requests, TILE), 1) + base)
            qt = dot(pick, q_ref[...]).astype(BF16)
            nope = jnp.concatenate([qt[:, j * 128 : j * 128 + 128] for j in range(QT)], axis=0)
            rot = jnp.concatenate(
                [qt[:, 1024 + j * 64 : 1024 + j * 64 + 64] for j in range(QT)], axis=0
            )
            lat = dot(nope, absorb_ref[...]).astype(BF16)
            scores = dot_nt(lat, lat_ref[slot, :keys]) + dot(rot, rope_ref[slot, :, :keys])
            positions = lax.broadcasted_iota(jnp.int32, (1, keys), 1)
            scores = jnp.where(positions < length, scores * scaling, NEGATIVE)
            top = jnp.max(scores, axis=1, keepdims=True)
            weights = jnp.exp(scores - top).astype(BF16)
            total = jnp.sum(weights.astype(F32), axis=1, keepdims=True)
            summed = dot(weights, lat_ref[slot, :keys])
            attended = (summed / total).astype(BF16)
            valued = dot(attended, value_ref[...]).astype(BF16)
            parts = split3(top + jnp.log(total))
            tail = jnp.zeros((TILE, 128), F32)
            for j in range(QT):
                for k in range(3):
                    piece = parts[k][j * TILE : (j + 1) * TILE]
                    tail = jnp.where(lane == k * 8 + j, piece, tail)
            block = jnp.concatenate(
                [valued[j * TILE : (j + 1) * TILE] for j in range(QT)] + [tail.astype(BF16)],
                axis=1,
            )
            acc[slot] += dot(place, block)
            return carry

        tiles = (count + TILE - 1) // TILE
        for keys in range(KEYS, most + 1, KEYS):

            @pl.when((length > keys - KEYS) & (length <= keys))
            def _():
                lax.fori_loop(0, tiles, lambda step, carry: tile(keys, step, carry), 0)

    logs = [jnp.where(on_cols[s], join3(acc[s, :, 1024:]), NEGATIVE) for s in range(slots)]
    top = logs[0]
    for s in range(1, slots):
        top = jnp.maximum(top, logs[s])
    shares = [jnp.exp(v - top) for v in logs]
    total = shares[0]
    for s in range(1, slots):
        total = total + shares[s]
    log_sum = top + jnp.log(total)
    for j in range(QT):
        out = 0.0
        for s in range(slots):
            out = out + (shares[s] / total)[:, j : j + 1] * acc[s, :, j * 128 : j * 128 + 128]
        out_ref[:, j * 128 : j * 128 + 128] = out.astype(BF16)
    parts = split3(log_sum)
    lane = lax.broadcasted_iota(jnp.int32, (requests, 128), 1)
    tail = jnp.zeros((requests, 128), F32)
    for j in range(QT):
        for k in range(3):
            tail = jnp.where(lane == k * 8 + j, parts[k][:, j : j + 1], tail)
    out_ref[:, 1024:] = tail.astype(BF16)


def attend(node_length, q_all, absorb, value, cache_latent, rope_t, leaf, parent):
    requests = q_all.shape[0]
    slots = cache_latent.shape[0]
    return pl.pallas_call(
        attn_kernel,
        name="attend_nodes",
        out_shape=jax.ShapeDtypeStruct((requests, MSG), BF16),
        in_specs=[pl.BlockSpec(memory_space=pltpu.SMEM)] + [vmem_spec()] * 7,
        out_specs=vmem_spec(),
        scratch_shapes=[VMEM((slots, requests, MSG), F32)],
        compiler_params=pltpu.CompilerParams(vmem_limit_bytes=32 << 20),
    )(node_length, q_all, absorb, value, cache_latent, rope_t, leaf[None, :], parent[None, :])


GAP = 384
SGAP = 256


def layer_kernel(
    msg_ref,
    q_ref,
    routes_ref,
    resid_ref,
    absorb_ref,
    value_ref,
    newlat_ref,
    newrope_ref,
    outw_ref,
    gain_ref,
    router_ref,
    gate_hbm,
    up_hbm,
    down_hbm,
    sgate_hbm,
    sup_hbm,
    sdown_hbm,
    out_ref,
    gate_up,
    down_w,
    sgate_up,
    sdown_w,
    got,
    valued_s,
    csend,
    crecv,
    acc,
    ysend,
    yrecv,
    zsend,
    zrecv,
    hidden_s,
    normed,
    packed,
    arrived,
    own_out,
    cross_send,
    cross_recv,
    ret_send,
    ret_recv,
    share_in,
    share_send,
    share_recv,
    part,
    lsend,
    lrecv,
    hsend,
    hrecv,
    wsem,
    ms,
    mr,
    cs,
    cr,
    ys,
    yr,
    zs,
    zr,
    ns,
    nr,
    ds,
    dr,
    fs,
    fr,
    os_,
    or_,
    rs,
    rr,
    xs,
    xr,
    bs,
    br,
    ls,
    lr,
    hs,
    hr,
):
    g, e, x, y, zl, zh, c = coords()
    mine = x * 4 + y
    ff = gate_hbm.shape[0]
    sff = sgate_hbm.shape[0]
    barrier = pltpu.get_barrier_semaphore()

    def plane(p):
        return dev(p // 4, p % 4, zl, zh, c)

    def hello(i, carry):
        greet(barrier, (lax.rem(g + i, 16), e))
        return carry

    lax.fori_loop(1, 16, hello, 0)
    other = dev(x, y, zl, zh, 1 - c)
    partner = dev(x, y, zl, 1 - zh, c)
    greet(barrier, other)
    greet(barrier, partner)
    for i in range(4):
        for k in range(1, 4):
            greet(barrier, dev(lax.rem(x + i, 4), lax.rem(y + k, 4), zl, zh, c))
    loads = [
        pltpu.make_async_copy(src, dst, wsem.at[i])
        for i, (src, dst) in enumerate(
            [
                (gate_hbm, gate_up.at[pl.ds(0, ff)]),
                (up_hbm, gate_up.at[pl.ds(GAP, ff)]),
                (down_hbm, down_w),
                (sgate_hbm, sgate_up.at[pl.ds(0, sff)]),
                (sup_hbm, sgate_up.at[pl.ds(SGAP, sff)]),
                (sdown_hbm, sdown_w),
            ]
        )
    ]
    for load in loads:
        load.start()
    gate_up[ff:GAP] = jnp.zeros((GAP - ff, gate_up.shape[1]), BF16)
    sgate_up[sff:SGAP] = jnp.zeros((SGAP - sff, sgate_up.shape[1]), BF16)

    scaling = float(128 + 64) ** (-0.5)
    q = q_ref[g]
    nope = jnp.concatenate([q[:, j * 128 : j * 128 + 128] for j in range(QT)], axis=0)
    rot = jnp.concatenate([q[:, 1024 + j * 64 : 1024 + j * 64 + 64] for j in range(QT)], axis=0)
    lat = dot(nope, absorb_ref[...]).astype(BF16)
    scores = dot_nt(lat, newlat_ref[...]) + dot(rot, newrope_ref[...])
    rows = REQ * QT
    qi = lax.broadcasted_iota(jnp.int32, (rows, rows), 0)
    ki = lax.broadcasted_iota(jnp.int32, (rows, rows), 1)
    usable = ((qi % REQ) == (ki // QT)) & ((ki % QT) <= (qi // REQ))
    scores = jnp.where(usable, scores * scaling, NEGATIVE)
    top = jnp.max(scores, axis=1, keepdims=True)
    weights = jnp.where(usable, jnp.exp(scores - top), 0.0).astype(BF16)
    total = jnp.sum(weights.astype(F32), axis=1, keepdims=True)
    summed = dot(weights, newlat_ref[...]) / total
    new_valued = dot(summed.astype(BF16), value_ref[...])
    new_log = top + jnp.log(total)

    pl.semaphore_wait(barrier, 29)

    def send(i, carry):
        peer = lax.rem(g + i, 16)
        remote(msg_ref.at[peer], got.at[g], ms.at[i], mr.at[i], (peer, e)).start()
        return carry

    lax.fori_loop(1, 16, send, 0)
    got[g] = msg_ref[g]

    experts = router_ref.shape[0]
    pairs = (zl // 2, 1 - zl // 2)
    picks, masks = [], []
    for q_ in range(2):
        routes = routes_ref[pl.ds(pairs[q_] * 4, 4)].reshape(32, 128)
        ids = lax.broadcasted_iota(jnp.int32, (32, experts), 1)
        chosen = jnp.zeros((32, experts), F32)
        for k in range(6):
            chosen = jnp.where(routes[:, k : k + 1] == ids, 1.0, chosen)
        ti = lax.broadcasted_iota(jnp.int32, (32, 32), 0)
        tj = lax.broadcasted_iota(jnp.int32, (32, 32), 1)
        before = flag((ti // 8 == tj // 8) & (tj < ti))
        rank = jnp.where(chosen > 0.0, dot(before, chosen.astype(BF16)), -1.0)
        col = lax.broadcasted_iota(jnp.int32, (experts, 128), 1)
        spread = flag(lax.broadcasted_iota(jnp.int32, (experts, 128), 0) == zl * 16 + col // 8)
        spread_rank = dot(rank.astype(BF16), spread)
        ct = lax.broadcasted_iota(jnp.int32, (32, 128), 1)
        rt = lax.broadcasted_iota(jnp.int32, (32, 128), 0)
        pick = jnp.where(
            (spread_rank == (ct % 2).astype(F32)) & (rt // 8 == (ct // 2) % 4), 1.0, 0.0
        )
        picks.append(pick)
        masks.append(chosen)

    def wait(i, carry):
        src = lax.rem(g - i + 16, 16)
        remote(msg_ref.at[src], got.at[src], ms.at[i], mr.at[i], other).wait()
        return carry

    lax.fori_loop(1, 16, wait, 0)

    logs = join3(got[:, :, 1024:].astype(F32).reshape(16 * REQ, 128)).reshape(16, REQ, 8)
    pieces = []
    for j in range(QT):
        log_j = logs[:, :, j : j + 1]
        new_j = new_log[j * REQ : (j + 1) * REQ]
        peak = jnp.maximum(jnp.max(log_j, axis=0), new_j)
        share = jnp.exp(log_j - peak[None])
        new_share = jnp.exp(new_j - peak)
        whole = jnp.sum(share, axis=0) + new_share
        value = jnp.sum(share * got[:, :, j * 128 : j * 128 + 128].astype(F32), axis=0)
        value = value + new_share * new_valued[j * REQ : (j + 1) * REQ]
        pieces.append((value / whole).astype(BF16))
    valued = jnp.concatenate(pieces, axis=0)
    di = lax.broadcasted_iota(jnp.int32, (rows, rows), 0)
    si = lax.broadcasted_iota(jnp.int32, (rows, rows), 1)
    req = ((di % 64) // 16) * 4 + ((di % 16) // 8) * 2 + di // 64
    perm = flag(si == (di % 8) * REQ + req)
    valued_s[...] = dot(perm, valued).astype(BF16).reshape(2, 64, 128)

    csend[...] = dot(valued_s[1 - c], outw_ref[...]).astype(BF16)
    remote(csend, crecv, cs, cr, other).start()
    own = dot(valued_s[c], outw_ref[...])
    remote(csend, crecv, cs, cr, other).wait()
    acc[...] = (own + crecv[...].astype(F32)).reshape(4, 16, 2048)
    ysend[...] = acc[...].astype(BF16)
    for i in (2, 1, 3):
        peer = lax.rem(y + i, 4)
        remote(ysend.at[peer], yrecv.at[i], ys.at[i], yr.at[i], dev(x, peer, zl, zh, c)).start()
    total_row = acc[y]
    for i in (1, 3, 2):
        remote(ysend.at[0], yrecv.at[i], ys.at[i], yr.at[i], other).wait()
        total_row = total_row + yrecv[i].astype(F32)
    zsend[...] = total_row.astype(BF16)
    remote(zsend, zrecv, zs, zr, partner).start()
    total_row = total_row + resid_ref[...].reshape(16, 2048).astype(F32)
    remote(zsend, zrecv, zs, zr, partner).wait()
    hidden = total_row + zrecv[...].astype(F32)
    hidden_s[...] = hidden.reshape(2, 8, 2048)
    square = jnp.mean(hidden * hidden, axis=1, keepdims=True)
    normed[zl] = (hidden * lax.rsqrt(square + EPSILON) * gain_ref[...].astype(F32)).astype(BF16)
    near = zl + 1 - 2 * (zl % 2)
    far = (2 - 2 * (zl // 2), 3 - 2 * (zl // 2))
    row = normed.at[zl]
    remote(row, row, ns.at[0], nr.at[0], dev(x, y, near, zh, c)).start()
    for i in range(2):
        remote(row, row, ns.at[1 + i], nr.at[1 + zl % 2], dev(x, y, far[i], zh, c)).start()

    def pack(chunk):
        tokens = normed[pl.ds(pairs[chunk] * 2, 2)].reshape(32, 2048)
        packed[chunk] = (
            lax.dot_general(
                picks[chunk].astype(BF16),
                tokens,
                (((0,), (0,)), ((), ())),
                preferred_element_type=F32,
            )
            .astype(BF16)
            .reshape(16, 8, 2048)
        )

        def send(i, carry):
            p = lax.rem(mine + i, 16)
            remote(
                packed.at[chunk, p],
                arrived.at[chunk, c, mine],
                ds.at[chunk, i],
                dr.at[chunk, i],
                plane(p),
            ).start()
            return carry

        lax.fori_loop(1, 16, send, 0)
        arrived[chunk, c, mine] = packed[chunk, mine]
        here = arrived.at[chunk, c, mine]
        remote(here, here, fs.at[chunk, 0], fr.at[chunk, 0], other).start()
        logits = dot_nt(tokens, router_ref[...])
        sigma = jax.nn.sigmoid(logits) * masks[chunk]
        route_w = ROUTE_SCALE * sigma / jnp.sum(sigma, axis=1, keepdims=True)
        col = lax.broadcasted_iota(jnp.int32, (experts, 128), 1)
        spread = flag(lax.broadcasted_iota(jnp.int32, (experts, 128), 0) == zl * 16 + col // 8)
        w_hi, w_mid, w_low = split3(route_w)
        return (
            dot(w_hi.astype(BF16), spread)
            + dot(w_mid.astype(BF16), spread)
            + dot(w_low.astype(BF16), spread)
        ) * picks[chunk]

    remote(row, normed.at[near], ns.at[0], nr.at[0], other).wait()
    combine0 = pack(0)
    for i in range(2):
        remote(row, normed.at[far[i]], ns.at[1 + i], nr.at[1 + i], other).wait()
    combine1 = pack(1)
    combines = (combine0, combine1)
    for z in range(4):
        both = normed[z].reshape(2, 8, 2048)
        share_in[x, z] = jnp.where(zh == 0, both[0], both[1])
    for i in (2, 1, 3):
        peer = lax.rem(x + i, 4)
        remote(share_in.at[x], share_in.at[x], xs.at[i], xr.at[i], dev(peer, y, zl, zh, c)).start()

    def forward(chunk):
        def step(i, carry):
            src = lax.rem(mine - i + 16, 16)
            block = arrived.at[chunk, c, src]
            remote(packed.at[chunk, src], block, ds.at[chunk, i], dr.at[chunk, i], other).wait()
            remote(block, block, fs.at[chunk, i], fr.at[chunk, i], other).start()
            return carry

        lax.fori_loop(1, 16, step, 0)

    def crossed(chunk):
        def step(i, carry):
            src = lax.rem(mine - i + 16, 16)
            block = arrived.at[chunk, c, src]
            remote(
                block, arrived.at[chunk, 1 - c, src], fs.at[chunk, i], fr.at[chunk, i], other
            ).wait()
            return carry

        lax.fori_loop(0, 16, step, 0)

    def ffn(rows_in, both_w, gap, units, down):
        val = dot_nt(rows_in, both_w[...])
        hidden = (jax.nn.silu(val[:, :units]) * val[:, gap : gap + units]).astype(BF16)
        return dot(hidden, down[...])

    def routed_ffn(chunk):
        out = ffn(arrived[chunk].reshape(256, 2048), gate_up, GAP, ff, down_w)
        first, second = out[:128], out[128:]
        own_out[chunk] = jnp.where(c == 0, first, second)
        cross_send[chunk] = jnp.where(c == 0, second, first).astype(BF16)
        remote(
            cross_send.at[chunk], cross_recv.at[chunk], os_.at[chunk], or_.at[chunk], other
        ).start()

    def give(chunk):
        remote(
            cross_send.at[chunk], cross_recv.at[chunk], os_.at[chunk], or_.at[chunk], other
        ).wait()
        ret_send[chunk] = (
            (own_out[chunk] + cross_recv[chunk].astype(F32)).astype(BF16).reshape(16, 8, 2048)
        )

        def step(i, carry):
            p = lax.rem(mine + i, 16)
            remote(
                ret_send.at[chunk, p],
                ret_recv.at[chunk, mine],
                rs.at[chunk, i],
                rr.at[chunk, i],
                plane(p),
            ).start()
            return carry

        lax.fori_loop(1, 16, step, 0)
        ret_recv[chunk, mine] = ret_send[chunk, mine]

    forward(0)
    for load in loads[:3]:
        load.wait()
    crossed(0)
    routed_ffn(0)
    forward(1)
    give(0)
    crossed(1)
    routed_ffn(1)

    for load in loads[3:]:
        load.wait()
    for i in range(1, 4):
        src = lax.rem(x - i + 4, 4)
        remote(share_in.at[x], share_in.at[src], xs.at[i], xr.at[i], other).wait()
    shared = ffn(share_in[...].reshape(128, 2048), sgate_up, SGAP, sff, sdown_w)
    share_send[...] = shared.astype(BF16).reshape(4, 32, 2048)
    for i in (2, 1, 3):
        peer = lax.rem(x + i, 4)
        remote(
            share_send.at[peer], share_recv.at[i], bs.at[i], br.at[i], dev(peer, y, zl, zh, c)
        ).start()
    give(1)
    for i in range(1, 4):
        remote(share_send.at[0], share_recv.at[i], bs.at[i], br.at[i], other).wait()
    share_sum = share_send[x].astype(F32)
    for i in range(1, 4):
        share_sum = share_sum + share_recv[i].astype(F32)
    for z in range(4):
        mine_z = share_sum[z * 8 : z * 8 + 8]
        part[z, 0] = jnp.where(zh == 0, mine_z, 0.0)
        part[z, 1] = jnp.where(zh == 1, mine_z, 0.0)

    def take(chunk):
        def step(i, carry):
            src = lax.rem(mine - i + 16, 16)
            remote(
                ret_send.at[chunk, src],
                ret_recv.at[chunk, src],
                rs.at[chunk, i],
                rr.at[chunk, i],
                other,
            ).wait()
            return carry

        lax.fori_loop(1, 16, step, 0)
        back = ret_recv[chunk].reshape(128, 2048)
        w_hi = combines[chunk].astype(BF16)
        w_low = (combines[chunk] - w_hi.astype(F32)).astype(BF16)
        routed = (dot(w_hi, back) + dot(w_low, back)).reshape(2, 2, 8, 2048)
        first = pl.ds(pairs[chunk] * 2, 2)
        part[first] = part[first] + routed
        lsend[first] = part[first].reshape(2, 16, 2048).astype(BF16)

    take(0)
    remote(lsend.at[near], lrecv.at[0], ls.at[0], lr.at[0], dev(x, y, near, zh, c)).start()
    take(1)
    for i in range(2):
        remote(
            lsend.at[far[i]],
            lrecv.at[1 + zl % 2],
            ls.at[1 + i],
            lr.at[1 + zl % 2],
            dev(x, y, far[i], zh, c),
        ).start()
    remote(lsend.at[near], lrecv.at[0], ls.at[0], lr.at[0], other).wait()
    for i in range(2):
        remote(lsend.at[far[i]], lrecv.at[1 + i], ls.at[1 + i], lr.at[1 + i], other).wait()
    both = part[zl].reshape(16, 2048)
    for i in range(3):
        both = both + lrecv[i].astype(F32)
    hsend[...] = jnp.where(zh == 0, both[8:], both[:8]).astype(BF16)
    remote(hsend, hrecv, hs, hr, partner).start()
    kept = hidden_s[zh] + jnp.where(zh == 0, both[:8], both[8:])
    remote(hsend, hrecv, hs, hr, partner).wait()
    out_ref[...] = (kept + hrecv[...].astype(F32)).astype(BF16)


def layer(vmem_args, weights):
    gate, up, down, sgate, sup, sdown = weights
    width = gate.shape[1]
    return pl.pallas_call(
        layer_kernel,
        name="layer",
        out_shape=jax.ShapeDtypeStruct((8, width), BF16),
        in_specs=[vmem_spec()] * len(vmem_args) + [any_spec()] * 6,
        out_specs=vmem_spec(),
        scratch_shapes=[
            VMEM((GAP + gate.shape[0], width), BF16),
            VMEM(down.shape, BF16),
            VMEM((SGAP + sgate.shape[0], width), BF16),
            VMEM(sdown.shape, BF16),
            VMEM((16, REQ, MSG), BF16),
            VMEM((2, 64, 128), BF16),
            VMEM((64, width), BF16),
            VMEM((64, width), BF16),
            VMEM((4, 16, width), F32),
            VMEM((4, 16, width), BF16),
            VMEM((4, 16, width), BF16),
            VMEM((16, width), BF16),
            VMEM((16, width), BF16),
            VMEM((2, 8, width), F32),
            VMEM((4, 16, width), BF16),
            VMEM((2, 16, 8, width), BF16),
            VMEM((2, 2, 16, 8, width), BF16),
            VMEM((2, 128, width), F32),
            VMEM((2, 128, width), BF16),
            VMEM((2, 128, width), BF16),
            VMEM((2, 16, 8, width), BF16),
            VMEM((2, 16, 8, width), BF16),
            VMEM((4, 4, 8, width), BF16),
            VMEM((4, 32, width), BF16),
            VMEM((4, 32, width), BF16),
            VMEM((4, 2, 8, width), F32),
            VMEM((4, 16, width), BF16),
            VMEM((3, 16, width), BF16),
            VMEM((8, width), BF16),
            VMEM((8, width), BF16),
            DMA((6,)),
            DMA((16,)),
            DMA((16,)),
            DMA,
            DMA,
            DMA((4,)),
            DMA((4,)),
            DMA,
            DMA,
            DMA((3,)),
            DMA((3,)),
            DMA((2, 16)),
            DMA((2, 16)),
            DMA((2, 16)),
            DMA((2, 16)),
            DMA((2,)),
            DMA((2,)),
            DMA((2, 16)),
            DMA((2, 16)),
            DMA((4,)),
            DMA((4,)),
            DMA((4,)),
            DMA((4,)),
            DMA((3,)),
            DMA((3,)),
            DMA,
            DMA,
        ],
        compiler_params=pltpu.CompilerParams(
            collective_id=1, has_side_effects=True, vmem_limit_bytes=44 << 20
        ),
    )(*vmem_args, *weights)


def on_device(
    query_nope,
    query_rope,
    absorb_weight,
    value_weight,
    output_weight,
    cache_latent,
    cache_rope,
    node_length,
    new_latent,
    new_rope,
    parent_node,
    leaf_node,
    residual,
    norm_gain,
    router_weight,
    routes,
    expert_gate,
    expert_up,
    expert_down,
    shared_gate,
    shared_up,
    shared_down,
):
    q_all, routes8, resid2 = gather(
        query_nope[:, 0, :], query_rope[:, 0, :].T, routes, residual
    )
    absorb, value = absorb_weight[0], value_weight[0]
    msg = attend(
        node_length,
        q_all.reshape(16 * REQ, -1),
        absorb,
        value,
        cache_latent,
        jnp.swapaxes(cache_rope, 1, 2),
        leaf_node,
        parent_node,
    )
    return layer(
        (
            msg.reshape(16, REQ, MSG),
            q_all,
            routes8,
            resid2,
            absorb,
            value,
            new_latent,
            new_rope.T,
            output_weight,
            norm_gain[None, :],
            router_weight.T,
        ),
        (
            expert_gate[0].T,
            expert_up[0].T,
            expert_down[0],
            shared_gate.T,
            shared_up.T,
            shared_down,
        ),
    )


def solution(mesh):
    in_specs = (
        P("group", "expert", None),
        P("group", "expert", None),
        P("expert", None, None),
        P("expert", None, None),
        P("expert", None),
        P("group", None, None),
        P("group", None, None),
        P("group"),
        P("group", None),
        P("group", None),
        P(),
        P(),
        P(("group", "expert"), None),
        P(),
        P(),
        P(("group", "expert"), None),
        P(("group", "expert"), None, None),
        P(("group", "expert"), None, None),
        P(("group", "expert"), None, None),
        P(None, "group"),
        P(None, "group"),
        P("group", None),
    )
    out_specs = P(("group", "expert"), None)
    return jax.shard_map(
        on_device, mesh=mesh, in_specs=in_specs, out_specs=out_specs, check_vma=False
    )
```

time: 158 us -> 133 us (0.84)
  Pallas kernels: 136 us -> 116 us
  local copies, waits for them, and re-layouts: 20.2 us -> 16.2 us
    pallas_call x1, Pallas kernels: 30.6 us -> 21.4 us  [gather(): pl.pallas_call(gather_kernel, name='gather_queries', out_shape=(jax.Shape...]
    pallas_call x2 -> x1, Pallas kernels: 96.6 us -> 88.4 us  [layer(): pl.pallas_call(layer_kernel, name='layer', out_shape=jax.ShapeDtypeStruct...]
    pallas_call x1, Pallas kernels: 8.48 us -> 6.27 us  [attend(): pl.pallas_call(attn_kernel, name='attend_nodes', out_shape=jax.ShapeDtype...]
    unnamed x45 -> x47, local copies, waits for them, and re-layouts: 15.3 us -> 15.5 us
where the time goes in v2:
time: 133 us; the launch traced here: 132 us
  Pallas kernels  116 us (87%)
  local copies, waits for them, and re-layouts  16.2 us (12%)
    pallas_call x1, Pallas kernels, layer(): pl.pallas_call(layer_kernel, name='layer', out_shape=jax.ShapeDtypeStruct...  88.4 us
    pallas_call x1, Pallas kernels, gather(): pl.pallas_call(gather_kernel, name='gather_queries', out_shape=(jax.Shape...  21.4 us
    unnamed x47, local copies, waits for them, and re-layouts  15.5 us
    pallas_call x1, Pallas kernels, attend(): pl.pallas_call(attn_kernel, name='attend_nodes', out_shape=jax.ShapeDtype...  6.27 us

profile of v2, /device:TPU:24, one launch (start us, length us, event | category | flops | bytes accessed | tf_op | source)
XLA Modules:
  0.0 132.4 jit_solution(12384631022523893950)
XLA Ops:
  0.0 0.7 broadcast_in_dim.11.gain_ref
  0.7 0.8 copy-done.15
  1.5 0.8 copy-done.16
  2.2 0.7 copy-done.18
  2.9 0.7 copy-done.19
  3.6 21.4 %gather_queries.1 = (bf16[16,16,1536]{2,1,0:T(8,128)(2,1)S(1)}, s32[8,8,128]{2,1,0:T(8,128)S(1)}, bf16[2,8,2048]{2,1,0:T(8,128)(2,1)S(1)}) custom-call(bf16[128,128]{1,0:T(8,128)(2,1)S(1)} %bitcast.35, bf16[64,128]{1,0:T(8,128)(2,1)S(1)} %bitcast.37, s32[8,6]{1,0:T(8,128)S(1)} %copy-done.19, bf16[8,2048]{1,0:T(8,128)(2,1)S(1)} %copy-done.16), custom_call_target="tpu_custom_call" | custom-call | tf_op jit(solution)/shard_map/gather_queries/pallas_call | solution.py:133
  25.0 0.0 copy-start
  25.0 1.6 %copy-done = bf16[2,1024,512]{2,1,0:T(8,128)(2,1)S(1)} copy-done((bf16[2,1024,512]{2,1,0:T(8,128)(2,1)S(1)}, bf16[2,1024,512]{2,1,0:T(8,128)(2,1)}, u32[]{:S(2)}) %copy-start) | copy-done | bytes 2097176
  26.6 0.9 copy-done.8
  27.5 0.9 copy-done.10
  28.4 0.9 copy-done.12
  29.4 0.7 copy-done.20
  30.1 0.7 copy-done.21
  30.7 0.7 copy-done.22
  31.4 0.0 copy-start.14
  31.4 6.3 %attend_nodes.1 = bf16[256,1152]{1,0:T(8,128)(2,1)S(1)} custom-call(s32[2]{0:T(128)S(1)} %copy-done.21, bf16[256,1536]{1,0:T(8,128)(2,1)S(1)} %bitcast.22, bf16[128,512]{1,0:T(8,128)(2,1)S(1)} %bitcast.29, bf16[512,128]{1,0:T(8,128)(2,1)S(1)} %bitcast.31, bf16[2,1024,512]{2,1,0:T(8,128)(2,1)S(1)} %copy-done, bf16[2,64,1024]{2,1,0:T(8,128)(2,1)S(1)} %bitcast.33, ...), custom_call_target="tpu_custom_call" | custom-call | tf_op jit(solution)/shard_map/attend_nodes/pallas_call | solution.py:285
  37.8 0.0 copy-start.3
  37.8 1.4 %copy-done.3 = bf16[1,352,2048]{2,1,0:T(8,128)(2,1)S(1)} copy-done((bf16[1,352,2048]{2,1,0:T(8,128)(2,1)S(1)}, bf16[1,352,2048]{2,1,0:T(8,128)(2,1)}, u32[]{:S(2)}) %copy-start.3) | copy-done | bytes 1441816
  39.1 1.1 copy-done.5
  40.2 1.1 copy-done.6
  41.3 1.0 copy-done.7
  42.4 0.9 copy-done.13
  43.3 88.4 %layer.1 = bf16[8,2048]{1,0:T(8,128)(2,1)S(1)} custom-call(bf16[16,16,1152]{2,1,0:T(8,128)(2,1)S(1)} %bitcast.23, bf16[16,16,1536]{2,1,0:T(8,128)(2,1)S(1)} %get-tuple-element.8.q_ref, s32[8,8,128]{2,1,0:T(8,128)S(1)} %get-tuple-element.9.routes_ref, bf16[2,8,2048]{2,1,0:T(8,128)(2,1)S(1)} %get-tuple-element.10.resid_ref, bf16[128,512]{1,0:T(8,128)(2,1)S(1)} %bitcast.30, ...), custom_call_target="tpu_custom_call" | custom-call | tf_op jit(solution)/shard_map/layer/pallas_call | solution.py:713
  131.8 0.6 copy.24
  (27 shorter events, 0.0 us)
Async XLA Ops:
  0.7 0.8 copy-start.15
  1.5 0.8 copy-start.16
  2.2 0.7 copy-start.18
  2.9 0.7 copy-start.19
  3.6 34.1 %copy-start.17 = (bf16[128,64]{0,1:T(8,128)(2,1)S(1)}, bf16[128,64]{0,1:T(8,128)(2,1)}, u32[]{:S(2)}) copy-start(bf16[128,64]{0,1:T(8,128)(2,1)} %param.31) | copy-start | bytes 49156
  25.0 1.6 %copy-start = (bf16[2,1024,512]{2,1,0:T(8,128)(2,1)S(1)}, bf16[2,1024,512]{2,1,0:T(8,128)(2,1)}, u32[]{:S(2)}) copy-start(bf16[2,1024,512]{2,1,0:T(8,128)(2,1)} %lat_ref.1) | copy-start | bytes 6291460
  26.6 0.9 copy-start.8
  27.5 0.9 copy-start.10
  28.4 0.9 copy-start.12
  29.4 0.7 copy-start.20
  30.1 0.7 copy-start.21
  30.7 0.7 copy-start.22
  31.4 6.3 %copy-start.1 = (bf16[1,2048,352]{1,2,0:T(8,128)(2,1)S(1)}, bf16[1,2048,352]{1,2,0:T(8,128)(2,1)}, u32[]{:S(2)}) copy-start(bf16[1,2048,352]{1,2,0:T(8,128)(2,1)} %param.38) | copy-start | bytes 4325380
  31.4 6.3 %copy-start.2 = (bf16[1,2048,352]{1,2,0:T(8,128)(2,1)S(1)}, bf16[1,2048,352]{1,2,0:T(8,128)(2,1)}, u32[]{:S(2)}) copy-start(bf16[1,2048,352]{1,2,0:T(8,128)(2,1)} %param.39) | copy-start | bytes 4325380
  31.4 6.3 %copy-start.4 = (bf16[2048,176]{0,1:T(8,128)(2,1)S(1)}, bf16[2048,176]{0,1:T(8,128)(2,1)}, u32[]{:S(2)}) copy-start(bf16[2048,176]{0,1:T(8,128)(2,1)} %param.41) | copy-start | bytes 2162692
  31.4 6.3 %copy-start.9 = (bf16[1,128,512]{2,1,0:T(8,128)(2,1)S(1)}, bf16[1,128,512]{2,1,0:T(8,128)(2,1)}, u32[]{:S(2)}) copy-start(bf16[1,128,512]{2,1,0:T(8,128)(2,1)} %param.24) | copy-start | bytes 393220
  31.4 6.4 %copy-start.11 = (bf16[1,512,128]{2,1,0:T(8,128)(2,1)S(1)}, bf16[1,512,128]{2,1,0:T(8,128)(2,1)}, u32[]{:S(2)}) copy-start(bf16[1,512,128]{2,1,0:T(8,128)(2,1)} %param.25) | copy-start | bytes 393220
  31.4 6.4 %copy-start.14 = (bf16[128,512]{1,0:T(8,128)(2,1)S(1)}, bf16[128,512]{1,0:T(8,128)(2,1)}, u32[]{:S(2)}) copy-start(bf16[128,512]{1,0:T(8,128)(2,1)} %newlat_ref.1) | copy-start | bytes 393220
  37.8 1.4 %copy-start.3 = (bf16[1,352,2048]{2,1,0:T(8,128)(2,1)S(1)}, bf16[1,352,2048]{2,1,0:T(8,128)(2,1)}, u32[]{:S(2)}) copy-start(bf16[1,352,2048]{2,1,0:T(8,128)(2,1)} %param.40) | copy-start | bytes 4325380
  39.1 1.1 copy-start.5
  40.2 1.1 copy-start.6
  41.3 1.0 copy-start.7
  42.4 0.9 copy-start.13

commit v3 on v2

--- a/solution.py
+++ b/solution.py
@@ -23,8 +23,19 @@
     return pl.BlockSpec(memory_space=pltpu.VMEM)
 
 
-def any_spec():
-    return pl.BlockSpec(memory_space=pl.ANY)
+def hbm_spec():
+    return pl.BlockSpec(memory_space=pltpu.HBM)
+
+
+def stay(x):
+    return pltpu.with_memory_space_constraint(x, pltpu.HBM)
+
+
+def start_loads(pairs, sem):
+    loads = [pltpu.make_async_copy(src, dst, sem.at[i]) for i, (src, dst) in enumerate(pairs)]
+    for load in loads:
+        load.start()
+    return loads
 
 
 def coords():
@@ -73,9 +84,10 @@
 
 
 def gather_kernel(
-    nope_ref, rope_ref, routes_ref, resid_ref, qall, routes8, resid2, mine, zq, zqr, xq, xqr, rs, rr, zs, zr
+    nope_hbm, rope_hbm, routes_hbm, qall, routes8, nope_v, rope_v, routes_v, mine, wsem, zq, zqr, xq, xqr, rs, rr
 ):
     g, e, x, y, zl, zh, c = coords()
+    loads = start_loads([(nope_hbm, nope_v), (rope_hbm, rope_v), (routes_hbm, routes_v)], wsem)
     barrier = pltpu.get_barrier_semaphore()
     partner = dev(x, y, zl, 1 - zh, c)
     me = zl * 2 + zh
@@ -90,17 +102,18 @@
     di = lax.broadcasted_iota(jnp.int32, (rows, rows), 0)
     si = lax.broadcasted_iota(jnp.int32, (rows, rows), 1)
     perm = flag(si == (di % REQ) * QT + di // REQ)
-    nope = dot(perm, nope_ref[...]).astype(BF16)
-    rope = dot_nt(perm, rope_ref[...]).astype(BF16)
+    for load in loads:
+        load.wait()
+    nope = dot(perm, nope_v[...]).astype(BF16)
+    rope = dot_nt(perm, rope_v[...]).astype(BF16)
     qall[g] = jnp.concatenate(
         [nope[j * REQ : (j + 1) * REQ] for j in range(QT)]
         + [rope[j * REQ : (j + 1) * REQ] for j in range(QT)],
         axis=1,
     )
     mine[...] = jnp.zeros_like(mine)
-    mine[:, 0 : routes_ref.shape[1]] = routes_ref[...]
+    mine[:, 0 : routes_v.shape[1]] = routes_v[...]
     routes8[me] = mine[...]
-    resid2[zh] = resid_ref[...]
     pl.semaphore_wait(barrier, 10)
 
     own = qall.at[g]
@@ -108,7 +121,6 @@
         remote(own, own, zq.at[i], zqr.at[i], dev(x, y, lax.rem(zl + i, 4), zh, c)).start()
     for k in (1, 3, 2):
         remote(own, own, xq.at[0, k], xqr.at[0, k], dev(lax.rem(x + k, 4), y, zl, zh, c)).start()
-    remote(resid_ref, resid2.at[zh], zs, zr, partner).start()
     for k in range(1, 8):
         s = lax.rem(me + k, 8)
         remote(mine, routes8.at[me], rs.at[k], rr.at[k], dev(x, y, s // 2, s % 2, c)).start()
@@ -119,7 +131,6 @@
             remote(
                 block, block, xq.at[i, k], xqr.at[i, k], dev(lax.rem(x + k, 4), y, zl, zh, c)
             ).start()
-    remote(resid_ref, resid2.at[1 - zh], zs, zr, partner).wait()
     for k in range(1, 8):
         s = lax.rem(me - k + 8, 8)
         remote(mine, routes8.at[s], rs.at[k], rr.at[k], partner).wait()
@@ -129,32 +140,33 @@
             remote(own, block, xq.at[i, k], xqr.at[i, k], partner).wait()
 
 
-def gather(nope, rope_t, routes, residual):
+def gather(nope, rope_t, routes):
     return pl.pallas_call(
         gather_kernel,
         name="gather_queries",
         out_shape=(
             jax.ShapeDtypeStruct((16, REQ, QT * 192), BF16),
             jax.ShapeDtypeStruct((8, 8, 128), jnp.int32),
-            jax.ShapeDtypeStruct((2,) + residual.shape, BF16),
         ),
-        in_specs=[vmem_spec()] * 4,
-        out_specs=(vmem_spec(),) * 3,
+        in_specs=[hbm_spec()] * 3,
+        out_specs=(vmem_spec(),) * 2,
         scratch_shapes=[
+            VMEM(nope.shape, BF16),
+            VMEM(rope_t.shape, BF16),
+            VMEM(routes.shape, jnp.int32),
             VMEM((8, 128), jnp.int32),
+            DMA((3,)),
             DMA((4,)),
             DMA((4,)),
             DMA((4, 4)),
             DMA((4, 4)),
             DMA((8,)),
             DMA((8,)),
-            DMA,
-            DMA,
         ],
         compiler_params=pltpu.CompilerParams(
             collective_id=0, has_side_effects=True, vmem_limit_bytes=24 << 20
         ),
-    )(nope, rope_t, routes, residual)
+    )(stay(nope), stay(rope_t), stay(routes))
 
 
 TILE = 32
@@ -182,46 +194,70 @@
 
 
 def attn_kernel(
+    q_ref,
+    len_hbm,
+    absorb_hbm,
+    value_hbm,
+    lat_hbm,
+    rope_hbm,
+    leaf_hbm,
+    parent_hbm,
+    out_ref,
     len_ref,
-    q_ref,
     absorb_ref,
     value_ref,
     lat_ref,
     rope_ref,
     leaf_ref,
     parent_ref,
-    out_ref,
-    acc,
+    picked,
+    done,
+    wsem,
 ):
     g = lax.axis_index("group")
+    loads = start_loads(
+        [
+            (leaf_hbm, leaf_ref),
+            (parent_hbm, parent_ref),
+            (len_hbm, len_ref),
+            (absorb_hbm, absorb_ref),
+            (lat_hbm, lat_ref),
+            (rope_hbm, rope_ref),
+            (value_hbm, value_ref),
+        ],
+        wsem,
+    )
     requests = q_ref.shape[0]
     slots, most = lat_ref.shape[0], lat_ref.shape[1]
     scaling = float(128 + 64) ** (-0.5)
-    earlier = flag(
-        lax.broadcasted_iota(jnp.int32, (requests, requests), 0)
-        < lax.broadcasted_iota(jnp.int32, (requests, requests), 1)
-    )
-    acc[...] = jnp.zeros_like(acc)
+    ids_0 = lax.broadcasted_iota(jnp.int32, (requests, requests), 0)
+    ids_1 = lax.broadcasted_iota(jnp.int32, (requests, requests), 1)
+    earlier = flag(ids_0 < ids_1)
+    done[...] = jnp.zeros_like(done)
     lane = lax.broadcasted_iota(jnp.int32, (TILE, 128), 1)
+    for load in loads[:2]:
+        load.wait()
     parent_col = eye_column(parent_ref[...])
-    on_cols = []
+    places, on_cols, counts = [], [], []
     for slot in range(slots):
         on_row = on_path(leaf_ref[...], parent_col, g * slots + slot)
         row_f = jnp.where(on_row, 1.0, 0.0)
-        count = jnp.sum(row_f).astype(jnp.int32)
+        counts.append(jnp.sum(row_f).astype(jnp.int32))
         rank_row = dot(jnp.broadcast_to(row_f, (8, requests)).astype(BF16), earlier)[0:1]
         rank_row = jnp.where(on_row, rank_row, -1.0)
         rank_col = eye_column(rank_row)
         on_cols.append(rank_col >= 0.0)
-        rank_row = rank_row.astype(jnp.int32)
-        rank_col = rank_col.astype(jnp.int32)
+        places.append(rank_col.astype(jnp.int32))
+        picked[slot] = dot(flag(rank_row.astype(jnp.int32) == ids_0), q_ref[...]).astype(BF16)
+    for load in loads[2:]:
+        load.wait()
+
+    for slot in range(slots):
         length = len_ref[slot]
 
         def tile(keys, step, carry):
-            base = step * TILE
-            pick = flag(rank_row == lax.broadcasted_iota(jnp.int32, (TILE, requests), 0) + base)
-            place = flag(rank_col == lax.broadcasted_iota(jnp.int32, (requests, TILE), 1) + base)
-            qt = dot(pick, q_ref[...]).astype(BF16)
+            here = pl.ds(pl.multiple_of(step * TILE, TILE), TILE)
+            qt = picked[slot, here]
             nope = jnp.concatenate([qt[:, j * 128 : j * 128 + 128] for j in range(QT)], axis=0)
             rot = jnp.concatenate(
                 [qt[:, 1024 + j * 64 : 1024 + j * 64 + 64] for j in range(QT)], axis=0
@@ -242,21 +278,21 @@
                 for k in range(3):
                     piece = parts[k][j * TILE : (j + 1) * TILE]
                     tail = jnp.where(lane == k * 8 + j, piece, tail)
-            block = jnp.concatenate(
+            done[slot, here] = jnp.concatenate(
                 [valued[j * TILE : (j + 1) * TILE] for j in range(QT)] + [tail.astype(BF16)],
                 axis=1,
             )
-            acc[slot] += dot(place, block)
             return carry
 
-        tiles = (count + TILE - 1) // TILE
+        tiles = (counts[slot] + TILE - 1) // TILE
         for keys in range(KEYS, most + 1, KEYS):
 
             @pl.when((length > keys - KEYS) & (length <= keys))
             def _():
                 lax.fori_loop(0, tiles, lambda step, carry: tile(keys, step, carry), 0)
 
-    logs = [jnp.where(on_cols[s], join3(acc[s, :, 1024:]), NEGATIVE) for s in range(slots)]
+    acc = [dot(flag(places[s] == ids_1), done[s]) for s in range(slots)]
+    logs = [jnp.where(on_cols[s], join3(acc[s][:, 1024:]), NEGATIVE) for s in range(slots)]
     top = logs[0]
     for s in range(1, slots):
         top = jnp.maximum(top, logs[s])
@@ -268,7 +304,7 @@
     for j in range(QT):
         out = 0.0
         for s in range(slots):
-            out = out + (shares[s] / total)[:, j : j + 1] * acc[s, :, j * 128 : j * 128 + 128]
+            out = out + (shares[s] / total)[:, j : j + 1] * acc[s][:, j * 128 : j * 128 + 128]
         out_ref[:, j * 128 : j * 128 + 128] = out.astype(BF16)
     parts = split3(log_sum)
     lane = lax.broadcasted_iota(jnp.int32, (requests, 128), 1)
@@ -286,11 +322,36 @@
         attn_kernel,
         name="attend_nodes",
         out_shape=jax.ShapeDtypeStruct((requests, MSG), BF16),
-        in_specs=[pl.BlockSpec(memory_space=pltpu.SMEM)] + [vmem_spec()] * 7,
+        in_specs=[vmem_spec()] + [hbm_spec()] * 7,
         out_specs=vmem_spec(),
-        scratch_shapes=[VMEM((slots, requests, MSG), F32)],
+        scratch_shapes=[
+            pltpu.SMEM(node_length.shape, jnp.int32),
+            VMEM(absorb.shape, BF16),
+            VMEM(value.shape, BF16),
+            VMEM(cache_latent.shape, BF16),
+            VMEM(rope_t.shape, BF16),
+            VMEM((1, leaf.shape[0]), jnp.int32),
+            VMEM((1, parent.shape[0]), jnp.int32),
+            VMEM((slots, requests, q_all.shape[1]), BF16),
+            VMEM((slots, requests, MSG), BF16),
+            DMA((7,)),
+        ],
         compiler_params=pltpu.CompilerParams(vmem_limit_bytes=32 << 20),
-    )(node_length, q_all, absorb, value, cache_latent, rope_t, leaf[None, :], parent[None, :])
+    )(
+        q_all,
+        *map(
+            stay,
+            (
+                node_length,
+                absorb,
+                value,
+                cache_latent,
+                rope_t,
+                leaf[None, :],
+                parent[None, :],
+            ),
+        ),
+    )
 
 
 GAP = 384
@@ -301,14 +362,14 @@
     msg_ref,
     q_ref,
     routes_ref,
-    resid_ref,
-    absorb_ref,
-    value_ref,
-    newlat_ref,
-    newrope_ref,
-    outw_ref,
     gain_ref,
-    router_ref,
+    absorb_hbm,
+    value_hbm,
+    newlat_hbm,
+    newrope_hbm,
+    outw_hbm,
+    resid_hbm,
+    router_hbm,
     gate_hbm,
     up_hbm,
     down_hbm,
@@ -316,6 +377,13 @@
     sup_hbm,
     sdown_hbm,
     out_ref,
+    absorb_ref,
+    value_ref,
+    newlat_ref,
+    newrope_ref,
+    outw_ref,
+    resid_ref,
+    router_ref,
     gate_up,
     down_w,
     sgate_up,
@@ -344,8 +412,6 @@
     part,
     lsend,
     lrecv,
-    hsend,
-    hrecv,
     wsem,
     ms,
     mr,
@@ -353,8 +419,6 @@
     cr,
     ys,
     yr,
-    zs,
-    zr,
     ns,
     nr,
     ds,
@@ -371,8 +435,6 @@
     br,
     ls,
     lr,
-    hs,
-    hr,
 ):
     g, e, x, y, zl, zh, c = coords()
     mine = x * 4 + y
@@ -395,25 +457,38 @@
     for i in range(4):
         for k in range(1, 4):
             greet(barrier, dev(lax.rem(x + i, 4), lax.rem(y + k, 4), zl, zh, c))
-    loads = [
-        pltpu.make_async_copy(src, dst, wsem.at[i])
-        for i, (src, dst) in enumerate(
-            [
-                (gate_hbm, gate_up.at[pl.ds(0, ff)]),
-                (up_hbm, gate_up.at[pl.ds(GAP, ff)]),
-                (down_hbm, down_w),
-                (sgate_hbm, sgate_up.at[pl.ds(0, sff)]),
-                (sup_hbm, sgate_up.at[pl.ds(SGAP, sff)]),
-                (sdown_hbm, sdown_w),
-            ]
-        )
-    ]
-    for load in loads:
-        load.start()
+    lines = (zl, zl + 1 - 2 * (zl % 2), zl + 2 - 4 * (zl // 2), 3 - zl)
+    halves = (zh, 1 - zh)
+
+    def line(d):
+        return dev(x, y, lines[d // 2], halves[d % 2], c)
+
+    for d in (3, 5, 7):
+        greet(barrier, line(d))
+    loads = start_loads(
+        [
+            (absorb_hbm, absorb_ref),
+            (value_hbm, value_ref),
+            (newlat_hbm, newlat_ref),
+            (newrope_hbm, newrope_ref),
+            (outw_hbm, outw_ref),
+            (resid_hbm, resid_ref),
+            (router_hbm, router_ref),
+            (gate_hbm, gate_up.at[pl.ds(0, ff)]),
+            (up_hbm, gate_up.at[pl.ds(GAP, ff)]),
+            (down_hbm, down_w),
+            (sgate_hbm, sgate_up.at[pl.ds(0, sff)]),
+            (sup_hbm, sgate_up.at[pl.ds(SGAP, sff)]),
+            (sdown_hbm, sdown_w),
+        ],
+        wsem,
+    )
     gate_up[ff:GAP] = jnp.zeros((GAP - ff, gate_up.shape[1]), BF16)
     sgate_up[sff:SGAP] = jnp.zeros((SGAP - sff, sgate_up.shape[1]), BF16)
 
     scaling = float(128 + 64) ** (-0.5)
+    for load in loads[:4]:
+        load.wait()
     q = q_ref[g]
     nope = jnp.concatenate([q[:, j * 128 : j * 128 + 128] for j in range(QT)], axis=0)
     rot = jnp.concatenate([q[:, 1024 + j * 64 : 1024 + j * 64 + 64] for j in range(QT)], axis=0)
@@ -431,7 +506,7 @@
     new_valued = dot(summed.astype(BF16), value_ref[...])
     new_log = top + jnp.log(total)
 
-    pl.semaphore_wait(barrier, 29)
+    pl.semaphore_wait(barrier, 32)
 
     def send(i, carry):
         peer = lax.rem(g + i, 16)
@@ -491,6 +566,8 @@
     perm = flag(si == (di % 8) * REQ + req)
     valued_s[...] = dot(perm, valued).astype(BF16).reshape(2, 64, 128)
 
+    for load in loads[4:7]:
+        load.wait()
     csend[...] = dot(valued_s[1 - c], outw_ref[...]).astype(BF16)
     remote(csend, crecv, cs, cr, other).start()
     own = dot(valued_s[c], outw_ref[...])
@@ -504,20 +581,34 @@
     for i in (1, 3, 2):
         remote(ysend.at[0], yrecv.at[i], ys.at[i], yr.at[i], other).wait()
         total_row = total_row + yrecv[i].astype(F32)
+    own_8 = lax.broadcasted_iota(jnp.int32, (16, 1), 0) // 8 == zh
+    resid = resid_ref[...].astype(F32)
+    total_row = total_row + jnp.where(own_8, jnp.concatenate([resid, resid], axis=0), 0.0)
     zsend[...] = total_row.astype(BF16)
-    remote(zsend, zrecv, zs, zr, partner).start()
-    total_row = total_row + resid_ref[...].reshape(16, 2048).astype(F32)
-    remote(zsend, zrecv, zs, zr, partner).wait()
-    hidden = total_row + zrecv[...].astype(F32)
+    for d in (1, 3, 2, 5, 7, 4, 6):
+        remote(zsend, zrecv.at[d], ns.at[d], nr.at[d], line(d)).start()
+
+    def column(d):
+        remote(zsend, zrecv.at[d], ns.at[d], nr.at[d], other).wait()
+        return zrecv[d].astype(F32)
+
+    def norm(hidden):
+        square = jnp.mean(hidden * hidden, axis=1, keepdims=True)
+        return (hidden * lax.rsqrt(square + EPSILON) * gain_ref[...].astype(F32)).astype(BF16)
+
+    hidden = total_row + column(1)
     hidden_s[...] = hidden.reshape(2, 8, 2048)
-    square = jnp.mean(hidden * hidden, axis=1, keepdims=True)
-    normed[zl] = (hidden * lax.rsqrt(square + EPSILON) * gain_ref[...].astype(F32)).astype(BF16)
-    near = zl + 1 - 2 * (zl % 2)
-    far = (2 - 2 * (zl // 2), 3 - 2 * (zl // 2))
-    row = normed.at[zl]
-    remote(row, row, ns.at[0], nr.at[0], dev(x, y, near, zh, c)).start()
-    for i in range(2):
-        remote(row, row, ns.at[1 + i], nr.at[1 + zl % 2], dev(x, y, far[i], zh, c)).start()
+    normed[zl] = norm(hidden)
+    share_in[x, zl] = normed[zl].reshape(2, 8, 2048)[0]
+
+    @pl.when(zh == 1)
+    def _():
+        share_in[x, zl] = normed[zl].reshape(2, 8, 2048)[1]
+
+    for i in (2, 1, 3):
+        block = share_in.at[x, zl]
+        peer = dev(lax.rem(x + i, 4), y, zl, zh, c)
+        remote(block, block, xs.at[0, i], xr.at[0, i], peer).start()
 
     def pack(chunk):
         tokens = normed[pl.ds(pairs[chunk] * 2, 2)].reshape(32, 2048)
@@ -559,18 +650,20 @@
             + dot(w_low.astype(BF16), spread)
         ) * picks[chunk]
 
-    remote(row, normed.at[near], ns.at[0], nr.at[0], other).wait()
+    normed[lines[1]] = norm(column(2) + column(3))
     combine0 = pack(0)
-    for i in range(2):
-        remote(row, normed.at[far[i]], ns.at[1 + i], nr.at[1 + i], other).wait()
+    normed[lines[2]] = norm(column(4) + column(5))
+    normed[lines[3]] = norm(column(6) + column(7))
     combine1 = pack(1)
     combines = (combine0, combine1)
-    for z in range(4):
-        both = normed[z].reshape(2, 8, 2048)
-        share_in[x, z] = jnp.where(zh == 0, both[0], both[1])
-    for i in (2, 1, 3):
-        peer = lax.rem(x + i, 4)
-        remote(share_in.at[x], share_in.at[x], xs.at[i], xr.at[i], dev(peer, y, zl, zh, c)).start()
+    for d in range(1, 4):
+        both = normed[lines[d]].reshape(2, 8, 2048)
+        share_in[x, lines[d]] = jnp.where(zh == 0, both[0], both[1])
+    for i in (1, 3, 2):
+        block = share_in.at[lax.rem(x - i + 4, 4), zl]
+        remote(share_in.at[x, zl], block, xs.at[0, i], xr.at[0, i], other).wait()
+        for d in range(1, 4):
+            remote(block, block, xs.at[d, i], xr.at[d, i], line(2 * d)).start()
 
     def forward(chunk):
         def step(i, carry):
@@ -630,7 +723,7 @@
         ret_recv[chunk, mine] = ret_send[chunk, mine]
 
     forward(0)
-    for load in loads[:3]:
+    for load in loads[7:10]:
         load.wait()
     crossed(0)
     routed_ffn(0)
@@ -639,11 +732,14 @@
     crossed(1)
     routed_ffn(1)
 
-    for load in loads[3:]:
+    for load in loads[10:]:
         load.wait()
-    for i in range(1, 4):
+    for i in (1, 3, 2):
         src = lax.rem(x - i + 4, 4)
-        remote(share_in.at[x], share_in.at[src], xs.at[i], xr.at[i], other).wait()
+        for d in range(1, 4):
+            remote(
+                share_in.at[src, zl], share_in.at[src, lines[d]], xs.at[d, i], xr.at[d, i], other
+            ).wait()
     shared = ffn(share_in[...].reshape(128, 2048), sgate_up, SGAP, sff, sdown_w)
     share_send[...] = shared.astype(BF16).reshape(4, 32, 2048)
     for i in (2, 1, 3):
@@ -681,42 +777,36 @@
         routed = (dot(w_hi, back) + dot(w_low, back)).reshape(2, 2, 8, 2048)
         first = pl.ds(pairs[chunk] * 2, 2)
         part[first] = part[first] + routed
-        lsend[first] = part[first].reshape(2, 16, 2048).astype(BF16)
+        lsend[first] = part[first].astype(BF16)
+
+    def hand(d):
+        block = lsend.at[lines[d // 2], halves[d % 2]]
+        return remote(block, lrecv.at[d], ls.at[d], lr.at[d], line(d))
 
     take(0)
-    remote(lsend.at[near], lrecv.at[0], ls.at[0], lr.at[0], dev(x, y, near, zh, c)).start()
+    for d in (1, 3, 2):
+        hand(d).start()
     take(1)
-    for i in range(2):
-        remote(
-            lsend.at[far[i]],
-            lrecv.at[1 + zl % 2],
-            ls.at[1 + i],
-            lr.at[1 + zl % 2],
-            dev(x, y, far[i], zh, c),
-        ).start()
-    remote(lsend.at[near], lrecv.at[0], ls.at[0], lr.at[0], other).wait()
-    for i in range(2):
-        remote(lsend.at[far[i]], lrecv.at[1 + i], ls.at[1 + i], lr.at[1 + i], other).wait()
-    both = part[zl].reshape(16, 2048)
-    for i in range(3):
-        both = both + lrecv[i].astype(F32)
-    hsend[...] = jnp.where(zh == 0, both[8:], both[:8]).astype(BF16)
-    remote(hsend, hrecv, hs, hr, partner).start()
-    kept = hidden_s[zh] + jnp.where(zh == 0, both[:8], both[8:])
-    remote(hsend, hrecv, hs, hr, partner).wait()
-    out_ref[...] = (kept + hrecv[...].astype(F32)).astype(BF16)
-
-
-def layer(vmem_args, weights):
+    for d in (5, 7, 4, 6):
+        hand(d).start()
+    result = hidden_s[zh] + part[zl, zh]
+    for d in (2, 1, 3, 4, 6, 5, 7):
+        hand(d).wait()
+        result = result + lrecv[d].astype(F32)
+    out_ref[...] = result.astype(BF16)
+
+
+def layer(vmem_args, more, weights):
     gate, up, down, sgate, sup, sdown = weights
     width = gate.shape[1]
     return pl.pallas_call(
         layer_kernel,
         name="layer",
         out_shape=jax.ShapeDtypeStruct((8, width), BF16),
-        in_specs=[vmem_spec()] * len(vmem_args) + [any_spec()] * 6,
+        in_specs=[vmem_spec()] * len(vmem_args) + [hbm_spec()] * (len(more) + 6),
         out_specs=vmem_spec(),
-        scratch_shapes=[
+        scratch_shapes=[VMEM(m.shape, BF16) for m in more]
+        + [
             VMEM((GAP + gate.shape[0], width), BF16),
             VMEM(down.shape, BF16),
             VMEM((SGAP + sgate.shape[0], width), BF16),
@@ -729,7 +819,7 @@
             VMEM((4, 16, width), BF16),
             VMEM((4, 16, width), BF16),
             VMEM((16, width), BF16),
-            VMEM((16, width), BF16),
+            VMEM((8, 16, width), BF16),
             VMEM((2, 8, width), F32),
             VMEM((4, 16, width), BF16),
             VMEM((2, 16, 8, width), BF16),
@@ -743,21 +833,17 @@
             VMEM((4, 32, width), BF16),
             VMEM((4, 32, width), BF16),
             VMEM((4, 2, 8, width), F32),
-            VMEM((4, 16, width), BF16),
-            VMEM((3, 16, width), BF16),
-            VMEM((8, width), BF16),
-            VMEM((8, width), BF16),
-            DMA((6,)),
+            VMEM((4, 2, 8, width), BF16),
+            VMEM((8, 8, width), BF16),
+            DMA((13,)),
             DMA((16,)),
             DMA((16,)),
             DMA,
             DMA,
             DMA((4,)),
             DMA((4,)),
-            DMA,
-            DMA,
-            DMA((3,)),
-            DMA((3,)),
+            DMA((8,)),
+            DMA((8,)),
             DMA((2, 16)),
             DMA((2, 16)),
             DMA((2, 16)),
@@ -766,19 +852,17 @@
             DMA((2,)),
             DMA((2, 16)),
             DMA((2, 16)),
+            DMA((4, 4)),
+            DMA((4, 4)),
             DMA((4,)),
             DMA((4,)),
-            DMA((4,)),
-            DMA((4,)),
-            DMA((3,)),
-            DMA((3,)),
-            DMA,
-            DMA,
+            DMA((8,)),
+            DMA((8,)),
         ],
         compiler_params=pltpu.CompilerParams(
             collective_id=1, has_side_effects=True, vmem_limit_bytes=44 << 20
         ),
-    )(*vmem_args, *weights)
+    )(*vmem_args, *map(stay, more), *map(stay, weights))
 
 
 def on_device(
@@ -805,9 +889,7 @@
     shared_up,
     shared_down,
 ):
-    q_all, routes8, resid2 = gather(
-        query_nope[:, 0, :], query_rope[:, 0, :].T, routes, residual
-    )
+    q_all, routes8 = gather(query_nope[:, 0, :], query_rope[:, 0, :].T, routes)
     absorb, value = absorb_weight[0], value_weight[0]
     msg = attend(
         node_length,
@@ -824,13 +906,15 @@
             msg.reshape(16, REQ, MSG),
             q_all,
             routes8,
-            resid2,
+            norm_gain[None, :],
+        ),
+        (
             absorb,
             value,
             new_latent,
             new_rope.T,
             output_weight,
-            norm_gain[None, :],
+            residual,
             router_weight.T,
         ),
         (

time: 133 us -> 108 us (0.81)
  local copies, waits for them, and re-layouts: 16.2 us -> 1.31 us
  Pallas kernels: 116 us -> 106 us
    unnamed x47 -> x1, local copies, waits for them, and re-layouts: 15.5 us -> 0.62 us
    pallas_call x1, Pallas kernels: 88.4 us -> 79.3 us  [layer(): pl.pallas_call(layer_kernel, name='layer', out_shape=jax.ShapeDtypeStruct...]
where the time goes in v3:
time: 108 us; the launch traced here: 107 us
  Pallas kernels  106 us (98%)
  local copies, waits for them, and re-layouts  1.31 us (1%)
    pallas_call x1, Pallas kernels, layer(): pl.pallas_call(layer_kernel, name='layer', out_shape=jax.ShapeDtypeStruct...  79.3 us
    pallas_call x1, Pallas kernels, gather(): pl.pallas_call(gather_kernel, name='gather_queries', out_shape=(jax.Shape...  21.2 us
    pallas_call x1, Pallas kernels, attend(): pl.pallas_call(attn_kernel, name='attend_nodes', out_shape=jax.ShapeDtype...  5.56 us

profile of v3, /device:TPU:24, one launch (start us, length us, event | category | flops | bytes accessed | tf_op | source)
XLA Modules:
  0.0 107.4 jit_solution(8827515507598152599)
XLA Ops:
  0.0 0.7 broadcast_in_dim.11.gain_ref
  0.7 21.2 %gather_queries.1 = (bf16[16,16,1536]{2,1,0:T(8,128)(2,1)S(1)}, s32[8,8,128]{2,1,0:T(8,128)S(1)}) custom-call(bf16[128,128]{1,0:T(8,128)(2,1)} %bitcast.35, bf16[64,128]{1,0:T(8,128)(2,1)} %bitcast.37, s32[8,6]{1,0:T(8,128)} %routes_hbm.1), custom_call_target="tpu_custom_call" | custom-call | tf_op jit(solution)/shard_map/gather_queries/pallas_call | solution.py:144
  21.9 5.6 %attend_nodes.1 = bf16[256,1152]{1,0:T(8,128)(2,1)S(1)} custom-call(bf16[256,1536]{1,0:T(8,128)(2,1)S(1)} %bitcast.22, s32[2]{0:T(128)} %len_hbm.1, bf16[128,512]{1,0:T(8,128)(2,1)} %bitcast.29, bf16[512,128]{1,0:T(8,128)(2,1)} %bitcast.31, bf16[2,1024,512]{2,1,0:T(8,128)(2,1)} %lat_hbm.1, bf16[2,64,1024]{2,1,0:T(8,128)(2,1)} %bitcast.33, ...), custom_call_target="tpu_custom_call" | custom-call | tf_op jit(solution)/shard_map/attend_nodes/pallas_call | solution.py:321
  27.4 79.3 %layer.1 = bf16[8,2048]{1,0:T(8,128)(2,1)S(1)} custom-call(bf16[16,16,1152]{2,1,0:T(8,128)(2,1)S(1)} %bitcast.23, bf16[16,16,1536]{2,1,0:T(8,128)(2,1)S(1)} %get-tuple-element.7.q_ref, s32[8,8,128]{2,1,0:T(8,128)S(1)} %get-tuple-element.8.routes_ref, bf16[1,2048]{1,0:T(2,128)(2,1)S(1)} %broadcast_in_dim.11.gain_ref, bf16[128,512]{1,0:T(8,128)(2,1)} %bitcast.30, ...), custom_call_target="tpu_custom_call" | custom-call | tf_op jit(solution)/shard_map/layer/pallas_call | solution.py:802
  106.8 0.6 copy.24

commit v4 on v3

--- a/solution.py
+++ b/solution.py
@@ -83,17 +83,78 @@
     return lax.dot_general(a, b, (((1,), (1,)), ((), ())), preferred_element_type=F32)
 
 
+def on_path(leaf_row, parent_col, node):
+    nodes = parent_col.shape[0]
+    ids = lax.broadcasted_iota(jnp.int32, (nodes, leaf_row.shape[1]), 0)
+    mid = jnp.sum(jnp.where(leaf_row == ids, parent_col, 0), axis=0, keepdims=True)
+    top = jnp.sum(jnp.where(mid == ids, parent_col, 0), axis=0, keepdims=True)
+    return (leaf_row == node) | (mid == node) | (top == node)
+
+
 def gather_kernel(
-    nope_hbm, rope_hbm, routes_hbm, qall, routes8, nope_v, rope_v, routes_v, mine, wsem, zq, zqr, xq, xqr, rs, rr
+    nope_hbm,
+    rope_hbm,
+    routes_hbm,
+    leaf_hbm,
+    parent_hbm,
+    outw_hbm,
+    lat_hbm,
+    krope_hbm,
+    absorb_hbm,
+    value_hbm,
+    qall,
+    routes8,
+    pick_ref,
+    place_ref,
+    outw,
+    lat_ref,
+    krope_ref,
+    absorb_ref,
+    value_ref,
+    nope_v,
+    rope_v,
+    routes_v,
+    leaf_v,
+    parent_v,
+    mine,
+    wsem,
+    zq,
+    zqr,
+    xq,
+    xqr,
+    rs,
+    rr,
+    ys,
+    yr,
+    cs,
+    cr,
 ):
     g, e, x, y, zl, zh, c = coords()
-    loads = start_loads([(nope_hbm, nope_v), (rope_hbm, rope_v), (routes_hbm, routes_v)], wsem)
+    half = outw.shape[3]
+    loads = start_loads(
+        [
+            (nope_hbm, nope_v),
+            (rope_hbm, rope_v),
+            (routes_hbm, routes_v),
+            (leaf_hbm, leaf_v),
+            (parent_hbm, parent_v),
+            (outw_hbm.at[:, pl.ds(0, half)], outw.at[y, c]),
+            (lat_hbm, lat_ref),
+            (krope_hbm, krope_ref),
+            (absorb_hbm, absorb_ref),
+            (value_hbm, value_ref),
+        ],
+        wsem,
+    )
     barrier = pltpu.get_barrier_semaphore()
     partner = dev(x, y, zl, 1 - zh, c)
+    other = dev(x, y, zl, zh, 1 - c)
     me = zl * 2 + zh
     for i in range(1, 4):
         greet(barrier, dev(lax.rem(x + i, 4), y, zl, zh, c))
         greet(barrier, dev(x, y, lax.rem(zl + i, 4), zh, c))
+        greet(barrier, dev(x, lax.rem(y + i, 4), zl, zh, c))
+    greet(barrier, other)
     for k in (1, 3, 5, 7):
         s = lax.rem(me + k, 8)
         greet(barrier, dev(x, y, s // 2, s % 2, c))
@@ -102,7 +163,7 @@
     di = lax.broadcasted_iota(jnp.int32, (rows, rows), 0)
     si = lax.broadcasted_iota(jnp.int32, (rows, rows), 1)
     perm = flag(si == (di % REQ) * QT + di // REQ)
-    for load in loads:
+    for load in loads[:3]:
         load.wait()
     nope = dot(perm, nope_v[...]).astype(BF16)
     rope = dot_nt(perm, rope_v[...]).astype(BF16)
@@ -114,23 +175,54 @@
     mine[...] = jnp.zeros_like(mine)
     mine[:, 0 : routes_v.shape[1]] = routes_v[...]
     routes8[me] = mine[...]
-    pl.semaphore_wait(barrier, 10)
+    pl.semaphore_wait(barrier, 14)
 
     own = qall.at[g]
     for i in (1, 3, 2):
         remote(own, own, zq.at[i], zqr.at[i], dev(x, y, lax.rem(zl + i, 4), zh, c)).start()
     for k in (1, 3, 2):
         remote(own, own, xq.at[0, k], xqr.at[0, k], dev(lax.rem(x + k, 4), y, zl, zh, c)).start()
+    for load in loads[3:6]:
+        load.wait()
+    own_w = outw.at[y, c]
+    for i in (1, 3, 2):
+        remote(own_w, own_w, ys.at[i], yr.at[i], dev(x, lax.rem(y + i, 4), zl, zh, c)).start()
+    remote(own_w, own_w, cs.at[0], cr.at[0], other).start()
     for k in range(1, 8):
         s = lax.rem(me + k, 8)
         remote(mine, routes8.at[me], rs.at[k], rr.at[k], dev(x, y, s // 2, s % 2, c)).start()
-    for i in (1, 3, 2):
+
+    def pass_on(i):
         block = qall.at[lax.rem(zl - i + 4, 4) * 4 + x]
         remote(own, block, zq.at[i], zqr.at[i], partner).wait()
         for k in (1, 3, 2):
             remote(
                 block, block, xq.at[i, k], xqr.at[i, k], dev(lax.rem(x + k, 4), y, zl, zh, c)
             ).start()
+
+    pass_on(1)
+    pass_on(3)
+    pass_on(2)
+
+    slots, _, requests = pick_ref.shape
+    ids_0 = lax.broadcasted_iota(jnp.int32, (requests, requests), 0)
+    ids_1 = lax.broadcasted_iota(jnp.int32, (requests, requests), 1)
+    earlier = flag(ids_0 < ids_1)
+    parent_col = eye_column(parent_v[...])
+    for slot in range(slots):
+        on_row = on_path(leaf_v[...], parent_col, g * slots + slot)
+        row_f = jnp.where(on_row, 1.0, 0.0)
+        rank_row = dot(jnp.broadcast_to(row_f, (8, requests)).astype(BF16), earlier)[0:1]
+        rank_row = jnp.where(on_row, rank_row, -1.0)
+        pick_ref[slot] = flag(rank_row.astype(jnp.int32) == ids_0)
+        place_ref[slot] = flag(eye_column(rank_row).astype(jnp.int32) == ids_1)
+
+    for i in (1, 3, 2):
+        block = outw.at[lax.rem(y - i + 4, 4), c]
+        remote(own_w, block, ys.at[i], yr.at[i], other).wait()
+        remote(block, block, cs.at[i], cr.at[i], other).start()
+    for load in loads[6:]:
+        load.wait()
     for k in range(1, 8):
         s = lax.rem(me - k + 8, 8)
         remote(mine, routes8.at[s], rs.at[k], rr.at[k], partner).wait()
@@ -138,35 +230,58 @@
         for k in (1, 3, 2):
             block = qall.at[lax.rem(zl - i + 4, 4) * 4 + lax.rem(x - k + 4, 4)]
             remote(own, block, xq.at[i, k], xqr.at[i, k], partner).wait()
-
-
-def gather(nope, rope_t, routes):
+    for i in range(4):
+        y_of = lax.rem(y - i + 4, 4)
+        remote(outw.at[y_of, c], outw.at[y_of, 1 - c], cs.at[i], cr.at[i], other).wait()
+
+
+def gather(nope, rope_t, routes, leaf, parent, outw, lat, krope_t, absorb, value):
+    requests = leaf.shape[0]
+    slots = lat.shape[0]
     return pl.pallas_call(
         gather_kernel,
         name="gather_queries",
         out_shape=(
             jax.ShapeDtypeStruct((16, REQ, QT * 192), BF16),
             jax.ShapeDtypeStruct((8, 8, 128), jnp.int32),
+            jax.ShapeDtypeStruct((slots, requests, requests), BF16),
+            jax.ShapeDtypeStruct((slots, requests, requests), BF16),
+            jax.ShapeDtypeStruct((4, 2, outw.shape[0], outw.shape[1] // 2), BF16),
+            jax.ShapeDtypeStruct(lat.shape, BF16),
+            jax.ShapeDtypeStruct(krope_t.shape, BF16),
+            jax.ShapeDtypeStruct(absorb.shape, BF16),
+            jax.ShapeDtypeStruct(value.shape, BF16),
         ),
-        in_specs=[hbm_spec()] * 3,
-        out_specs=(vmem_spec(),) * 2,
+        in_specs=[hbm_spec()] * 10,
+        out_specs=(vmem_spec(),) * 9,
         scratch_shapes=[
             VMEM(nope.shape, BF16),
             VMEM(rope_t.shape, BF16),
             VMEM(routes.shape, jnp.int32),
+            VMEM((1, requests), jnp.int32),
+            VMEM((1, parent.shape[0]), jnp.int32),
             VMEM((8, 128), jnp.int32),
-            DMA((3,)),
+            DMA((10,)),
             DMA((4,)),
             DMA((4,)),
             DMA((4, 4)),
             DMA((4, 4)),
             DMA((8,)),
             DMA((8,)),
+            DMA((4,)),
+            DMA((4,)),
+            DMA((4,)),
+            DMA((4,)),
         ],
         compiler_params=pltpu.CompilerParams(
             collective_id=0, has_side_effects=True, vmem_limit_bytes=24 << 20
         ),
-    )(stay(nope), stay(rope_t), stay(routes))
+    )(
+        *map(
+            stay,
+            (nope, rope_t, routes, leaf[None, :], parent[None, :], outw, lat, krope_t, absorb, value),
+        )
+    )
 
 
 TILE = 32
@@ -185,72 +300,32 @@
     return part[:, 0:8] + part[:, 8:16] + part[:, 16:24]
 
 
-def on_path(leaf_row, parent_col, node):
-    nodes = parent_col.shape[0]
-    ids = lax.broadcasted_iota(jnp.int32, (nodes, leaf_row.shape[1]), 0)
-    mid = jnp.sum(jnp.where(leaf_row == ids, parent_col, 0), axis=0, keepdims=True)
-    top = jnp.sum(jnp.where(mid == ids, parent_col, 0), axis=0, keepdims=True)
-    return (leaf_row == node) | (mid == node) | (top == node)
-
-
 def attn_kernel(
     q_ref,
-    len_hbm,
-    absorb_hbm,
-    value_hbm,
-    lat_hbm,
-    rope_hbm,
-    leaf_hbm,
-    parent_hbm,
-    out_ref,
-    len_ref,
+    pick_ref,
+    place_ref,
     absorb_ref,
     value_ref,
     lat_ref,
     rope_ref,
-    leaf_ref,
-    parent_ref,
+    len_hbm,
+    out_ref,
+    len_ref,
     picked,
     done,
     wsem,
 ):
-    g = lax.axis_index("group")
-    loads = start_loads(
-        [
-            (leaf_hbm, leaf_ref),
-            (parent_hbm, parent_ref),
-            (len_hbm, len_ref),
-            (absorb_hbm, absorb_ref),
-            (lat_hbm, lat_ref),
-            (rope_hbm, rope_ref),
-            (value_hbm, value_ref),
-        ],
-        wsem,
-    )
+    (load,) = start_loads([(len_hbm, len_ref)], wsem)
     requests = q_ref.shape[0]
     slots, most = lat_ref.shape[0], lat_ref.shape[1]
     scaling = float(128 + 64) ** (-0.5)
-    ids_0 = lax.broadcasted_iota(jnp.int32, (requests, requests), 0)
-    ids_1 = lax.broadcasted_iota(jnp.int32, (requests, requests), 1)
-    earlier = flag(ids_0 < ids_1)
     done[...] = jnp.zeros_like(done)
     lane = lax.broadcasted_iota(jnp.int32, (TILE, 128), 1)
-    for load in loads[:2]:
-        load.wait()
-    parent_col = eye_column(parent_ref[...])
-    places, on_cols, counts = [], [], []
+    counts = []
     for slot in range(slots):
-        on_row = on_path(leaf_ref[...], parent_col, g * slots + slot)
-        row_f = jnp.where(on_row, 1.0, 0.0)
-        counts.append(jnp.sum(row_f).astype(jnp.int32))
-        rank_row = dot(jnp.broadcast_to(row_f, (8, requests)).astype(BF16), earlier)[0:1]
-        rank_row = jnp.where(on_row, rank_row, -1.0)
-        rank_col = eye_column(rank_row)
-        on_cols.append(rank_col >= 0.0)
-        places.append(rank_col.astype(jnp.int32))
-        picked[slot] = dot(flag(rank_row.astype(jnp.int32) == ids_0), q_ref[...]).astype(BF16)
-    for load in loads[2:]:
-        load.wait()
+        picked[slot] = dot(pick_ref[slot], q_ref[...]).astype(BF16)
+        counts.append(jnp.sum(pick_ref[slot].astype(F32)).astype(jnp.int32))
+    load.wait()
 
     for slot in range(slots):
         length = len_ref[slot]
@@ -273,7 +348,7 @@
             attended = (summed / total).astype(BF16)
             valued = dot(attended, value_ref[...]).astype(BF16)
             parts = split3(top + jnp.log(total))
-            tail = jnp.zeros((TILE, 128), F32)
+            tail = jnp.where(lane == 24, 1.0, 0.0)
             for j in range(QT):
                 for k in range(3):
                     piece = parts[k][j * TILE : (j + 1) * TILE]
@@ -291,8 +366,10 @@
             def _():
                 lax.fori_loop(0, tiles, lambda step, carry: tile(keys, step, carry), 0)
 
-    acc = [dot(flag(places[s] == ids_1), done[s]) for s in range(slots)]
-    logs = [jnp.where(on_cols[s], join3(acc[s][:, 1024:]), NEGATIVE) for s in range(slots)]
+    acc = [dot(place_ref[s], done[s]) for s in range(slots)]
+    logs = [
+        jnp.where(a[:, 1048:1049] > 0.5, join3(a[:, 1024:]), NEGATIVE) for a in acc
+    ]
     top = logs[0]
     for s in range(1, slots):
         top = jnp.maximum(top, logs[s])
@@ -315,43 +392,23 @@
     out_ref[:, 1024:] = tail.astype(BF16)
 
 
-def attend(node_length, q_all, absorb, value, cache_latent, rope_t, leaf, parent):
+def attend(node_length, q_all, pick, place, absorb, value, lat, rope_t):
     requests = q_all.shape[0]
-    slots = cache_latent.shape[0]
+    slots = lat.shape[0]
     return pl.pallas_call(
         attn_kernel,
         name="attend_nodes",
         out_shape=jax.ShapeDtypeStruct((requests, MSG), BF16),
-        in_specs=[vmem_spec()] + [hbm_spec()] * 7,
+        in_specs=[vmem_spec()] * 7 + [hbm_spec()],
         out_specs=vmem_spec(),
         scratch_shapes=[
             pltpu.SMEM(node_length.shape, jnp.int32),
-            VMEM(absorb.shape, BF16),
-            VMEM(value.shape, BF16),
-            VMEM(cache_latent.shape, BF16),
-            VMEM(rope_t.shape, BF16),
-            VMEM((1, leaf.shape[0]), jnp.int32),
-            VMEM((1, parent.shape[0]), jnp.int32),
             VMEM((slots, requests, q_all.shape[1]), BF16),
             VMEM((slots, requests, MSG), BF16),
-            DMA((7,)),
+            DMA((1,)),
         ],
         compiler_params=pltpu.CompilerParams(vmem_limit_bytes=32 << 20),
-    )(
-        q_all,
-        *map(
-            stay,
-            (
-                node_length,
-                absorb,
-                value,
-                cache_latent,
-                rope_t,
-                leaf[None, :],
-                parent[None, :],
-            ),
-        ),
-    )
+    )(q_all, pick, place, absorb, value, lat, rope_t, stay(node_length))
 
 
 GAP = 384
@@ -362,14 +419,15 @@
     msg_ref,
     q_ref,
     routes_ref,
-    gain_ref,
-    absorb_hbm,
-    value_hbm,
+    outw1,
+    absorb_ref,
+    value_ref,
+    gain_hbm,
     newlat_hbm,
     newrope_hbm,
-    outw_hbm,
     resid_hbm,
     router_hbm,
+    outw_hbm,
     gate_hbm,
     up_hbm,
     down_hbm,
@@ -377,24 +435,19 @@
     sup_hbm,
     sdown_hbm,
     out_ref,
-    absorb_ref,
-    value_ref,
+    gain_ref,
     newlat_ref,
     newrope_ref,
-    outw_ref,
     resid_ref,
     router_ref,
+    outw2,
     gate_up,
     down_w,
     sgate_up,
     sdown_w,
     got,
     valued_s,
-    csend,
-    crecv,
-    acc,
-    ysend,
-    yrecv,
+    vin,
     zsend,
     zrecv,
     hidden_s,
@@ -419,6 +472,8 @@
     cr,
     ys,
     yr,
+    vs,
+    vr,
     ns,
     nr,
     ds,
@@ -438,6 +493,7 @@
 ):
     g, e, x, y, zl, zh, c = coords()
     mine = x * 4 + y
+    half = outw2.shape[3]
     ff = gate_hbm.shape[0]
     sff = sgate_hbm.shape[0]
     barrier = pltpu.get_barrier_semaphore()
@@ -465,15 +521,16 @@
 
     for d in (3, 5, 7):
         greet(barrier, line(d))
+    for i in range(1, 4):
+        greet(barrier, dev(x, lax.rem(y + i, 4), zl, zh, 1 - c))
     loads = start_loads(
         [
-            (absorb_hbm, absorb_ref),
-            (value_hbm, value_ref),
+            (gain_hbm, gain_ref),
             (newlat_hbm, newlat_ref),
             (newrope_hbm, newrope_ref),
-            (outw_hbm, outw_ref),
             (resid_hbm, resid_ref),
             (router_hbm, router_ref),
+            (outw_hbm.at[:, pl.ds(half, half)], outw2.at[y, c]),
             (gate_hbm, gate_up.at[pl.ds(0, ff)]),
             (up_hbm, gate_up.at[pl.ds(GAP, ff)]),
             (down_hbm, down_w),
@@ -486,8 +543,24 @@
     gate_up[ff:GAP] = jnp.zeros((GAP - ff, gate_up.shape[1]), BF16)
     sgate_up[sff:SGAP] = jnp.zeros((SGAP - sff, sgate_up.shape[1]), BF16)
 
+    pl.semaphore_wait(barrier, 35)
+
+    def send(i, carry):
+        peer = lax.rem(g + i, 16)
+        remote(msg_ref.at[peer], got.at[g], ms.at[i], mr.at[i], (peer, e)).start()
+        return carry
+
+    lax.fori_loop(1, 16, send, 0)
+    got[g] = msg_ref[g]
+
+    loads[5].wait()
+    own_w = outw2.at[y, c]
+    for i in (1, 3, 2):
+        remote(own_w, own_w, ys.at[i], yr.at[i], dev(x, lax.rem(y + i, 4), zl, zh, c)).start()
+    remote(own_w, own_w, cs.at[0], cr.at[0], other).start()
+
     scaling = float(128 + 64) ** (-0.5)
-    for load in loads[:4]:
+    for load in loads[:5]:
         load.wait()
     q = q_ref[g]
     nope = jnp.concatenate([q[:, j * 128 : j * 128 + 128] for j in range(QT)], axis=0)
@@ -505,16 +578,6 @@
     summed = dot(weights, newlat_ref[...]) / total
     new_valued = dot(summed.astype(BF16), value_ref[...])
     new_log = top + jnp.log(total)
-
-    pl.semaphore_wait(barrier, 32)
-
-    def send(i, carry):
-        peer = lax.rem(g + i, 16)
-        remote(msg_ref.at[peer], got.at[g], ms.at[i], mr.at[i], (peer, e)).start()
-        return carry
-
-    lax.fori_loop(1, 16, send, 0)
-    got[g] = msg_ref[g]
 
     experts = router_ref.shape[0]
     pairs = (zl // 2, 1 - zl // 2)
@@ -540,6 +603,11 @@
         picks.append(pick)
         masks.append(chosen)
 
+    for i in (1, 3, 2):
+        block = outw2.at[lax.rem(y - i + 4, 4), c]
+        remote(own_w, block, ys.at[i], yr.at[i], other).wait()
+        remote(block, block, cs.at[i], cr.at[i], other).start()
+
     def wait(i, carry):
         src = lax.rem(g - i + 16, 16)
         remote(msg_ref.at[src], got.at[src], ms.at[i], mr.at[i], other).wait()
@@ -564,23 +632,27 @@
     si = lax.broadcasted_iota(jnp.int32, (rows, rows), 1)
     req = ((di % 64) // 16) * 4 + ((di % 16) // 8) * 2 + di // 64
     perm = flag(si == (di % 8) * REQ + req)
-    valued_s[...] = dot(perm, valued).astype(BF16).reshape(2, 64, 128)
-
-    for load in loads[4:7]:
-        load.wait()
-    csend[...] = dot(valued_s[1 - c], outw_ref[...]).astype(BF16)
-    remote(csend, crecv, cs, cr, other).start()
-    own = dot(valued_s[c], outw_ref[...])
-    remote(csend, crecv, cs, cr, other).wait()
-    acc[...] = (own + crecv[...].astype(F32)).reshape(4, 16, 2048)
-    ysend[...] = acc[...].astype(BF16)
-    for i in (2, 1, 3):
-        peer = lax.rem(y + i, 4)
-        remote(ysend.at[peer], yrecv.at[i], ys.at[i], yr.at[i], dev(x, peer, zl, zh, c)).start()
-    total_row = acc[y]
-    for i in (1, 3, 2):
-        remote(ysend.at[0], yrecv.at[i], ys.at[i], yr.at[i], other).wait()
-        total_row = total_row + yrecv[i].astype(F32)
+    valued_s[...] = dot(perm, valued).astype(BF16).reshape(2, 4, 16, 128)
+    vin[y, c] = valued_s[c, y]
+    for k in (5, 7, 6, 2, 1, 3, 4):
+        to_y, to_c = lax.rem(y + k % 4, 4), lax.rem(c + k // 4, 2)
+        remote(
+            valued_s.at[to_c, to_y], vin.at[y, c], vs.at[k], vr.at[k], dev(x, to_y, zl, zh, to_c)
+        ).start()
+    for i in range(4):
+        y_of = lax.rem(y - i + 4, 4)
+        remote(outw2.at[y_of, c], outw2.at[y_of, 1 - c], cs.at[i], cr.at[i], other).wait()
+    for k in (4, 1, 3, 5, 7, 2, 6):
+        block = vin.at[lax.rem(y - k % 4 + 4, 4), lax.rem(c + k // 4, 2)]
+        remote(valued_s.at[0, 0], block, vs.at[k], vr.at[k], other).wait()
+    heads = jnp.concatenate([vin[k // 2, k % 2] for k in range(8)], axis=1)
+    total_row = jnp.concatenate(
+        [
+            dot(heads, outw1[...].reshape(1024, half)),
+            dot(heads, outw2[...].reshape(1024, half)),
+        ],
+        axis=1,
+    )
     own_8 = lax.broadcasted_iota(jnp.int32, (16, 1), 0) // 8 == zh
     resid = resid_ref[...].astype(F32)
     total_row = total_row + jnp.where(own_8, jnp.concatenate([resid, resid], axis=0), 0.0)
@@ -592,9 +664,11 @@
         remote(zsend, zrecv.at[d], ns.at[d], nr.at[d], other).wait()
         return zrecv[d].astype(F32)
 
+    gain = gain_ref[...].reshape(1, gain_ref.shape[0]).astype(F32)
+
     def norm(hidden):
         square = jnp.mean(hidden * hidden, axis=1, keepdims=True)
-        return (hidden * lax.rsqrt(square + EPSILON) * gain_ref[...].astype(F32)).astype(BF16)
+        return (hidden * lax.rsqrt(square + EPSILON) * gain).astype(BF16)
 
     hidden = total_row + column(1)
     hidden_s[...] = hidden.reshape(2, 8, 2048)
@@ -723,7 +797,7 @@
         ret_recv[chunk, mine] = ret_send[chunk, mine]
 
     forward(0)
-    for load in loads[7:10]:
+    for load in loads[6:9]:
         load.wait()
     crossed(0)
     routed_ffn(0)
@@ -732,7 +806,7 @@
     crossed(1)
     routed_ffn(1)
 
-    for load in loads[10:]:
+    for load in loads[9:]:
         load.wait()
     for i in (1, 3, 2):
         src = lax.rem(x - i + 4, 4)
@@ -805,19 +879,16 @@
         out_shape=jax.ShapeDtypeStruct((8, width), BF16),
         in_specs=[vmem_spec()] * len(vmem_args) + [hbm_spec()] * (len(more) + 6),
         out_specs=vmem_spec(),
-        scratch_shapes=[VMEM(m.shape, BF16) for m in more]
+        scratch_shapes=[VMEM(m.shape, BF16) for m in more[:-1]]
         + [
+            VMEM((4, 2, 128, width // 2), BF16),
             VMEM((GAP + gate.shape[0], width), BF16),
             VMEM(down.shape, BF16),
             VMEM((SGAP + sgate.shape[0], width), BF16),
             VMEM(sdown.shape, BF16),
             VMEM((16, REQ, MSG), BF16),
-            VMEM((2, 64, 128), BF16),
-            VMEM((64, width), BF16),
-            VMEM((64, width), BF16),
-            VMEM((4, 16, width), F32),
-            VMEM((4, 16, width), BF16),
-            VMEM((4, 16, width), BF16),
+            VMEM((2, 4, 16, 128), BF16),
+            VMEM((4, 2, 16, 128), BF16),
             VMEM((16, width), BF16),
             VMEM((8, 16, width), BF16),
             VMEM((2, 8, width), F32),
@@ -835,13 +906,15 @@
             VMEM((4, 2, 8, width), F32),
             VMEM((4, 2, 8, width), BF16),
             VMEM((8, 8, width), BF16),
-            DMA((13,)),
+            DMA((12,)),
             DMA((16,)),
             DMA((16,)),
-            DMA,
-            DMA,
-            DMA((4,)),
-            DMA((4,)),
+            DMA((4,)),
+            DMA((4,)),
+            DMA((4,)),
+            DMA((4,)),
+            DMA((8,)),
+            DMA((8,)),
             DMA((8,)),
             DMA((8,)),
             DMA((2, 16)),
@@ -889,34 +962,24 @@
     shared_up,
     shared_down,
 ):
-    q_all, routes8 = gather(query_nope[:, 0, :], query_rope[:, 0, :].T, routes)
-    absorb, value = absorb_weight[0], value_weight[0]
-    msg = attend(
-        node_length,
-        q_all.reshape(16 * REQ, -1),
-        absorb,
-        value,
+    q_all, routes8, pick, place, outw, lat, krope, absorb, value = gather(
+        query_nope[:, 0, :],
+        query_rope[:, 0, :].T,
+        routes,
+        leaf_node,
+        parent_node,
+        output_weight,
         cache_latent,
         jnp.swapaxes(cache_rope, 1, 2),
-        leaf_node,
-        parent_node,
+        absorb_weight[0],
+        value_weight[0],
+    )
+    msg = attend(
+        node_length, q_all.reshape(16 * REQ, -1), pick, place, absorb, value, lat, krope
     )
     return layer(
-        (
-            msg.reshape(16, REQ, MSG),
-            q_all,
-            routes8,
-            norm_gain[None, :],
-        ),
-        (
-            absorb,
-            value,
-            new_latent,
-            new_rope.T,
-            output_weight,
-            residual,
-            router_weight.T,
-        ),
+        (msg.reshape(16, REQ, MSG), q_all, routes8, outw, absorb, value),
+        (norm_gain, new_latent, new_rope.T, residual, router_weight.T, output_weight),
         (
             expert_gate[0].T,
             expert_up[0].T,

time: 108 us -> 111 us (1.028)
  Pallas kernels: 106 us -> 110 us
    pallas_call x1, Pallas kernels: 79.3 us -> 83 us  [layer(): pl.pallas_call(layer_kernel, name='layer', out_shape=jax.ShapeDtypeStruct...]
where the time goes in v4:
time: 111 us
  Pallas kernels  110 us (99%)
    pallas_call x1, Pallas kernels, layer(): pl.pallas_call(layer_kernel, name='layer', out_shape=jax.ShapeDtypeStruct...  83 us
    pallas_call x1, Pallas kernels, gather(): pl.pallas_call(gather_kernel, name='gather_queries', out_shape=(jax.Shape...  22.2 us
    pallas_call x1, Pallas kernels, attend(): pl.pallas_call(attn_kernel, name='attend_nodes', out_shape=jax.ShapeDtype...  5.07 us

profile of v4, /device:TPU:24, one launch (start us, length us, event | category | flops | bytes accessed | tf_op | source)
XLA Modules:
  0.0 110.9 jit_solution(13368958132420294596)
XLA Ops:
  0.0 22.2 %gather_queries.1 = (bf16[16,16,1536]{2,1,0:T(8,128)(2,1)S(1)}, s32[8,8,128]{2,1,0:T(8,128)S(1)}, bf16[2,256,256]{2,1,0:T(8,128)(2,1)S(1)}, bf16[2,256,256]{2,1,...) custom-call(bf16[128,128]{1,0:T(8,128)(2,1)} %bitcast.33, ...), custom_call_target="tpu_custom_call" | custom-call | tf_op jit(solution)/shard_map/gather_queries/pallas_call | solution.py:241
  22.2 5.1 %attend_nodes.1 = bf16[256,1152]{1,0:T(8,128)(2,1)S(1)} custom-call(bf16[256,1536]{1,0:T(8,128)(2,1)S(1)} %bitcast.22, bf16[2,256,256]{2,1,0:T(8,128)(2,1)S(1)} %get-tuple-element.15.pick_ref, bf16[2,256,256]{2,1,0:T(8,128)(2,1)S(1)} %get-tuple-element.16.place_ref, bf16[128,512]{1,0:T(8,128)(2,1)S(1)} %get-tuple-element.17.absorb_ref, ...), custom_call_target="tpu_custom_call" | custom-call | tf_op jit(solution)/shard_map/attend_nodes/pallas_call | solution.py:398
  27.2 83.0 %layer.1 = bf16[8,2048]{1,0:T(8,128)(2,1)S(1)} custom-call(bf16[16,16,1152]{2,1,0:T(8,128)(2,1)S(1)} %bitcast.23, bf16[16,16,1536]{2,1,0:T(8,128)(2,1)S(1)} %get-tuple-element.14.q_ref, s32[8,8,128]{2,1,0:T(8,128)S(1)} %get-tuple-element.21.routes_ref, bf16[4,2,128,1024]{3,2,1,0:T(8,128)(2,1)S(1)} %get-tuple-element.22.outw1, ...), custom_call_target="tpu_custom_call" | custom-call | tf_op jit(solution)/shard_map/layer/pallas_call | solution.py:876
  110.3 0.6 copy.24

commit v5 on v4

--- a/solution.py
+++ b/solution.py
@@ -97,7 +97,6 @@
     routes_hbm,
     leaf_hbm,
     parent_hbm,
-    outw_hbm,
     lat_hbm,
     krope_hbm,
     absorb_hbm,
@@ -106,7 +105,6 @@
     routes8,
     pick_ref,
     place_ref,
-    outw,
     lat_ref,
     krope_ref,
     absorb_ref,
@@ -124,13 +122,8 @@
     xqr,
     rs,
     rr,
-    ys,
-    yr,
-    cs,
-    cr,
 ):
     g, e, x, y, zl, zh, c = coords()
-    half = outw.shape[3]
     loads = start_loads(
         [
             (nope_hbm, nope_v),
@@ -138,7 +131,6 @@
             (routes_hbm, routes_v),
             (leaf_hbm, leaf_v),
             (parent_hbm, parent_v),
-            (outw_hbm.at[:, pl.ds(0, half)], outw.at[y, c]),
             (lat_hbm, lat_ref),
             (krope_hbm, krope_ref),
             (absorb_hbm, absorb_ref),
@@ -148,13 +140,10 @@
     )
     barrier = pltpu.get_barrier_semaphore()
     partner = dev(x, y, zl, 1 - zh, c)
-    other = dev(x, y, zl, zh, 1 - c)
     me = zl * 2 + zh
     for i in range(1, 4):
         greet(barrier, dev(lax.rem(x + i, 4), y, zl, zh, c))
         greet(barrier, dev(x, y, lax.rem(zl + i, 4), zh, c))
-        greet(barrier, dev(x, lax.rem(y + i, 4), zl, zh, c))
-    greet(barrier, other)
     for k in (1, 3, 5, 7):
         s = lax.rem(me + k, 8)
         greet(barrier, dev(x, y, s // 2, s % 2, c))
@@ -175,19 +164,13 @@
     mine[...] = jnp.zeros_like(mine)
     mine[:, 0 : routes_v.shape[1]] = routes_v[...]
     routes8[me] = mine[...]
-    pl.semaphore_wait(barrier, 14)
+    pl.semaphore_wait(barrier, 10)
 
     own = qall.at[g]
     for i in (1, 3, 2):
         remote(own, own, zq.at[i], zqr.at[i], dev(x, y, lax.rem(zl + i, 4), zh, c)).start()
     for k in (1, 3, 2):
         remote(own, own, xq.at[0, k], xqr.at[0, k], dev(lax.rem(x + k, 4), y, zl, zh, c)).start()
-    for load in loads[3:6]:
-        load.wait()
-    own_w = outw.at[y, c]
-    for i in (1, 3, 2):
-        remote(own_w, own_w, ys.at[i], yr.at[i], dev(x, lax.rem(y + i, 4), zl, zh, c)).start()
-    remote(own_w, own_w, cs.at[0], cr.at[0], other).start()
     for k in range(1, 8):
         s = lax.rem(me + k, 8)
         remote(mine, routes8.at[me], rs.at[k], rr.at[k], dev(x, y, s // 2, s % 2, c)).start()
@@ -204,6 +187,8 @@
     pass_on(3)
     pass_on(2)
 
+    for load in loads[3:5]:
+        load.wait()
     slots, _, requests = pick_ref.shape
     ids_0 = lax.broadcasted_iota(jnp.int32, (requests, requests), 0)
     ids_1 = lax.broadcasted_iota(jnp.int32, (requests, requests), 1)
@@ -217,11 +202,7 @@
         pick_ref[slot] = flag(rank_row.astype(jnp.int32) == ids_0)
         place_ref[slot] = flag(eye_column(rank_row).astype(jnp.int32) == ids_1)
 
-    for i in (1, 3, 2):
-        block = outw.at[lax.rem(y - i + 4, 4), c]
-        remote(own_w, block, ys.at[i], yr.at[i], other).wait()
-        remote(block, block, cs.at[i], cr.at[i], other).start()
-    for load in loads[6:]:
+    for load in loads[5:]:
         load.wait()
     for k in range(1, 8):
         s = lax.rem(me - k + 8, 8)
@@ -230,12 +211,9 @@
         for k in (1, 3, 2):
             block = qall.at[lax.rem(zl - i + 4, 4) * 4 + lax.rem(x - k + 4, 4)]
             remote(own, block, xq.at[i, k], xqr.at[i, k], partner).wait()
-    for i in range(4):
-        y_of = lax.rem(y - i + 4, 4)
-        remote(outw.at[y_of, c], outw.at[y_of, 1 - c], cs.at[i], cr.at[i], other).wait()
-
-
-def gather(nope, rope_t, routes, leaf, parent, outw, lat, krope_t, absorb, value):
+
+
+def gather(nope, rope_t, routes, leaf, parent, lat, krope_t, absorb, value):
     requests = leaf.shape[0]
     slots = lat.shape[0]
     return pl.pallas_call(
@@ -246,14 +224,13 @@
             jax.ShapeDtypeStruct((8, 8, 128), jnp.int32),
             jax.ShapeDtypeStruct((slots, requests, requests), BF16),
             jax.ShapeDtypeStruct((slots, requests, requests), BF16),
-            jax.ShapeDtypeStruct((4, 2, outw.shape[0], outw.shape[1] // 2), BF16),
             jax.ShapeDtypeStruct(lat.shape, BF16),
             jax.ShapeDtypeStruct(krope_t.shape, BF16),
             jax.ShapeDtypeStruct(absorb.shape, BF16),
             jax.ShapeDtypeStruct(value.shape, BF16),
         ),
-        in_specs=[hbm_spec()] * 10,
-        out_specs=(vmem_spec(),) * 9,
+        in_specs=[hbm_spec()] * 9,
+        out_specs=(vmem_spec(),) * 8,
         scratch_shapes=[
             VMEM(nope.shape, BF16),
             VMEM(rope_t.shape, BF16),
@@ -261,17 +238,13 @@
             VMEM((1, requests), jnp.int32),
             VMEM((1, parent.shape[0]), jnp.int32),
             VMEM((8, 128), jnp.int32),
-            DMA((10,)),
+            DMA((9,)),
             DMA((4,)),
             DMA((4,)),
             DMA((4, 4)),
             DMA((4, 4)),
             DMA((8,)),
             DMA((8,)),
-            DMA((4,)),
-            DMA((4,)),
-            DMA((4,)),
-            DMA((4,)),
         ],
         compiler_params=pltpu.CompilerParams(
             collective_id=0, has_side_effects=True, vmem_limit_bytes=24 << 20
@@ -279,7 +252,7 @@
     )(
         *map(
             stay,
-            (nope, rope_t, routes, leaf[None, :], parent[None, :], outw, lat, krope_t, absorb, value),
+            (nope, rope_t, routes, leaf[None, :], parent[None, :], lat, krope_t, absorb, value),
         )
     )
 
@@ -296,8 +269,13 @@
     return hi.astype(F32), mid.astype(F32), low.astype(F32)
 
 
-def join3(part):
-    return part[:, 0:8] + part[:, 8:16] + part[:, 16:24]
+def pack_logs(logs):
+    hi, mid, low = split3(logs)
+    return hi + pltpu.roll(mid, 8, 1) + pltpu.roll(low, 16, 1)
+
+
+def join_logs(tail):
+    return tail + pltpu.roll(tail, 120, 1) + pltpu.roll(tail, 112, 1)
 
 
 def attn_kernel(
@@ -347,12 +325,11 @@
             summed = dot(weights, lat_ref[slot, :keys])
             attended = (summed / total).astype(BF16)
             valued = dot(attended, value_ref[...]).astype(BF16)
-            parts = split3(top + jnp.log(total))
-            tail = jnp.where(lane == 24, 1.0, 0.0)
+            log_sum = top + jnp.log(total)
+            logs = jnp.zeros((TILE, 128), F32)
             for j in range(QT):
-                for k in range(3):
-                    piece = parts[k][j * TILE : (j + 1) * TILE]
-                    tail = jnp.where(lane == k * 8 + j, piece, tail)
+                logs = jnp.where(lane == j, log_sum[j * TILE : (j + 1) * TILE], logs)
+            tail = jnp.where((lane >= 24) & (lane < 32), 1.0, pack_logs(logs))
             done[slot, here] = jnp.concatenate(
                 [valued[j * TILE : (j + 1) * TILE] for j in range(QT)] + [tail.astype(BF16)],
                 axis=1,
@@ -367,9 +344,8 @@
                 lax.fori_loop(0, tiles, lambda step, carry: tile(keys, step, carry), 0)
 
     acc = [dot(place_ref[s], done[s]) for s in range(slots)]
-    logs = [
-        jnp.where(a[:, 1048:1049] > 0.5, join3(a[:, 1024:]), NEGATIVE) for a in acc
-    ]
+    tails = [a[:, 1024:] for a in acc]
+    logs = [jnp.where(pltpu.roll(t, 104, 1) > 0.5, join_logs(t), NEGATIVE) for t in tails]
     top = logs[0]
     for s in range(1, slots):
         top = jnp.maximum(top, logs[s])
@@ -377,19 +353,15 @@
     total = shares[0]
     for s in range(1, slots):
         total = total + shares[s]
-    log_sum = top + jnp.log(total)
+    shares = [v / total for v in shares]
     for j in range(QT):
         out = 0.0
         for s in range(slots):
-            out = out + (shares[s] / total)[:, j : j + 1] * acc[s][:, j * 128 : j * 128 + 128]
+            out = out + shares[s][:, j : j + 1] * acc[s][:, j * 128 : j * 128 + 128]
         out_ref[:, j * 128 : j * 128 + 128] = out.astype(BF16)
-    parts = split3(log_sum)
-    lane = lax.broadcasted_iota(jnp.int32, (requests, 128), 1)
-    tail = jnp.zeros((requests, 128), F32)
-    for j in range(QT):
-        for k in range(3):
-            tail = jnp.where(lane == k * 8 + j, parts[k][:, j : j + 1], tail)
-    out_ref[:, 1024:] = tail.astype(BF16)
+    lanes = lax.broadcasted_iota(jnp.int32, (requests, 128), 1)
+    log_sum = jnp.where(lanes < QT, top + jnp.log(total), 0.0)
+    out_ref[:, 1024:] = pack_logs(log_sum).astype(BF16)
 
 
 def attend(node_length, q_all, pick, place, absorb, value, lat, rope_t):
@@ -419,7 +391,6 @@
     msg_ref,
     q_ref,
     routes_ref,
-    outw1,
     absorb_ref,
     value_ref,
     gain_hbm,
@@ -440,14 +411,20 @@
     newrope_ref,
     resid_ref,
     router_ref,
-    outw2,
+    outw_ref,
     gate_up,
     down_w,
     sgate_up,
     sdown_w,
     got,
+    got_z,
+    blended,
     valued_s,
-    vin,
+    csend,
+    crecv,
+    acc,
+    ysend,
+    yrecv,
     zsend,
     zrecv,
     hidden_s,
@@ -460,20 +437,24 @@
     ret_send,
     ret_recv,
     share_in,
+    share_out,
     share_send,
     share_recv,
+    share_sum,
+    share_x,
+    share_back,
     part,
     lsend,
     lrecv,
     wsem,
     ms,
     mr,
+    gs,
+    gr,
     cs,
     cr,
     ys,
     yr,
-    vs,
-    vr,
     ns,
     nr,
     ds,
@@ -488,12 +469,13 @@
     xr,
     bs,
     br,
+    us,
+    ur,
     ls,
     lr,
 ):
     g, e, x, y, zl, zh, c = coords()
     mine = x * 4 + y
-    half = outw2.shape[3]
     ff = gate_hbm.shape[0]
     sff = sgate_hbm.shape[0]
     barrier = pltpu.get_barrier_semaphore()
@@ -501,11 +483,6 @@
     def plane(p):
         return dev(p // 4, p % 4, zl, zh, c)
 
-    def hello(i, carry):
-        greet(barrier, (lax.rem(g + i, 16), e))
-        return carry
-
-    lax.fori_loop(1, 16, hello, 0)
     other = dev(x, y, zl, zh, 1 - c)
     partner = dev(x, y, zl, 1 - zh, c)
     greet(barrier, other)
@@ -519,10 +496,10 @@
     def line(d):
         return dev(x, y, lines[d // 2], halves[d % 2], c)
 
-    for d in (3, 5, 7):
+    for d in range(2, 8):
         greet(barrier, line(d))
     for i in range(1, 4):
-        greet(barrier, dev(x, lax.rem(y + i, 4), zl, zh, 1 - c))
+        greet(barrier, dev(lax.rem(x + i, 4), y, zl, zh, c))
     loads = start_loads(
         [
             (gain_hbm, gain_ref),
@@ -530,7 +507,7 @@
             (newrope_hbm, newrope_ref),
             (resid_hbm, resid_ref),
             (router_hbm, router_ref),
-            (outw_hbm.at[:, pl.ds(half, half)], outw2.at[y, c]),
+            (outw_hbm, outw_ref),
             (gate_hbm, gate_up.at[pl.ds(0, ff)]),
             (up_hbm, gate_up.at[pl.ds(GAP, ff)]),
             (down_hbm, down_w),
@@ -543,24 +520,22 @@
     gate_up[ff:GAP] = jnp.zeros((GAP - ff, gate_up.shape[1]), BF16)
     sgate_up[sff:SGAP] = jnp.zeros((SGAP - sff, sgate_up.shape[1]), BF16)
 
-    pl.semaphore_wait(barrier, 35)
-
-    def send(i, carry):
-        peer = lax.rem(g + i, 16)
-        remote(msg_ref.at[peer], got.at[g], ms.at[i], mr.at[i], (peer, e)).start()
-        return carry
-
-    lax.fori_loop(1, 16, send, 0)
-    got[g] = msg_ref[g]
-
-    loads[5].wait()
-    own_w = outw2.at[y, c]
-    for i in (1, 3, 2):
-        remote(own_w, own_w, ys.at[i], yr.at[i], dev(x, lax.rem(y + i, 4), zl, zh, c)).start()
-    remote(own_w, own_w, cs.at[0], cr.at[0], other).start()
+    pl.semaphore_wait(barrier, 23)
+
+    homes = (lines[2], lines[3], lines[1], zl)
+    for n in range(4):
+        for i in (2, 1, 3):
+            peer = lax.rem(x + i, 4)
+            remote(
+                msg_ref.at[homes[n] * 4 + peer],
+                got.at[n, i],
+                ms.at[n, i],
+                mr.at[n, i],
+                dev(peer, y, zl, zh, c),
+            ).start()
 
     scaling = float(128 + 64) ** (-0.5)
-    for load in loads[:5]:
+    for load in loads[:6]:
         load.wait()
     q = q_ref[g]
     nope = jnp.concatenate([q[:, j * 128 : j * 128 + 128] for j in range(QT)], axis=0)
@@ -578,6 +553,47 @@
     summed = dot(weights, newlat_ref[...]) / total
     new_valued = dot(summed.astype(BF16), value_ref[...])
     new_log = top + jnp.log(total)
+
+    def blend(parts, more=None):
+        logs = [join_logs(p[:, 1024:].astype(F32)) for p in parts]
+        if more is not None:
+            logs.append(more[1])
+        peak = logs[0]
+        for v in logs[1:]:
+            peak = jnp.maximum(peak, v)
+        shares = [jnp.exp(v - peak) for v in logs]
+        whole = shares[0]
+        for v in shares[1:]:
+            whole = whole + v
+        shares = [v / whole for v in shares]
+        values = []
+        for j in range(QT):
+            value = 0.0
+            for p, share in zip(parts, shares):
+                value = value + share[:, j : j + 1] * p[:, j * 128 : j * 128 + 128].astype(F32)
+            if more is not None:
+                value = value + shares[-1][:, j : j + 1] * more[0][j * REQ : (j + 1) * REQ]
+            values.append(value.astype(BF16))
+        return values, peak + jnp.log(whole)
+
+    def along_x(n):
+        for i in (1, 3, 2):
+            src = msg_ref.at[homes[n] * 4 + lax.rem(x + i, 4)]
+            remote(src, got.at[n, i], ms.at[n, i], mr.at[n, i], other).wait()
+        return [msg_ref[homes[n] * 4 + x]] + [got[n, i] for i in range(1, 4)]
+
+    lane = lax.broadcasted_iota(jnp.int32, (REQ, 128), 1)
+
+    def along_z(n):
+        return remote(
+            blended.at[n], got_z.at[n], gs.at[n], gr.at[n], dev(x, y, homes[n], zh, c)
+        )
+
+    for n in range(3):
+        values, log_sum = blend(along_x(n))
+        tail = pack_logs(jnp.where(lane < QT, log_sum, 0.0)).astype(BF16)
+        blended[n] = jnp.concatenate(values + [tail], axis=1)
+        along_z(n).start()
 
     experts = router_ref.shape[0]
     pairs = (zl // 2, 1 - zl // 2)
@@ -603,56 +619,32 @@
         picks.append(pick)
         masks.append(chosen)
 
-    for i in (1, 3, 2):
-        block = outw2.at[lax.rem(y - i + 4, 4), c]
-        remote(own_w, block, ys.at[i], yr.at[i], other).wait()
-        remote(block, block, cs.at[i], cr.at[i], other).start()
-
-    def wait(i, carry):
-        src = lax.rem(g - i + 16, 16)
-        remote(msg_ref.at[src], got.at[src], ms.at[i], mr.at[i], other).wait()
-        return carry
-
-    lax.fori_loop(1, 16, wait, 0)
-
-    logs = join3(got[:, :, 1024:].astype(F32).reshape(16 * REQ, 128)).reshape(16, REQ, 8)
-    pieces = []
+    here = along_x(3)
+    logs = jnp.zeros((REQ, 128), F32)
     for j in range(QT):
-        log_j = logs[:, :, j : j + 1]
-        new_j = new_log[j * REQ : (j + 1) * REQ]
-        peak = jnp.maximum(jnp.max(log_j, axis=0), new_j)
-        share = jnp.exp(log_j - peak[None])
-        new_share = jnp.exp(new_j - peak)
-        whole = jnp.sum(share, axis=0) + new_share
-        value = jnp.sum(share * got[:, :, j * 128 : j * 128 + 128].astype(F32), axis=0)
-        value = value + new_share * new_valued[j * REQ : (j + 1) * REQ]
-        pieces.append((value / whole).astype(BF16))
+        logs = jnp.where(lane == j, new_log[j * REQ : (j + 1) * REQ], logs)
+    for n in (2, 0, 1):
+        along_z(n).wait()
+    pieces, _ = blend(here + [got_z[n] for n in range(3)], (new_valued, logs))
     valued = jnp.concatenate(pieces, axis=0)
     di = lax.broadcasted_iota(jnp.int32, (rows, rows), 0)
     si = lax.broadcasted_iota(jnp.int32, (rows, rows), 1)
     req = ((di % 64) // 16) * 4 + ((di % 16) // 8) * 2 + di // 64
     perm = flag(si == (di % 8) * REQ + req)
-    valued_s[...] = dot(perm, valued).astype(BF16).reshape(2, 4, 16, 128)
-    vin[y, c] = valued_s[c, y]
-    for k in (5, 7, 6, 2, 1, 3, 4):
-        to_y, to_c = lax.rem(y + k % 4, 4), lax.rem(c + k // 4, 2)
-        remote(
-            valued_s.at[to_c, to_y], vin.at[y, c], vs.at[k], vr.at[k], dev(x, to_y, zl, zh, to_c)
-        ).start()
-    for i in range(4):
-        y_of = lax.rem(y - i + 4, 4)
-        remote(outw2.at[y_of, c], outw2.at[y_of, 1 - c], cs.at[i], cr.at[i], other).wait()
-    for k in (4, 1, 3, 5, 7, 2, 6):
-        block = vin.at[lax.rem(y - k % 4 + 4, 4), lax.rem(c + k // 4, 2)]
-        remote(valued_s.at[0, 0], block, vs.at[k], vr.at[k], other).wait()
-    heads = jnp.concatenate([vin[k // 2, k % 2] for k in range(8)], axis=1)
-    total_row = jnp.concatenate(
-        [
-            dot(heads, outw1[...].reshape(1024, half)),
-            dot(heads, outw2[...].reshape(1024, half)),
-        ],
-        axis=1,
-    )
+    valued_s[...] = dot(perm, valued).astype(BF16).reshape(2, 64, 128)
+    csend[...] = dot(valued_s[1 - c], outw_ref[...]).astype(BF16)
+    remote(csend, crecv, cs, cr, other).start()
+    own = dot(valued_s[c], outw_ref[...])
+    remote(csend, crecv, cs, cr, other).wait()
+    acc[...] = (own + crecv[...].astype(F32)).reshape(4, 16, 2048)
+    ysend[...] = acc[...].astype(BF16)
+    for i in (2, 1, 3):
+        peer = lax.rem(y + i, 4)
+        remote(ysend.at[peer], yrecv.at[i], ys.at[i], yr.at[i], dev(x, peer, zl, zh, c)).start()
+    total_row = acc[y]
+    for i in (1, 3, 2):
+        remote(ysend.at[0], yrecv.at[i], ys.at[i], yr.at[i], other).wait()
+        total_row = total_row + yrecv[i].astype(F32)
     own_8 = lax.broadcasted_iota(jnp.int32, (16, 1), 0) // 8 == zh
     resid = resid_ref[...].astype(F32)
     total_row = total_row + jnp.where(own_8, jnp.concatenate([resid, resid], axis=0), 0.0)
@@ -815,23 +807,14 @@
                 share_in.at[src, zl], share_in.at[src, lines[d]], xs.at[d, i], xr.at[d, i], other
             ).wait()
     shared = ffn(share_in[...].reshape(128, 2048), sgate_up, SGAP, sff, sdown_w)
-    share_send[...] = shared.astype(BF16).reshape(4, 32, 2048)
-    for i in (2, 1, 3):
-        peer = lax.rem(x + i, 4)
+    share_out[...] = shared.reshape(4, 4, 8, 2048)
+    for z in range(4):
+        share_send[z] = share_out[:, z].astype(BF16)
+    for d in (2, 3, 1):
         remote(
-            share_send.at[peer], share_recv.at[i], bs.at[i], br.at[i], dev(peer, y, zl, zh, c)
+            share_send.at[lines[d]], share_recv.at[d], bs.at[d], br.at[d], line(2 * d)
         ).start()
     give(1)
-    for i in range(1, 4):
-        remote(share_send.at[0], share_recv.at[i], bs.at[i], br.at[i], other).wait()
-    share_sum = share_send[x].astype(F32)
-    for i in range(1, 4):
-        share_sum = share_sum + share_recv[i].astype(F32)
-    for z in range(4):
-        mine_z = share_sum[z * 8 : z * 8 + 8]
-        part[z, 0] = jnp.where(zh == 0, mine_z, 0.0)
-        part[z, 1] = jnp.where(zh == 1, mine_z, 0.0)
-
     def take(chunk):
         def step(i, carry):
             src = lax.rem(mine - i + 16, 16)
@@ -850,8 +833,8 @@
         w_low = (combines[chunk] - w_hi.astype(F32)).astype(BF16)
         routed = (dot(w_hi, back) + dot(w_low, back)).reshape(2, 2, 8, 2048)
         first = pl.ds(pairs[chunk] * 2, 2)
-        part[first] = part[first] + routed
-        lsend[first] = part[first].astype(BF16)
+        part[first] = routed
+        lsend[first] = routed.astype(BF16)
 
     def hand(d):
         block = lsend.at[lines[d // 2], halves[d % 2]]
@@ -860,10 +843,26 @@
     take(0)
     for d in (1, 3, 2):
         hand(d).start()
+    for d in (1, 2, 3):
+        remote(share_send.at[lines[d]], share_recv.at[d], bs.at[d], br.at[d], other).wait()
+    for n in range(4):
+        both = share_out[n, zl]
+        for d in range(1, 4):
+            both = both + share_recv[d, n].astype(F32)
+        share_sum[n] = both
+        share_x[n] = both.astype(BF16)
+    for i in (2, 1, 3):
+        peer = lax.rem(x + i, 4)
+        remote(
+            share_x.at[peer], share_back.at[i], us.at[i], ur.at[i], dev(peer, y, zl, zh, c)
+        ).start()
     take(1)
     for d in (5, 7, 4, 6):
         hand(d).start()
-    result = hidden_s[zh] + part[zl, zh]
+    result = hidden_s[zh] + part[zl, zh] + share_sum[x]
+    for i in (1, 3, 2):
+        remote(share_x.at[lax.rem(x + i, 4)], share_back.at[i], us.at[i], ur.at[i], other).wait()
+        result = result + share_back[i].astype(F32)
     for d in (2, 1, 3, 4, 6, 5, 7):
         hand(d).wait()
         result = result + lrecv[d].astype(F32)
@@ -879,16 +878,21 @@
         out_shape=jax.ShapeDtypeStruct((8, width), BF16),
         in_specs=[vmem_spec()] * len(vmem_args) + [hbm_spec()] * (len(more) + 6),
         out_specs=vmem_spec(),
-        scratch_shapes=[VMEM(m.shape, BF16) for m in more[:-1]]
+        scratch_shapes=[VMEM(m.shape, BF16) for m in more]
         + [
-            VMEM((4, 2, 128, width // 2), BF16),
             VMEM((GAP + gate.shape[0], width), BF16),
             VMEM(down.shape, BF16),
             VMEM((SGAP + sgate.shape[0], width), BF16),
             VMEM(sdown.shape, BF16),
-            VMEM((16, REQ, MSG), BF16),
-            VMEM((2, 4, 16, 128), BF16),
-            VMEM((4, 2, 16, 128), BF16),
+            VMEM((4, 4, REQ, MSG), BF16),
+            VMEM((3, REQ, MSG), BF16),
+            VMEM((3, REQ, MSG), BF16),
+            VMEM((2, 64, 128), BF16),
+            VMEM((64, width), BF16),
+            VMEM((64, width), BF16),
+            VMEM((4, 16, width), F32),
+            VMEM((4, 16, width), BF16),
+            VMEM((4, 16, width), BF16),
             VMEM((16, width), BF16),
             VMEM((8, 16, width), BF16),
             VMEM((2, 8, width), F32),
@@ -901,20 +905,24 @@
             VMEM((2, 16, 8, width), BF16),
             VMEM((2, 16, 8, width), BF16),
             VMEM((4, 4, 8, width), BF16),
-            VMEM((4, 32, width), BF16),
-            VMEM((4, 32, width), BF16),
+            VMEM((4, 4, 8, width), F32),
+            VMEM((4, 4, 8, width), BF16),
+            VMEM((4, 4, 8, width), BF16),
+            VMEM((4, 8, width), F32),
+            VMEM((4, 8, width), BF16),
+            VMEM((4, 8, width), BF16),
             VMEM((4, 2, 8, width), F32),
             VMEM((4, 2, 8, width), BF16),
             VMEM((8, 8, width), BF16),
             DMA((12,)),
-            DMA((16,)),
-            DMA((16,)),
+            DMA((4, 4)),
+            DMA((4, 4)),
+            DMA((3,)),
+            DMA((3,)),
+            DMA,
+            DMA,
             DMA((4,)),
             DMA((4,)),
-            DMA((4,)),
-            DMA((4,)),
-            DMA((8,)),
-            DMA((8,)),
             DMA((8,)),
             DMA((8,)),
             DMA((2, 16)),
@@ -927,6 +935,8 @@
             DMA((2, 16)),
             DMA((4, 4)),
             DMA((4, 4)),
+            DMA((4,)),
+            DMA((4,)),
             DMA((4,)),
             DMA((4,)),
             DMA((8,)),
@@ -962,13 +972,12 @@
     shared_up,
     shared_down,
 ):
-    q_all, routes8, pick, place, outw, lat, krope, absorb, value = gather(
+    q_all, routes8, pick, place, lat, krope, absorb, value = gather(
         query_nope[:, 0, :],
         query_rope[:, 0, :].T,
         routes,
         leaf_node,
         parent_node,
-        output_weight,
         cache_latent,
         jnp.swapaxes(cache_rope, 1, 2),
         absorb_weight[0],
@@ -978,7 +987,7 @@
         node_length, q_all.reshape(16 * REQ, -1), pick, place, absorb, value, lat, krope
     )
     return layer(
-        (msg.reshape(16, REQ, MSG), q_all, routes8, outw, absorb, value),
+        (msg.reshape(16, REQ, MSG), q_all, routes8, absorb, value),
         (norm_gain, new_latent, new_rope.T, residual, router_weight.T, output_weight),
         (
             expert_gate[0].T,

time: 111 us -> 103 us (0.928); the launches traced: 111 us -> 102 us
  Pallas kernels: 110 us -> 101 us
    pallas_call x1, Pallas kernels: 83 us -> 73.9 us  [layer(): pl.pallas_call(layer_kernel, name='layer', out_shape=jax.ShapeDtypeStruct...]
where the time goes in v5:
time: 103 us; the launch traced here: 102 us
  Pallas kernels  101 us (98%)
    pallas_call x1, Pallas kernels, layer(): pl.pallas_call(layer_kernel, name='layer', out_shape=jax.ShapeDtypeStruct...  73.9 us
    pallas_call x1, Pallas kernels, gather(): pl.pallas_call(gather_kernel, name='gather_queries', out_shape=(jax.Shape...  21.2 us
    pallas_call x1, Pallas kernels, attend(): pl.pallas_call(attn_kernel, name='attend_nodes', out_shape=jax.ShapeDtype...  5.76 us

profile of v5, /device:TPU:24, one launch (start us, length us, event | category | flops | bytes accessed | tf_op | source)
XLA Modules:
  0.0 101.6 jit_solution(243931719199173489)
XLA Ops:
  0.0 21.2 %gather_queries.1 = (bf16[16,16,1536]{2,1,0:T(8,128)(2,1)S(1)}, s32[8,8,128]{2,1,0:T(8,128)S(1)}, bf16[2,256,256]{2,1,0:T(8,128)(2,1)S(1)}, bf16[2,256,256]{2,1,...) custom-call(bf16[128,128]{1,0:T(8,128)(2,1)} %bitcast.33, ...), custom_call_target="tpu_custom_call" | custom-call | tf_op jit(solution)/shard_map/gather_queries/pallas_call | solution.py:219
  21.2 5.8 %attend_nodes.1 = bf16[256,1152]{1,0:T(8,128)(2,1)S(1)} custom-call(bf16[256,1536]{1,0:T(8,128)(2,1)S(1)} %bitcast.22, bf16[2,256,256]{2,1,0:T(8,128)(2,1)S(1)} %get-tuple-element.14.pick_ref, bf16[2,256,256]{2,1,0:T(8,128)(2,1)S(1)} %get-tuple-element.15.place_ref, bf16[128,512]{1,0:T(8,128)(2,1)S(1)} %get-tuple-element.16.absorb_ref, ...), custom_call_target="tpu_custom_call" | custom-call | tf_op jit(solution)/shard_map/attend_nodes/pallas_call | solution.py:370
  27.0 73.9 %layer.1 = bf16[8,2048]{1,0:T(8,128)(2,1)S(1)} custom-call(bf16[16,16,1152]{2,1,0:T(8,128)(2,1)S(1)} %bitcast.23, bf16[16,16,1536]{2,1,0:T(8,128)(2,1)S(1)} %get-tuple-element.13.q_ref, s32[8,8,128]{2,1,0:T(8,128)S(1)} %get-tuple-element.20.routes_ref, bf16[128,512]{1,0:T(8,128)(2,1)S(1)} %get-tuple-element.16.absorb_ref, ...), custom_call_target="tpu_custom_call" | custom-call | tf_op jit(solution)/shard_map/layer/pallas_call | solution.py:875
  100.9 0.6 copy.24

commit v6 on v5

--- a/solution.py
+++ b/solution.py
@@ -382,6 +382,11 @@
         compiler_params=pltpu.CompilerParams(vmem_limit_bytes=32 << 20),
     )(q_all, pick, place, absorb, value, lat, rope_t, stay(node_length))
 
+
+OFFSETS = sorted(
+    [(i, j) for i in range(4) for j in range(4) if i or j],
+    key=lambda o: -min(o[0], 4 - o[0]) - min(o[1], 4 - o[1]),
+)
 
 GAP = 384
 SGAP = 256
@@ -480,8 +485,8 @@
     sff = sgate_hbm.shape[0]
     barrier = pltpu.get_barrier_semaphore()
 
-    def plane(p):
-        return dev(p // 4, p % 4, zl, zh, c)
+    def source(i):
+        return lax.rem(x - i // 4 + 4, 4) * 4 + lax.rem(y - i % 4 + 4, 4)
 
     other = dev(x, y, zl, zh, 1 - c)
     partner = dev(x, y, zl, 1 - zh, c)
@@ -632,29 +637,47 @@
     req = ((di % 64) // 16) * 4 + ((di % 16) // 8) * 2 + di // 64
     perm = flag(si == (di % 8) * REQ + req)
     valued_s[...] = dot(perm, valued).astype(BF16).reshape(2, 64, 128)
-    csend[...] = dot(valued_s[1 - c], outw_ref[...]).astype(BF16)
-    remote(csend, crecv, cs, cr, other).start()
-    own = dot(valued_s[c], outw_ref[...])
-    remote(csend, crecv, cs, cr, other).wait()
-    acc[...] = (own + crecv[...].astype(F32)).reshape(4, 16, 2048)
-    ysend[...] = acc[...].astype(BF16)
-    for i in (2, 1, 3):
-        peer = lax.rem(y + i, 4)
-        remote(ysend.at[peer], yrecv.at[i], ys.at[i], yr.at[i], dev(x, peer, zl, zh, c)).start()
-    total_row = acc[y]
-    for i in (1, 3, 2):
-        remote(ysend.at[0], yrecv.at[i], ys.at[i], yr.at[i], other).wait()
-        total_row = total_row + yrecv[i].astype(F32)
+    half = outw_ref.shape[1] // 2
+    cols = [pl.ds(h * half, half) for h in range(2)]
     own_8 = lax.broadcasted_iota(jnp.int32, (16, 1), 0) // 8 == zh
-    resid = resid_ref[...].astype(F32)
-    total_row = total_row + jnp.where(own_8, jnp.concatenate([resid, resid], axis=0), 0.0)
-    zsend[...] = total_row.astype(BF16)
-    for d in (1, 3, 2, 5, 7, 4, 6):
-        remote(zsend, zrecv.at[d], ns.at[d], nr.at[d], line(d)).start()
+    for h in range(2):
+        csend[h] = dot(valued_s[1 - c], outw_ref[:, cols[h]]).astype(BF16)
+        remote(csend.at[h], crecv.at[h], cs.at[h], cr.at[h], other).start()
+    own = [dot(valued_s[c], outw_ref[:, cols[h]]) for h in range(2)]
+    for h in range(2):
+        remote(csend.at[h], crecv.at[h], cs.at[h], cr.at[h], other).wait()
+        acc[h] = (own[h] + crecv[h].astype(F32)).reshape(4, 16, half)
+        ysend[h] = acc[h].astype(BF16)
+        for i in (2, 1, 3):
+            peer = lax.rem(y + i, 4)
+            remote(
+                ysend.at[h, peer],
+                yrecv.at[h, i],
+                ys.at[h, i],
+                yr.at[h, i],
+                dev(x, peer, zl, zh, c),
+            ).start()
+    sums = []
+    for h in range(2):
+        row = acc[h, y]
+        for i in (1, 3, 2):
+            remote(ysend.at[h, 0], yrecv.at[h, i], ys.at[h, i], yr.at[h, i], other).wait()
+            row = row + yrecv[h, i].astype(F32)
+        resid = resid_ref[:, cols[h]].astype(F32)
+        row = row + jnp.where(own_8, jnp.concatenate([resid, resid], axis=0), 0.0)
+        zsend[h] = row.astype(BF16)
+        sums.append(row)
+        for d in (1, 3, 2):
+            remote(zsend.at[h], zrecv.at[d, h], ns.at[d, h], nr.at[d, h], line(d)).start()
+    for h in range(2):
+        for d in (5, 7, 4, 6):
+            remote(zsend.at[h], zrecv.at[d, h], ns.at[d, h], nr.at[d, h], line(d)).start()
+    total_row = jnp.concatenate(sums, axis=1)
 
     def column(d):
-        remote(zsend, zrecv.at[d], ns.at[d], nr.at[d], other).wait()
-        return zrecv[d].astype(F32)
+        for h in range(2):
+            remote(zsend.at[h], zrecv.at[d, h], ns.at[d, h], nr.at[d, h], other).wait()
+        return jnp.concatenate([zrecv[d, 0], zrecv[d, 1]], axis=1).astype(F32)
 
     gain = gain_ref[...].reshape(1, gain_ref.shape[0]).astype(F32)
 
@@ -689,18 +712,15 @@
             .reshape(16, 8, 2048)
         )
 
-        def send(i, carry):
-            p = lax.rem(mine + i, 16)
+        for dx, dy in OFFSETS:
+            to_x, to_y = lax.rem(x + dx, 4), lax.rem(y + dy, 4)
             remote(
-                packed.at[chunk, p],
+                packed.at[chunk, to_x * 4 + to_y],
                 arrived.at[chunk, c, mine],
-                ds.at[chunk, i],
-                dr.at[chunk, i],
-                plane(p),
+                ds.at[chunk, dx * 4 + dy],
+                dr.at[chunk, dx * 4 + dy],
+                dev(to_x, to_y, zl, zh, c),
             ).start()
-            return carry
-
-        lax.fori_loop(1, 16, send, 0)
         arrived[chunk, c, mine] = packed[chunk, mine]
         here = arrived.at[chunk, c, mine]
         remote(here, here, fs.at[chunk, 0], fr.at[chunk, 0], other).start()
@@ -733,7 +753,7 @@
 
     def forward(chunk):
         def step(i, carry):
-            src = lax.rem(mine - i + 16, 16)
+            src = source(i)
             block = arrived.at[chunk, c, src]
             remote(packed.at[chunk, src], block, ds.at[chunk, i], dr.at[chunk, i], other).wait()
             remote(block, block, fs.at[chunk, i], fr.at[chunk, i], other).start()
@@ -743,7 +763,7 @@
 
     def crossed(chunk):
         def step(i, carry):
-            src = lax.rem(mine - i + 16, 16)
+            src = source(i)
             block = arrived.at[chunk, c, src]
             remote(
                 block, arrived.at[chunk, 1 - c, src], fs.at[chunk, i], fr.at[chunk, i], other
@@ -774,18 +794,15 @@
             (own_out[chunk] + cross_recv[chunk].astype(F32)).astype(BF16).reshape(16, 8, 2048)
         )
 
-        def step(i, carry):
-            p = lax.rem(mine + i, 16)
+        for dx, dy in OFFSETS:
+            to_x, to_y = lax.rem(x + dx, 4), lax.rem(y + dy, 4)
             remote(
-                ret_send.at[chunk, p],
+                ret_send.at[chunk, to_x * 4 + to_y],
                 ret_recv.at[chunk, mine],
-                rs.at[chunk, i],
-                rr.at[chunk, i],
-                plane(p),
+                rs.at[chunk, dx * 4 + dy],
+                rr.at[chunk, dx * 4 + dy],
+                dev(to_x, to_y, zl, zh, c),
             ).start()
-            return carry
-
-        lax.fori_loop(1, 16, step, 0)
         ret_recv[chunk, mine] = ret_send[chunk, mine]
 
     forward(0)
@@ -797,6 +814,8 @@
     give(0)
     crossed(1)
     routed_ffn(1)
+
+    give(1)
 
     for load in loads[9:]:
         load.wait()
@@ -814,10 +833,9 @@
         remote(
             share_send.at[lines[d]], share_recv.at[d], bs.at[d], br.at[d], line(2 * d)
         ).start()
-    give(1)
     def take(chunk):
         def step(i, carry):
-            src = lax.rem(mine - i + 16, 16)
+            src = source(i)
             remote(
                 ret_send.at[chunk, src],
                 ret_recv.at[chunk, src],
@@ -842,6 +860,9 @@
 
     take(0)
     for d in (1, 3, 2):
+        hand(d).start()
+    take(1)
+    for d in (5, 7, 4, 6):
         hand(d).start()
     for d in (1, 2, 3):
         remote(share_send.at[lines[d]], share_recv.at[d], bs.at[d], br.at[d], other).wait()
@@ -856,16 +877,13 @@
         remote(
             share_x.at[peer], share_back.at[i], us.at[i], ur.at[i], dev(peer, y, zl, zh, c)
         ).start()
-    take(1)
-    for d in (5, 7, 4, 6):
-        hand(d).start()
     result = hidden_s[zh] + part[zl, zh] + share_sum[x]
+    for d in (2, 1, 3, 4, 6, 5, 7):
+        hand(d).wait()
+        result = result + lrecv[d].astype(F32)
     for i in (1, 3, 2):
         remote(share_x.at[lax.rem(x + i, 4)], share_back.at[i], us.at[i], ur.at[i], other).wait()
         result = result + share_back[i].astype(F32)
-    for d in (2, 1, 3, 4, 6, 5, 7):
-        hand(d).wait()
-        result = result + lrecv[d].astype(F32)
     out_ref[...] = result.astype(BF16)
 
 
@@ -888,13 +906,13 @@
             VMEM((3, REQ, MSG), BF16),
             VMEM((3, REQ, MSG), BF16),
             VMEM((2, 64, 128), BF16),
-            VMEM((64, width), BF16),
-            VMEM((64, width), BF16),
-            VMEM((4, 16, width), F32),
-            VMEM((4, 16, width), BF16),
-            VMEM((4, 16, width), BF16),
-            VMEM((16, width), BF16),
-            VMEM((8, 16, width), BF16),
+            VMEM((2, 64, width // 2), BF16),
+            VMEM((2, 64, width // 2), BF16),
+            VMEM((2, 4, 16, width // 2), F32),
+            VMEM((2, 4, 16, width // 2), BF16),
+            VMEM((2, 4, 16, width // 2), BF16),
+            VMEM((2, 16, width // 2), BF16),
+            VMEM((8, 2, 16, width // 2), BF16),
             VMEM((2, 8, width), F32),
             VMEM((4, 16, width), BF16),
             VMEM((2, 16, 8, width), BF16),
@@ -919,12 +937,12 @@
             DMA((4, 4)),
             DMA((3,)),
             DMA((3,)),
-            DMA,
-            DMA,
-            DMA((4,)),
-            DMA((4,)),
-            DMA((8,)),
-            DMA((8,)),
+            DMA((2,)),
+            DMA((2,)),
+            DMA((2, 4)),
+            DMA((2, 4)),
+            DMA((8, 2)),
+            DMA((8, 2)),
             DMA((2, 16)),
             DMA((2, 16)),
             DMA((2, 16)),

time: 103 us -> 101 us (0.981)
  Pallas kernels: 101 us -> 99.2 us
    pallas_call x1, Pallas kernels: 5.76 us -> 4.55 us  [attend(): pl.pallas_call(attn_kernel, name='attend_nodes', out_shape=jax.ShapeDtype...]
where the time goes in v6:
time: 101 us; the launch traced here: 99.9 us
  Pallas kernels  99.2 us (98%)
    pallas_call x1, Pallas kernels, layer(): pl.pallas_call(layer_kernel, name='layer', out_shape=jax.ShapeDtypeStruct...  73.5 us
    pallas_call x1, Pallas kernels, gather(): pl.pallas_call(gather_kernel, name='gather_queries', out_shape=(jax.Shape...  21.2 us
    pallas_call x1, Pallas kernels, attend(): pl.pallas_call(attn_kernel, name='attend_nodes', out_shape=jax.ShapeDtype...  4.55 us

profile of v6, /device:TPU:24, one launch (start us, length us, event | category | flops | bytes accessed | tf_op | source)
XLA Modules:
  0.0 99.9 jit_solution(4338223830255127439)
XLA Ops:
  0.0 21.2 %gather_queries.1 = (bf16[16,16,1536]{2,1,0:T(8,128)(2,1)S(1)}, s32[8,8,128]{2,1,0:T(8,128)S(1)}, bf16[2,256,256]{2,1,0:T(8,128)(2,1)S(1)}, bf16[2,256,256]{2,1,...) custom-call(bf16[128,128]{1,0:T(8,128)(2,1)} %bitcast.33, ...), custom_call_target="tpu_custom_call" | custom-call | tf_op jit(solution)/shard_map/gather_queries/pallas_call | solution.py:219
  21.2 4.5 %attend_nodes.1 = bf16[256,1152]{1,0:T(8,128)(2,1)S(1)} custom-call(bf16[256,1536]{1,0:T(8,128)(2,1)S(1)} %bitcast.22, bf16[2,256,256]{2,1,0:T(8,128)(2,1)S(1)} %get-tuple-element.14.pick_ref, bf16[2,256,256]{2,1,0:T(8,128)(2,1)S(1)} %get-tuple-element.15.place_ref, bf16[128,512]{1,0:T(8,128)(2,1)S(1)} %get-tuple-element.16.absorb_ref, ...), custom_call_target="tpu_custom_call" | custom-call | tf_op jit(solution)/shard_map/attend_nodes/pallas_call | solution.py:370
  25.8 73.5 %layer.1 = bf16[8,2048]{1,0:T(8,128)(2,1)S(1)} custom-call(bf16[16,16,1152]{2,1,0:T(8,128)(2,1)S(1)} %bitcast.23, bf16[16,16,1536]{2,1,0:T(8,128)(2,1)S(1)} %get-tuple-element.13.q_ref, s32[8,8,128]{2,1,0:T(8,128)S(1)} %get-tuple-element.20.routes_ref, bf16[128,512]{1,0:T(8,128)(2,1)S(1)} %get-tuple-element.16.absorb_ref, ...), custom_call_target="tpu_custom_call" | custom-call | tf_op jit(solution)/shard_map/layer/pallas_call | solution.py:893
  99.3 0.6 copy.24

commit v7 on v6

--- a/solution.py
+++ b/solution.py
@@ -169,7 +169,7 @@
     own = qall.at[g]
     for i in (1, 3, 2):
         remote(own, own, zq.at[i], zqr.at[i], dev(x, y, lax.rem(zl + i, 4), zh, c)).start()
-    for k in (1, 3, 2):
+    for k in (2, 1, 3):
         remote(own, own, xq.at[0, k], xqr.at[0, k], dev(lax.rem(x + k, 4), y, zl, zh, c)).start()
     for k in range(1, 8):
         s = lax.rem(me + k, 8)
@@ -178,7 +178,7 @@
     def pass_on(i):
         block = qall.at[lax.rem(zl - i + 4, 4) * 4 + x]
         remote(own, block, zq.at[i], zqr.at[i], partner).wait()
-        for k in (1, 3, 2):
+        for k in (2, 1, 3):
             remote(
                 block, block, xq.at[i, k], xqr.at[i, k], dev(lax.rem(x + k, 4), y, zl, zh, c)
             ).start()
@@ -724,6 +724,9 @@
         arrived[chunk, c, mine] = packed[chunk, mine]
         here = arrived.at[chunk, c, mine]
         remote(here, here, fs.at[chunk, 0], fr.at[chunk, 0], other).start()
+
+    def weigh(chunk):
+        tokens = normed[pl.ds(pairs[chunk] * 2, 2)].reshape(32, 2048)
         logits = dot_nt(tokens, router_ref[...])
         sigma = jax.nn.sigmoid(logits) * masks[chunk]
         route_w = ROUTE_SCALE * sigma / jnp.sum(sigma, axis=1, keepdims=True)
@@ -737,11 +740,10 @@
         ) * picks[chunk]
 
     normed[lines[1]] = norm(column(2) + column(3))
-    combine0 = pack(0)
+    pack(0)
     normed[lines[2]] = norm(column(4) + column(5))
     normed[lines[3]] = norm(column(6) + column(7))
-    combine1 = pack(1)
-    combines = (combine0, combine1)
+    pack(1)
     for d in range(1, 4):
         both = normed[lines[d]].reshape(2, 8, 2048)
         share_in[x, lines[d]] = jnp.where(zh == 0, both[0], both[1])
@@ -810,8 +812,8 @@
         load.wait()
     crossed(0)
     routed_ffn(0)
+    give(0)
     forward(1)
-    give(0)
     crossed(1)
     routed_ffn(1)
 
@@ -833,6 +835,8 @@
         remote(
             share_send.at[lines[d]], share_recv.at[d], bs.at[d], br.at[d], line(2 * d)
         ).start()
+    combines = [weigh(chunk) for chunk in range(2)]
+
     def take(chunk):
         def step(i, carry):
             src = source(i)

time: 101 us -> 101 us (level)
    pallas_call x1, Pallas kernels: 4.55 us -> 6.83 us  [attend(): pl.pallas_call(attn_kernel, name='attend_nodes', out_shape=jax.ShapeDtype...]
    pallas_call x1, Pallas kernels: 73.5 us -> 72.2 us  [layer(): pl.pallas_call(layer_kernel, name='layer', out_shape=jax.ShapeDtypeStruct...]
where the time goes in v7:
time: 101 us
  Pallas kernels  100 us (99%)
    pallas_call x1, Pallas kernels, layer(): pl.pallas_call(layer_kernel, name='layer', out_shape=jax.ShapeDtypeStruct...  72.2 us
    pallas_call x1, Pallas kernels, gather(): pl.pallas_call(gather_kernel, name='gather_queries', out_shape=(jax.Shape...  21 us
    pallas_call x1, Pallas kernels, attend(): pl.pallas_call(attn_kernel, name='attend_nodes', out_shape=jax.ShapeDtype...  6.83 us

profile of v7, /device:TPU:24, one launch (start us, length us, event | category | flops | bytes accessed | tf_op | source)
XLA Modules:
  0.0 100.7 jit_solution(7671458944584699116)
XLA Ops:
  0.0 21.0 %gather_queries.1 = (bf16[16,16,1536]{2,1,0:T(8,128)(2,1)S(1)}, s32[8,8,128]{2,1,0:T(8,128)S(1)}, bf16[2,256,256]{2,1,0:T(8,128)(2,1)S(1)}, bf16[2,256,256]{2,1,...) custom-call(bf16[128,128]{1,0:T(8,128)(2,1)} %bitcast.33, ...), custom_call_target="tpu_custom_call" | custom-call | tf_op jit(solution)/shard_map/gather_queries/pallas_call | solution.py:219
  21.0 6.8 %attend_nodes.1 = bf16[256,1152]{1,0:T(8,128)(2,1)S(1)} custom-call(bf16[256,1536]{1,0:T(8,128)(2,1)S(1)} %bitcast.22, bf16[2,256,256]{2,1,0:T(8,128)(2,1)S(1)} %get-tuple-element.14.pick_ref, bf16[2,256,256]{2,1,0:T(8,128)(2,1)S(1)} %get-tuple-element.15.place_ref, bf16[128,512]{1,0:T(8,128)(2,1)S(1)} %get-tuple-element.16.absorb_ref, ...), custom_call_target="tpu_custom_call" | custom-call | tf_op jit(solution)/shard_map/attend_nodes/pallas_call | solution.py:370
  27.8 72.2 %layer.1 = bf16[8,2048]{1,0:T(8,128)(2,1)S(1)} custom-call(bf16[16,16,1152]{2,1,0:T(8,128)(2,1)S(1)} %bitcast.23, bf16[16,16,1536]{2,1,0:T(8,128)(2,1)S(1)} %get-tuple-element.13.q_ref, s32[8,8,128]{2,1,0:T(8,128)S(1)} %get-tuple-element.20.routes_ref, bf16[128,512]{1,0:T(8,128)(2,1)S(1)} %get-tuple-element.16.absorb_ref, ...), custom_call_target="tpu_custom_call" | custom-call | tf_op jit(solution)/shard_map/layer/pallas_call | solution.py:897
  100.1 0.6 copy.24
